TPU v7x, 128 devices: a whole 4x4x4 slice. The times are simulated.
128 devices in a mesh: slab: 8 (over x, core), seq: 16 (over z, y).
Axes of the slice: x: 4, y: 4, z: 4, core: 2. Of those that a mesh axis runs over, the one named last changes fastest.
Arguments:
- query: bfloat16 [65536, 1024], P(('slab', 'seq')), may hold values from -6 to 6
- key: bfloat16 [65536, 1024], P(('slab', 'seq')), may hold values from -6 to 6
- value: bfloat16 [65536, 1024], P(('slab', 'seq')), may hold values from -6 to 6
- grad_out: bfloat16 [65536, 1024], P(('slab', 'seq')), may hold values from -6 to 6
- pattern: int32 [1024, 8], P('slab'), may hold values from 0 to 159, as said below
- valid_rows: int32 [1024], replicated, may hold values from 16 to 64
Outputs:
- attn_out: bfloat16 [65536, 1024], P(('slab', 'seq'))
- grad_query: bfloat16 [65536, 1024], P(('slab', 'seq'))
- grad_key: bfloat16 [65536, 1024], P(('slab', 'seq'))
- grad_value: bfloat16 [65536, 1024], P(('slab', 'seq'))
Inputs may be any that keep to these rules, and one draw needn't show every extreme that they name: `pattern`: row b lists 8 different numbers; its first entry is 16 + b % 128, the block itself; every target lies in 0 to 1023.
All inputs are finite; a program needn't handle non-finite values.
Results may differ from a plain program's by a relative error of at most 0.019.
Values may be sent and summed in bfloat16 or wider, within the bound.
No kernel may reach another device: no remote copies, remote signals or barrier semaphores. Data moves between devices by JAX's collectives and lax.ppermute only.
A program may use at most 128 MiB of HBM per device.

v0:
```python
from functools import partial
import math

import jax
import jax.numpy as jnp
from jax import lax
from jax.sharding import PartitionSpec as P

HEAD_DIM = 64
BLOCK = 64
FACE = 16


score_scale = 0.125


def with_halo(shard, sides, width):
    for axis, dim in sides:
        size, length = (lax.axis_size(axis), shard.shape[dim])
        up = [(i, (i + 1) % size) for i in range(size - 1)]
        down = [(j, i) for i, j in up]
        last = lax.slice_in_dim(shard, length - width, length, axis=dim)
        first = lax.slice_in_dim(shard, 0, width, axis=dim)
        before = lax.ppermute(last, axis, up)
        after = lax.ppermute(first, axis, down)
        shard = jnp.concatenate([before, shard, after], axis=dim)
    return shard


def block_step(grad_acc, block_items, key_blocks, live_counts):
    q_blk, g_blk, slot_ids = block_items
    groups, block_rows, head_num, head_width = q_blk.shape
    keys_num = slot_ids.shape[1]
    head_cols = head_num * head_width
    ext_blocks = key_blocks.shape[0]
    match = slot_ids[:, :, None] == jnp.arange(ext_blocks, dtype=jnp.int32)[None, None, :]
    selector = match.astype(jnp.bfloat16)
    picked = jnp.einsum(
        "qke,ebc->qkbc", selector, key_blocks, preferred_element_type=jnp.float32
    ).astype(jnp.bfloat16)
    k_blk = picked[..., :head_cols].reshape(groups, keys_num, block_rows, head_num, head_width)
    v_blk = picked[..., head_cols:].reshape(groups, keys_num, block_rows, head_num, head_width)
    slot_counts = jnp.sum(jnp.where(match, live_counts[None, None, :], 0), axis=2)
    is_live = jnp.arange(block_rows)[None, None, :] < slot_counts[:, :, None]
    live_mask = is_live[:, None, None, :, :]
    scores = (
        jnp.einsum("qahd,qkbhd->qhakb", q_blk, k_blk, preferred_element_type=jnp.float32)
        * score_scale
    )
    row_top = jnp.max(jnp.where(live_mask, scores, -jnp.inf), axis=(3, 4), keepdims=True)
    weight = jnp.where(live_mask, jnp.exp(scores - row_top), 0.0)
    totals = jnp.sum(weight, axis=(3, 4), keepdims=True)
    prob_b = (weight / totals).astype(jnp.bfloat16)
    out_blk = jnp.einsum(
        "qhakb,qkbhd->qahd", prob_b, v_blk, preferred_element_type=jnp.float32
    ).astype(jnp.bfloat16)
    delta_row = jnp.sum(g_blk.astype(jnp.float32) * out_blk.astype(jnp.float32), axis=3)
    delta_row = jnp.transpose(delta_row, (0, 2, 1))[:, :, :, None, None]
    grad_prob = jnp.einsum("qahd,qkbhd->qhakb", g_blk, v_blk, preferred_element_type=jnp.float32)
    dscore = (prob_b.astype(jnp.float32) * (grad_prob - delta_row)).astype(jnp.bfloat16)
    dq_blk = (
        score_scale
        * jnp.einsum("qhakb,qkbhd->qahd", dscore, k_blk, preferred_element_type=jnp.float32)
    ).astype(jnp.bfloat16)
    dk_tile = score_scale * jnp.einsum(
        "qhakb,qahd->qkbhd", dscore, q_blk, preferred_element_type=jnp.float32
    )
    dv_tile = jnp.einsum("qhakb,qahd->qkbhd", prob_b, g_blk, preferred_element_type=jnp.float32)
    grad_tiles = jnp.concatenate(
        [
            dk_tile.reshape(groups, keys_num, block_rows, head_cols),
            dv_tile.reshape(groups, keys_num, block_rows, head_cols),
        ],
        axis=3,
    )
    upper_part = grad_tiles.astype(jnp.bfloat16)
    lower_part = (grad_tiles - upper_part.astype(jnp.float32)).astype(jnp.bfloat16)
    added = jnp.einsum("qke,qkbc->ebc", selector, upper_part, preferred_element_type=jnp.float32)
    added = added + jnp.einsum(
        "qke,qkbc->ebc", selector, lower_part, preferred_element_type=jnp.float32
    )
    return (grad_acc + added, (out_blk, dq_blk))


def body(query, key, value, grad_out, pattern, valid_rows):
    q_heads, k_heads, v_heads = (
        lax.all_to_all(query, "seq", split_axis=1, concat_axis=0, tiled=True),
        lax.all_to_all(key, "seq", split_axis=1, concat_axis=0, tiled=True),
        lax.all_to_all(value, "seq", split_axis=1, concat_axis=0, tiled=True),
    )
    g_heads = lax.all_to_all(grad_out, "seq", split_axis=1, concat_axis=0, tiled=True)
    slab_rows, head_cols = q_heads.shape
    face_rows = FACE * BLOCK
    head_num = head_cols // HEAD_DIM
    extended = with_halo(jnp.concatenate([k_heads, v_heads], axis=1), (("slab", 0),), face_rows)
    ext_blocks = extended.shape[0] // BLOCK
    key_blocks = extended.reshape(ext_blocks, BLOCK, 2 * head_cols)
    padded = jnp.pad(valid_rows, (FACE, FACE))
    local_blocks = pattern.shape[0]
    start_row = lax.axis_index("slab") * local_blocks
    live_counts = lax.dynamic_slice_in_dim(padded, start_row, ext_blocks)
    group_size = math.gcd(local_blocks, max(1, 1024 // BLOCK))
    steps_num = local_blocks // group_size
    shape_five = (steps_num, group_size, BLOCK, head_num, HEAD_DIM)
    block_items = (
        q_heads.reshape(shape_five),
        g_heads.reshape(shape_five),
        pattern.reshape(steps_num, group_size, pattern.shape[1]),
    )
    init_acc = jnp.zeros((ext_blocks, BLOCK, 2 * head_cols), jnp.float32)
    grad_acc, (out_heads, dq_heads) = lax.scan(
        partial(block_step, key_blocks=key_blocks, live_counts=live_counts), init_acc, block_items
    )
    out_heads = out_heads.reshape(slab_rows, head_cols)
    dq_heads = dq_heads.reshape(slab_rows, head_cols)
    grad_rows = grad_acc.reshape(ext_blocks * BLOCK, 2 * head_cols)
    own_rows = grad_rows[face_rows : face_rows + slab_rows]
    rims = jnp.concatenate([grad_rows[:face_rows], grad_rows[face_rows + slab_rows :]], axis=0)
    received = with_halo(rims.astype(jnp.bfloat16), (("slab", 0),), face_rows).astype(rims.dtype)
    own_rows = own_rows.at[:face_rows].add(received[:face_rows])
    own_rows = own_rows.at[slab_rows - face_rows :].add(received[3 * face_rows :])
    dk_heads = own_rows[:, :head_cols].astype(jnp.bfloat16)
    dv_heads = own_rows[:, head_cols:].astype(jnp.bfloat16)
    attn_out, grad_query, grad_key, grad_value = (
        lax.all_to_all(out_heads, "seq", split_axis=0, concat_axis=1, tiled=True),
        lax.all_to_all(dq_heads, "seq", split_axis=0, concat_axis=1, tiled=True),
        lax.all_to_all(dk_heads, "seq", split_axis=0, concat_axis=1, tiled=True),
        lax.all_to_all(dv_heads, "seq", split_axis=0, concat_axis=1, tiled=True),
    )
    return (attn_out, grad_query, grad_key, grad_value)


def solution(mesh):
    return jax.shard_map(
        body,
        mesh=mesh,
        in_specs=(
            P(("slab", "seq"), None),
            P(("slab", "seq"), None),
            P(("slab", "seq"), None),
            P(("slab", "seq"), None),
            P("slab", None),
            P(),
        ),
        out_specs=(
            P(("slab", "seq"), None),
            P(("slab", "seq"), None),
            P(("slab", "seq"), None),
            P(("slab", "seq"), None),
        ),
        check_vma=False,
    )
```

profile of v0, /device:TPU:2, one launch (start us, length us, event | category | flops | bytes accessed | tf_op | source)
XLA Modules:
  0.0 569.6 jit_solution(16343273101846685830)
XLA Ops:
  3.0 8.0 %all-to-all-start.1 = ((bf16[512,16,64]{0,2,1:T(8,128)(2,1)}), bf16[512,16,64]{0,2,1:T(8,128)(2,1)S(1)}, u32[]{:S(2)}, u32[]{:S(2)}) async-start(bf16[512,16,64]{0,2,1:T(8,128)(2,1)} %bitcast.3), calls=%async_computation.1 | async-start | bytes 2097152 | tf_op jit(solution)/shard_map/all_to_all | solution.py:88
  12.4 16.3 %all-to-all-done.1 = bf16[512,16,64]{0,2,1:T(8,128)(2,1)S(1)} async-done(((bf16[512,16,64]{0,2,1:T(8,128)(2,1)}), bf16[512,16,64]{0,2,1:T(8,128)(2,1)S(1)}, u32[]{:S(2)}, u32[]{:S(2)}) %all-to-all-start.1) | async-done | bytes 1048608 | tf_op jit(solution)/shard_map/all_to_all | solution.py:88
  28.7 3.7 all-to-all-start.2
  33.7 15.0 %all-to-all-done.2 = bf16[512,16,64]{0,2,1:T(8,128)(2,1)S(1)} async-done(((bf16[512,16,64]{0,2,1:T(8,128)(2,1)}), bf16[512,16,64]{0,2,1:T(8,128)(2,1)S(1)}, u32[]{:S(2)}, u32[]{:S(2)}) %all-to-all-start.2) | async-done | bytes 1048608 | tf_op jit(solution)/shard_map/all_to_all | solution.py:89
  48.7 3.7 all-to-all-start.3
  55.9 12.8 %all-to-all-done.3 = bf16[512,16,64]{0,2,1:T(8,128)(2,1)S(1)} async-done(((bf16[512,16,64]{0,2,1:T(8,128)(2,1)}), bf16[512,16,64]{0,2,1:T(8,128)(2,1)S(1)}, u32[]{:S(2)}, u32[]{:S(2)}) %all-to-all-start.3) | async-done | bytes 1048608 | tf_op jit(solution)/shard_map/all_to_all | solution.py:91
  69.6 3.7 all-to-all-start
  77.4 3.6 collective-permute-start.1
  84.0 3.9 reshape.208
  95.5 3.4 copy.121
  98.9 363.6 %while.17 = (s32[]{:T(128)}, f32[160,64,128]{2,0,1:T(8,128)}, bf16[8,16,64,1,64]{2,1,0,4,3:T(8,128)(2,1)}, bf16[8,16,64,1,64]{2,1,0,4,3:T(8,128)(2,1)}, s32[8,16...) while((s32[]{:T(128)}, f32[160,64,128]{2,0,1:T(8,128)}, ...), condition=%wide.region_5.6_spmd.clone, body=%wide.region_0.5_spmd.clone.sunk | while | flops 1433203584 | bytes 111127928 | solution.py:111
  106.5 3.3 select_reduce_fusion.5
  112.8 4.2 copy.195
  131.4 4.1 fusion.98
  135.5 7.8 %fusion.99 = f32[160,64,128]{2,0,1:T(8,128)} fusion(f32[160,64,128,1]{2,0,3,1:T(8,128)} %fusion.98, f32[160,64,128]{2,0,1:T(8,128)} %get-tuple-element.264, pred[]{:T(512)S(6)} %compare.14, bf16[16,8,64,128]{3,2,1,0:T(8,128)(2,1)} %subtract_convert_fusion.2, s32[16,8]{0,1:T(8,128)S(1)} %bitcast.229), kind=kOutput, calls=%fused_computation.1.clone.1 | convolution fusion | flops 339496960 | bytes 17826304 | tf_op jit(solution)/shard_map/while/body/eval_jaxpr/qke,qkbc->ebc/dot_general | solution.py:79
  150.7 3.3 select_reduce_fusion.5
  157.0 4.2 copy.195
  175.5 4.1 fusion.98
  179.6 9.3 %fusion.99 = f32[160,64,128]{2,0,1:T(8,128)} fusion(f32[160,64,128,1]{2,0,3,1:T(8,128)} %fusion.98, f32[160,64,128]{2,0,1:T(8,128)} %get-tuple-element.264, pred[]{:T(512)S(6)} %compare.14, bf16[16,8,64,128]{3,2,1,0:T(8,128)(2,1)} %subtract_convert_fusion.2, s32[16,8]{0,1:T(8,128)S(1)} %bitcast.229), kind=kOutput, calls=%fused_computation.1.clone.1 | convolution fusion | flops 339496960 | bytes 17826304 | tf_op jit(solution)/shard_map/while/body/eval_jaxpr/qke,qkbc->ebc/dot_general | solution.py:79
  196.2 3.3 select_reduce_fusion.5
  202.6 4.2 copy.195
  221.1 4.1 fusion.98
  225.2 9.3 %fusion.99 = f32[160,64,128]{2,0,1:T(8,128)} fusion(f32[160,64,128,1]{2,0,3,1:T(8,128)} %fusion.98, f32[160,64,128]{2,0,1:T(8,128)} %get-tuple-element.264, pred[]{:T(512)S(6)} %compare.14, bf16[16,8,64,128]{3,2,1,0:T(8,128)(2,1)} %subtract_convert_fusion.2, s32[16,8]{0,1:T(8,128)S(1)} %bitcast.229), kind=kOutput, calls=%fused_computation.1.clone.1 | convolution fusion | flops 339496960 | bytes 17826304 | tf_op jit(solution)/shard_map/while/body/eval_jaxpr/qke,qkbc->ebc/dot_general | solution.py:79
  248.2 4.2 copy.195
  266.7 4.1 fusion.98
  270.8 9.3 %fusion.99 = f32[160,64,128]{2,0,1:T(8,128)} fusion(f32[160,64,128,1]{2,0,3,1:T(8,128)} %fusion.98, f32[160,64,128]{2,0,1:T(8,128)} %get-tuple-element.264, pred[]{:T(512)S(6)} %compare.14, bf16[16,8,64,128]{3,2,1,0:T(8,128)(2,1)} %subtract_convert_fusion.2, s32[16,8]{0,1:T(8,128)S(1)} %bitcast.229), kind=kOutput, calls=%fused_computation.1.clone.1 | convolution fusion | flops 339496960 | bytes 17826304 | tf_op jit(solution)/shard_map/while/body/eval_jaxpr/qke,qkbc->ebc/dot_general | solution.py:79
  293.8 4.2 copy.195
  312.3 4.1 fusion.98
  316.4 9.3 %fusion.99 = f32[160,64,128]{2,0,1:T(8,128)} fusion(f32[160,64,128,1]{2,0,3,1:T(8,128)} %fusion.98, f32[160,64,128]{2,0,1:T(8,128)} %get-tuple-element.264, pred[]{:T(512)S(6)} %compare.14, bf16[16,8,64,128]{3,2,1,0:T(8,128)(2,1)} %subtract_convert_fusion.2, s32[16,8]{0,1:T(8,128)S(1)} %bitcast.229), kind=kOutput, calls=%fused_computation.1.clone.1 | convolution fusion | flops 339496960 | bytes 17826304 | tf_op jit(solution)/shard_map/while/body/eval_jaxpr/qke,qkbc->ebc/dot_general | solution.py:79
  339.4 4.2 copy.195
  357.9 4.1 fusion.98
  362.0 9.3 %fusion.99 = f32[160,64,128]{2,0,1:T(8,128)} fusion(f32[160,64,128,1]{2,0,3,1:T(8,128)} %fusion.98, f32[160,64,128]{2,0,1:T(8,128)} %get-tuple-element.264, pred[]{:T(512)S(6)} %compare.14, bf16[16,8,64,128]{3,2,1,0:T(8,128)(2,1)} %subtract_convert_fusion.2, s32[16,8]{0,1:T(8,128)S(1)} %bitcast.229), kind=kOutput, calls=%fused_computation.1.clone.1 | convolution fusion | flops 339496960 | bytes 17826304 | tf_op jit(solution)/shard_map/while/body/eval_jaxpr/qke,qkbc->ebc/dot_general | solution.py:79
  385.0 4.2 copy.195
  403.5 4.1 fusion.98
  407.6 9.3 %fusion.99 = f32[160,64,128]{2,0,1:T(8,128)} fusion(f32[160,64,128,1]{2,0,3,1:T(8,128)} %fusion.98, f32[160,64,128]{2,0,1:T(8,128)} %get-tuple-element.264, pred[]{:T(512)S(6)} %compare.14, bf16[16,8,64,128]{3,2,1,0:T(8,128)(2,1)} %subtract_convert_fusion.2, s32[16,8]{0,1:T(8,128)S(1)} %bitcast.229), kind=kOutput, calls=%fused_computation.1.clone.1 | convolution fusion | flops 339496960 | bytes 17826304 | tf_op jit(solution)/shard_map/while/body/eval_jaxpr/qke,qkbc->ebc/dot_general | solution.py:79
  430.6 4.2 copy.195
  449.1 4.1 fusion.98
  453.2 9.3 %fusion.99 = f32[160,64,128]{2,0,1:T(8,128)} fusion(f32[160,64,128,1]{2,0,3,1:T(8,128)} %fusion.98, f32[160,64,128]{2,0,1:T(8,128)} %get-tuple-element.264, pred[]{:T(512)S(6)} %compare.14, bf16[16,8,64,128]{3,2,1,0:T(8,128)(2,1)} %subtract_convert_fusion.2, s32[16,8]{0,1:T(8,128)S(1)} %bitcast.229), kind=kOutput, calls=%fused_computation.1.clone.1 | convolution fusion | flops 339496960 | bytes 17826304 | tf_op jit(solution)/shard_map/while/body/eval_jaxpr/qke,qkbc->ebc/dot_general | solution.py:79
  462.5 7.2 %copy.177 = bf16[160,64,128]{2,1,0:T(8,128)(2,1)} copy(f32[160,64,128]{2,0,1:T(8,128)} %get-tuple-element.79) | data formatting | bytes 7864320 | tf_op jit(solution)/shard_map/while | solution.py:111
  472.5 5.8 %all-to-all-start.4 = ((bf16[16,512,64]{1,2,0:T(8,128)(2,1)}), bf16[16,512,64]{1,2,0:T(8,128)(2,1)S(1)}, u32[]{:S(2)}, u32[]{:S(2)}) async-start(bf16[16,512,64]{1,2,0:T(8,128)(2,1)} %copy.124), calls=%async_computation.4 | async-start | bytes 2097152 | tf_op jit(solution)/shard_map/all_to_all | solution.py:125
  481.3 3.6 collective-permute-start.3
  484.9 5.5 copy.127
  504.3 7.3 %all-to-all-start.5 = ((bf16[16,512,64]{1,2,0:T(8,128)(2,1)}), bf16[16,512,64]{1,2,0:T(8,128)(2,1)}, u32[]{:S(2)}, u32[]{:S(2)}) async-start(bf16[16,512,64]{1,2,0:T(8,128)(2,1)} %copy.126), calls=%async_computation.5 | async-start | bytes 2097152 | tf_op jit(solution)/shard_map/all_to_all | solution.py:126
  517.0 12.2 %all-to-all-done.5 = bf16[16,512,64]{1,2,0:T(8,128)(2,1)} async-done(((bf16[16,512,64]{1,2,0:T(8,128)(2,1)}), bf16[16,512,64]{1,2,0:T(8,128)(2,1)}, u32[]{:S(2)}, u32[]{:S(2)}) %all-to-all-start.5) | async-done | bytes 1048608 | tf_op jit(solution)/shard_map/all_to_all | solution.py:126
  529.3 4.3 all-to-all-start.6
  535.2 14.3 %all-to-all-done.6 = bf16[16,512,64]{1,2,0:T(8,128)(2,1)} async-done(((bf16[16,512,64]{1,2,0:T(8,128)(2,1)}), bf16[16,512,64]{1,2,0:T(8,128)(2,1)}, u32[]{:S(2)}, u32[]{:S(2)}) %all-to-all-start.6) | async-done | bytes 1048608 | tf_op jit(solution)/shard_map/all_to_all | solution.py:127
  549.5 3.7 all-to-all-start.7
  559.0 9.2 %all-to-all-done.7 = bf16[16,512,64]{1,2,0:T(8,128)(2,1)S(1)} async-done(((bf16[16,512,64]{1,2,0:T(8,128)(2,1)}), bf16[16,512,64]{1,2,0:T(8,128)(2,1)S(1)}, u32[]{:S(2)}, u32[]{:S(2)}) %all-to-all-start.7) | async-done | bytes 1048608 | tf_op jit(solution)/shard_map/all_to_all | solution.py:128
  (299 shorter events, 271.2 us)
Async XLA Ops:
  0.6 10.4 %copy-start.9 = (bf16[512,1024]{1,0:T(8,128)(2,1)S(1)}, bf16[512,1024]{1,0:T(8,128)(2,1)}, u32[]{:S(2)}) copy-start(bf16[512,1024]{1,0:T(8,128)(2,1)} %param.14) | copy-start | bytes 3145732
  3.0 25.7 %all-to-all-start.1 = ((bf16[512,16,64]{0,2,1:T(8,128)(2,1)}), bf16[512,16,64]{0,2,1:T(8,128)(2,1)S(1)}, u32[]{:S(2)}, u32[]{:S(2)}) async-start(bf16[512,16,64]{0,2,1:T(8,128)(2,1)} %bitcast.3), calls=%async_computation.1 | async-start | bytes 2097152 | tf_op jit(solution)/shard_map/all_to_all | solution.py:88
  11.1 21.3 %copy-start.10 = (bf16[512,1024]{1,0:T(8,128)(2,1)S(1)}, bf16[512,1024]{1,0:T(8,128)(2,1)}, u32[]{:S(2)}) copy-start(bf16[512,1024]{1,0:T(8,128)(2,1)} %param.15) | copy-start | bytes 3145732
  28.7 20.0 %all-to-all-start.2 = ((bf16[512,16,64]{0,2,1:T(8,128)(2,1)}), bf16[512,16,64]{0,2,1:T(8,128)(2,1)S(1)}, u32[]{:S(2)}, u32[]{:S(2)}) async-start(bf16[512,16,64]{0,2,1:T(8,128)(2,1)} %bitcast.5), calls=%async_computation.2 | async-start | bytes 2097152 | tf_op jit(solution)/shard_map/all_to_all | solution.py:89
  48.7 19.9 %all-to-all-start.3 = ((bf16[512,16,64]{0,2,1:T(8,128)(2,1)}), bf16[512,16,64]{0,2,1:T(8,128)(2,1)S(1)}, u32[]{:S(2)}, u32[]{:S(2)}) async-start(bf16[512,16,64]{0,2,1:T(8,128)(2,1)} %bitcast.216), calls=%async_computation.3 | async-start | bytes 2097152 | tf_op jit(solution)/shard_map/all_to_all | solution.py:91
  68.6 12.4 %copy-start.11 = (s32[128,8]{0,1:T(8,128)S(1)}, s32[128,8]{0,1:T(8,128)}, u32[]{:S(2)}) copy-start(s32[128,8]{0,1:T(8,128)} %param.16) | copy-start | bytes 12292
  68.6 12.5 %copy-start.12 = (s32[1024]{0:T(1024)S(1)}, s32[1024]{0:T(1024)}, u32[]{:S(2)}) copy-start(s32[1024]{0:T(1024)} %param.17) | copy-start | bytes 12292
  69.6 19.7 %all-to-all-start = ((bf16[512,16,64]{0,2,1:T(8,128)(2,1)}), bf16[512,16,64]{0,2,1:T(8,128)(2,1)S(1)}, u32[]{:S(2)}, u32[]{:S(2)}) async-start(bf16[512,16,64]{0,2,1:T(8,128)(2,1)} %bitcast.213), calls=%async_computation | async-start | bytes 2097152 | tf_op jit(solution)/shard_map/all_to_all | solution.py:87
  74.6 13.4 %copy-start.6 = (bf16[8192,128]{0,1:T(8,128)(2,1)}, bf16[8192,128]{0,1:T(8,128)(2,1)S(1)}, u32[]{:S(2)}) copy-start(bf16[8192,128]{0,1:T(8,128)(2,1)S(1)} %constant_dynamic-update-slice_fusion) | copy-start | bytes 6291460
  75.5 15.6 %collective-permute-start = (bf16[1024,128]{0,1:T(8,128)(2,1)}, bf16[1024,128]{0,1:T(8,128)(2,1)S(1)}, u32[]{:S(2)}, u32[]{:S(2)}) collective-permute-start(bf16[1024,128]{0,1:T(8,128)(2,1)} %get-tuple-element.179), channel_id=1, source_target_pairs={{0,16},{16,32},{32,48},{48,64},{64,80},{80,96},{96,112},{1,17},{17... | collective-permute-start | bytes 786440 | tf_op jit(solution)/shard_map/ppermute | solution.py:24
  77.4 13.7 %collective-permute-start.1 = (bf16[1024,128]{0,1:T(8,128)(2,1)}, bf16[1024,128]{0,1:T(8,128)(2,1)}, u32[]{:S(2)}, u32[]{:S(2)}) collective-permute-start(bf16[1024,128]{0,1:T(8,128)(2,1)} %get-tuple-element.180), channel_id=1, source_target_pairs={{16,0},{32,16},{48,32},{64,48},{80,64},{96,80},{112,96},{17,1},{33... | collective-permute-start | bytes 786440 | tf_op jit(solution)/shard_map/ppermute | solution.py:25
  99.1 3.7 copy-start.2
  106.1 3.8 copy-start
  120.5 2.8 copy-start.1
  135.5 7.8 %copy-start.3 = (bf16[160,64,128]{2,0,1:T(8,128)(2,1)S(1)}, bf16[160,64,128]{2,0,1:T(8,128)(2,1)}, u32[]{:S(2)}) copy-start(bf16[160,64,128]{2,0,1:T(8,128)(2,1)} %copy-done.2) | copy-start | bytes 7864324 | tf_op jit(solution)/shard_map/while
  143.3 3.7 copy-start.2
  150.2 3.8 copy-start
  164.6 2.8 copy-start.1
  179.6 9.3 %copy-start.3 = (bf16[160,64,128]{2,0,1:T(8,128)(2,1)S(1)}, bf16[160,64,128]{2,0,1:T(8,128)(2,1)}, u32[]{:S(2)}) copy-start(bf16[160,64,128]{2,0,1:T(8,128)(2,1)} %copy-done.2) | copy-start | bytes 7864324 | tf_op jit(solution)/shard_map/while
  188.9 3.7 copy-start.2
  195.8 3.8 copy-start
  210.2 2.8 copy-start.1
  225.2 9.3 %copy-start.3 = (bf16[160,64,128]{2,0,1:T(8,128)(2,1)S(1)}, bf16[160,64,128]{2,0,1:T(8,128)(2,1)}, u32[]{:S(2)}) copy-start(bf16[160,64,128]{2,0,1:T(8,128)(2,1)} %copy-done.2) | copy-start | bytes 7864324 | tf_op jit(solution)/shard_map/while
  234.5 3.7 copy-start.2
  241.4 3.8 copy-start
  270.8 9.3 %copy-start.3 = (bf16[160,64,128]{2,0,1:T(8,128)(2,1)S(1)}, bf16[160,64,128]{2,0,1:T(8,128)(2,1)}, u32[]{:S(2)}) copy-start(bf16[160,64,128]{2,0,1:T(8,128)(2,1)} %copy-done.2) | copy-start | bytes 7864324 | tf_op jit(solution)/shard_map/while
  280.1 3.7 copy-start.2
  287.0 3.8 copy-start
  316.4 9.3 %copy-start.3 = (bf16[160,64,128]{2,0,1:T(8,128)(2,1)S(1)}, bf16[160,64,128]{2,0,1:T(8,128)(2,1)}, u32[]{:S(2)}) copy-start(bf16[160,64,128]{2,0,1:T(8,128)(2,1)} %copy-done.2) | copy-start | bytes 7864324 | tf_op jit(solution)/shard_map/while
  325.7 3.7 copy-start.2
  332.6 3.8 copy-start
  362.0 9.3 %copy-start.3 = (bf16[160,64,128]{2,0,1:T(8,128)(2,1)S(1)}, bf16[160,64,128]{2,0,1:T(8,128)(2,1)}, u32[]{:S(2)}) copy-start(bf16[160,64,128]{2,0,1:T(8,128)(2,1)} %copy-done.2) | copy-start | bytes 7864324 | tf_op jit(solution)/shard_map/while
  371.3 3.7 copy-start.2
  378.2 3.8 copy-start
  407.6 9.3 %copy-start.3 = (bf16[160,64,128]{2,0,1:T(8,128)(2,1)S(1)}, bf16[160,64,128]{2,0,1:T(8,128)(2,1)}, u32[]{:S(2)}) copy-start(bf16[160,64,128]{2,0,1:T(8,128)(2,1)} %copy-done.2) | copy-start | bytes 7864324 | tf_op jit(solution)/shard_map/while
  416.9 3.7 copy-start.2
  423.8 3.8 copy-start
  453.2 9.3 %copy-start.3 = (bf16[160,64,128]{2,0,1:T(8,128)(2,1)S(1)}, bf16[160,64,128]{2,0,1:T(8,128)(2,1)}, u32[]{:S(2)}) copy-start(bf16[160,64,128]{2,0,1:T(8,128)(2,1)} %copy-done.2) | copy-start | bytes 7864324 | tf_op jit(solution)/shard_map/while
  462.5 7.2 %copy-start.8 = (bf16[8,16,64,1,64]{2,1,0,4,3:T(8,128)(2,1)S(1)}, bf16[8,16,64,1,64]{2,1,0,4,3:T(8,128)(2,1)}, u32[]{:S(2)}) copy-start(bf16[8,16,64,1,64]{2,1,0,4,3:T(8,128)(2,1)} %get-tuple-element.77) | copy-start | bytes 3145732
  472.5 31.8 %all-to-all-start.4 = ((bf16[16,512,64]{1,2,0:T(8,128)(2,1)}), bf16[16,512,64]{1,2,0:T(8,128)(2,1)S(1)}, u32[]{:S(2)}, u32[]{:S(2)}) async-start(bf16[16,512,64]{1,2,0:T(8,128)(2,1)} %copy.124), calls=%async_computation.4 | async-start | bytes 2097152 | tf_op jit(solution)/shard_map/all_to_all | solution.py:125
  479.4 19.7 %collective-permute-start.2 = (bf16[1024,128]{1,0:T(8,128)(2,1)S(1)}, bf16[1024,128]{1,0:T(8,128)(2,1)S(1)}, u32[]{:S(2)}, u32[]{:S(2)}) collective-permute-start(bf16[1024,128]{1,0:T(8,128)(2,1)S(1)} %bitcast.220), channel_id=1, source_target_pairs={{0,16},{16,32},{32,48},{48,64},{64,80},{80,96},{96,112},{1,17},{17... | collective-permute-start | bytes 786440 | tf_op jit(solution)/shard_map/ppermute | solution.py:24
  481.3 17.7 %collective-permute-start.3 = (bf16[1024,128]{1,0:T(8,128)(2,1)S(1)}, bf16[1024,128]{1,0:T(8,128)(2,1)}, u32[]{:S(2)}, u32[]{:S(2)}) collective-permute-start(bf16[1024,128]{1,0:T(8,128)(2,1)S(1)} %bitcast.223), channel_id=1, source_target_pairs={{16,0},{32,16},{48,32},{64,48},{80,64},{96,80},{112,96},{17,1},{33... | collective-permute-start | bytes 786440 | tf_op jit(solution)/shard_map/ppermute | solution.py:25
  490.5 3.8 copy-start.4
  494.2 4.8 slice-start
  504.3 25.0 %all-to-all-start.5 = ((bf16[16,512,64]{1,2,0:T(8,128)(2,1)}), bf16[16,512,64]{1,2,0:T(8,128)(2,1)}, u32[]{:S(2)}, u32[]{:S(2)}) async-start(bf16[16,512,64]{1,2,0:T(8,128)(2,1)} %copy.126), calls=%async_computation.5 | async-start | bytes 2097152 | tf_op jit(solution)/shard_map/all_to_all | solution.py:126
  514.2 19.4 %copy-start.5 = (bf16[8192,64]{1,0:T(8,128)(2,1)S(1)}, bf16[8192,64]{1,0:T(8,128)(2,1)}, u32[]{:S(2)}) copy-start(bf16[8192,64]{1,0:T(8,128)(2,1)} %get-tuple-element.177) | copy-start | bytes 3145732
  529.3 20.3 %all-to-all-start.6 = ((bf16[16,512,64]{1,2,0:T(8,128)(2,1)}), bf16[16,512,64]{1,2,0:T(8,128)(2,1)}, u32[]{:S(2)}, u32[]{:S(2)}) async-start(bf16[16,512,64]{1,2,0:T(8,128)(2,1)} %copy.131), calls=%async_computation.6 | async-start | bytes 2097152 | tf_op jit(solution)/shard_map/all_to_all | solution.py:127
  549.5 18.7 %all-to-all-start.7 = ((bf16[16,512,64]{1,2,0:T(8,128)(2,1)}), bf16[16,512,64]{1,2,0:T(8,128)(2,1)S(1)}, u32[]{:S(2)}, u32[]{:S(2)}) async-start(bf16[16,512,64]{1,2,0:T(8,128)(2,1)} %copy.133), calls=%async_computation.7 | async-start | bytes 2097152 | tf_op jit(solution)/shard_map/all_to_all | solution.py:128
  (6 other events, 14.8 us)
where the time goes:
time: 579 us; the launch traced here: 570 us
  matrix products  201 us (35%)
  local copies, waits for them, and re-layouts  168 us (29%)
  waiting for transfers between devices  81.2 us (14%)
  other arithmetic  65.9 us (11%)
  starting transfers between devices  51.2 us (9%)
    dot_general x8, matrix products, block_step(): jnp.einsum('qke,qkbc->ebc', selector, lower_part, preferred_element_type=...  72.7 us
    slice x16, local copies, waits for them, and re-layouts, block_step(): picked[..., head_cols:]  56 us
    dot_general x8, matrix products, block_step(): jnp.einsum('qke,qkbc->ebc', selector, upper_part, preferred_element_type=...  32.9 us
    dot_general x8, matrix products, block_step(): jnp.einsum('qahd,qkbhd->qhakb', q_blk, k_blk, preferred_element_type=jnp....  26.7 us
    slice x8, local copies, waits for them, and re-layouts, block_step(): picked[..., :head_cols]  26 us
    dot_general x8, matrix products, block_step(): jnp.einsum('qahd,qkbhd->qhakb', g_blk, v_blk, preferred_element_type=jnp....  22 us
    unnamed x29, local copies, waits for them, and re-layouts  21.6 us
    convert_element_type x8, other arithmetic, block_step(): (grad_tiles - upper_part.astype(jnp.float32)).astype(jnp.bfloat16)  20.4 us
  transfers between devices with their start and end apart: 12, of which 7 were waited for; matrix products, arithmetic and copies ran while one was open for 8% of the time, Pallas kernels for 0%

commit v1 on v0

v1 whole, which is shorter than its diff:
```python
from functools import partial
import math

import jax
import jax.numpy as jnp
from jax import lax
from jax.experimental import pallas as pl
from jax.experimental.pallas import tpu as pltpu
from jax.sharding import PartitionSpec as P

HEAD_DIM = 64
BLOCK = 64
FACE = 16
PAIR = 2 * HEAD_DIM

score_scale = 0.125
exp2_scale = score_scale * math.log2(math.e)


def pack_kernel(a_ref, b_ref, out_ref):
    a, b = a_ref[...], b_ref[...]
    out_ref[0] = jnp.concatenate([a[:, :HEAD_DIM], b[:, :HEAD_DIM]], axis=1)
    out_ref[1] = jnp.concatenate([a[:, HEAD_DIM:], b[:, HEAD_DIM:]], axis=1)


def pack_heads(a, b):
    rows, cols = a.shape
    heads = cols // HEAD_DIM
    half = pl.BlockSpec((rows, PAIR), lambda i: (0, i))
    return pl.pallas_call(
        pack_kernel,
        out_shape=jax.ShapeDtypeStruct((heads, rows, PAIR), a.dtype),
        grid=(heads // 2,),
        in_specs=[half, half],
        out_specs=pl.BlockSpec((2, rows, PAIR), lambda i: (i, 0, 0)),
        name="pack_heads",
    )(a, b)


def unpack_kernel(x_ref, a_ref, b_ref):
    x, y = x_ref[0], x_ref[1]
    a_ref[...] = jnp.concatenate([x[:, :HEAD_DIM], y[:, :HEAD_DIM]], axis=1)
    b_ref[...] = jnp.concatenate([x[:, HEAD_DIM:], y[:, HEAD_DIM:]], axis=1)


def unpack_heads(x):
    heads, rows, _ = x.shape
    full = jax.ShapeDtypeStruct((rows, heads * HEAD_DIM), x.dtype)
    half = pl.BlockSpec((rows, PAIR), lambda i: (0, i))
    return pl.pallas_call(
        unpack_kernel,
        out_shape=(full, full),
        grid=(heads // 2,),
        in_specs=[pl.BlockSpec((2, rows, PAIR), lambda i: (i, 0, 0))],
        out_specs=(half, half),
        name="unpack_heads",
    )(x)


def attention_kernel(
    pattern_ref, valid_ref, start_ref, qg_ref, kv_hbm, before_hbm, after_hbm,
    od_ref, mid_ref, face_ref, rim_ref, kv_ref, acc_ref, sems, *, keys_num, unroll,
):
    step = pl.program_id(0)
    face = before_hbm.shape[0]
    own = kv_hbm.shape[0]
    blocks = qg_ref.shape[0] // BLOCK

    @pl.when(step == 0)
    def _():
        copies = [
            pltpu.make_async_copy(before_hbm, kv_ref.at[pl.ds(0, face)], sems.at[0]),
            pltpu.make_async_copy(kv_hbm, kv_ref.at[pl.ds(face, own)], sems.at[1]),
            pltpu.make_async_copy(after_hbm, kv_ref.at[pl.ds(face + own, face)], sems.at[2]),
        ]
        for copy in copies:
            copy.start()
        acc_ref[...] = jnp.zeros_like(acc_ref)
        for copy in copies:
            copy.wait()

    start = start_ref[0]
    low = lax.broadcasted_iota(jnp.int32, (BLOCK, PAIR), 1) < HEAD_DIM
    lane = lax.broadcasted_iota(jnp.int32, (1, PAIR), 1)

    def one_block(i, _):
        rows = pl.ds(pl.multiple_of(i * BLOCK, BLOCK), BLOCK)
        base = (step * blocks + i) * keys_num
        slots = [pattern_ref[base + j] for j in range(keys_num)]
        counts = [valid_ref[start + slot] for slot in slots]
        spans = [pl.ds(pl.multiple_of(slot * BLOCK, BLOCK), BLOCK) for slot in slots]
        kv = jnp.concatenate([kv_ref[span, :] for span in spans], axis=0)
        bias = jnp.concatenate(
            [
                jnp.where(
                    lane < jnp.where(lane < HEAD_DIM, counts[j], counts[j + 1] + HEAD_DIM),
                    0.0,
                    -jnp.inf,
                )
                for j in range(0, keys_num, 2)
            ],
            axis=1,
        )
        qg = qg_ref[rows, :]
        zero = jnp.zeros_like(qg)
        gq = jnp.concatenate([jnp.where(low, zero, qg), jnp.where(low, qg, zero)], axis=0)
        both = lax.dot_general(
            gq, kv, (((1,), (1,)), ((), ())), preferred_element_type=jnp.float32
        )
        grad_prob, scores = both[:BLOCK], both[BLOCK:] + bias
        top = jnp.max(scores, axis=1, keepdims=True)
        weight = jnp.exp2((scores - top) * exp2_scale)
        total = jnp.sum(weight, axis=1, keepdims=True)
        prob = (weight * (1.0 / total)).astype(jnp.bfloat16)
        prob_wide = prob.astype(jnp.float32)
        delta = jnp.sum(prob_wide * grad_prob, axis=1, keepdims=True)
        dscore = (prob_wide * (grad_prob - delta)).astype(jnp.bfloat16)
        pd = jnp.concatenate([prob, dscore], axis=0)
        od = jnp.dot(pd, kv, preferred_element_type=jnp.float32)
        od_ref[rows, :] = jnp.where(low, od[BLOCK:] * score_scale, od[:BLOCK]).astype(od_ref.dtype)
        dkv = lax.dot_general(
            pd, gq, (((0,), (0,)), ((), ())), preferred_element_type=jnp.float32
        )
        for j, span in enumerate(spans):
            acc_ref[span, :] += dkv[j * BLOCK : (j + 1) * BLOCK]
        return 0

    lax.fori_loop(0, blocks, one_block, 0, unroll=unroll)

    @pl.when(step == pl.num_programs(0) - 1)
    def _():
        def scaled(first, size):
            lanes = lax.broadcasted_iota(jnp.int32, (size, PAIR), 1) < HEAD_DIM
            tile = acc_ref[pl.ds(first, size), :]
            return jnp.where(lanes, tile * score_scale, tile)

        rim_ref[:face] = scaled(0, face).astype(rim_ref.dtype)
        rim_ref[face:] = scaled(face + own, face).astype(rim_ref.dtype)
        face_ref[:face] = scaled(face, face)
        face_ref[face:] = scaled(own, face)
        mid_ref[...] = scaled(2 * face, own - 2 * face).astype(mid_ref.dtype)


def attention(pattern, valid_rows, start, qg, kv, before, after, unroll=2):
    tokens, keys_num = qg.shape[0], pattern.shape[1]
    own, face = kv.shape[0], before.shape[0]
    rows = math.gcd(tokens, 8 * BLOCK)
    smem = pl.BlockSpec(memory_space=pltpu.SMEM)
    raw = pl.BlockSpec(memory_space=pl.ANY)
    tile = pl.BlockSpec((rows, PAIR), lambda i: (i, 0))

    def whole(size):
        return pl.BlockSpec((size, PAIR), lambda i: (0, 0))

    return pl.pallas_call(
        partial(attention_kernel, keys_num=keys_num, unroll=unroll),
        out_shape=(
            jax.ShapeDtypeStruct((tokens, PAIR), qg.dtype),
            jax.ShapeDtypeStruct((own - 2 * face, PAIR), qg.dtype),
            jax.ShapeDtypeStruct((2 * face, PAIR), jnp.float32),
            jax.ShapeDtypeStruct((2 * face, PAIR), qg.dtype),
        ),
        grid=(tokens // rows,),
        in_specs=[smem, smem, smem, tile, raw, raw, raw],
        out_specs=(tile, whole(own - 2 * face), whole(2 * face), whole(2 * face)),
        scratch_shapes=[
            pltpu.VMEM((own + 2 * face, PAIR), qg.dtype),
            pltpu.VMEM((own + 2 * face, PAIR), jnp.float32),
            pltpu.SemaphoreType.DMA((3,)),
        ],
        compiler_params=pltpu.CompilerParams(vmem_limit_bytes=40 << 20),
        name="block_attention",
    )(pattern.reshape(-1), valid_rows, start, qg, kv, before, after)


def body(query, key, value, grad_out, pattern, valid_rows):
    def exchange(x):
        return lax.all_to_all(x, "seq", split_axis=0, concat_axis=0, tiled=True)

    size = lax.axis_size("slab")
    up = [(i, i + 1) for i in range(size - 1)]
    down = [(i + 1, i) for i in range(size - 1)]
    shards, face = lax.axis_size("seq"), FACE * BLOCK
    kv = exchange(pack_heads(key, value))
    qg = exchange(pack_heads(query, grad_out))
    kv = kv.reshape(-1, PAIR)
    qg = qg.reshape(-1, PAIR)
    own = kv.shape[0]
    before = lax.ppermute(kv[own - face :], "slab", up)
    after = lax.ppermute(kv[:face], "slab", down)
    start = (lax.axis_index("slab") * pattern.shape[0] - FACE).astype(jnp.int32).reshape(1)
    od, mid, faces, rims = attention(pattern, valid_rows, start, qg, kv, before, after)
    od = exchange(od.reshape(shards, -1, PAIR))
    to_before = lax.ppermute(rims[:face], "slab", down)
    to_after = lax.ppermute(rims[face:], "slab", up)
    first = (faces[:face] + to_after.astype(jnp.float32)).astype(mid.dtype)
    last = (faces[face:] + to_before.astype(jnp.float32)).astype(mid.dtype)
    dkv = exchange(jnp.concatenate([first, mid, last], axis=0).reshape(shards, -1, PAIR))
    grad_query, attn_out = unpack_heads(od)
    grad_key, grad_value = unpack_heads(dkv)
    return (attn_out, grad_query, grad_key, grad_value)


def solution(mesh):
    rows = P(("slab", "seq"), None)
    return jax.shard_map(
        body,
        mesh=mesh,
        in_specs=(rows, rows, rows, rows, P("slab", None), P()),
        out_specs=(rows, rows, rows, rows),
        check_vma=False,
    )
```

time: 579 us -> 240 us (0.41); the launches traced: 570 us -> 239 us
  matrix products: 201 us -> 0 us
  local copies, waits for them, and re-layouts: 168 us -> 6.56 us
  Pallas kernels: 0 us -> 102 us
  other arithmetic: 65.9 us -> 1.62 us
  starting transfers between devices: 51.2 us -> 32 us
  waiting for transfers between devices: 81.2 us -> 95.2 us
    dot_general x56 -> x0, matrix products: 183 us -> none  [the longest x8 72.7 us: block_step(): jnp.einsum('qke,qkbc->ebc', selector, lower_part, preferred_element_type=...]
    pallas_call x0 -> x5, Pallas kernels: none -> 102 us  [the longest x1 78.2 us: attention(): pl.pallas_call(partial(attention_kernel, keys_num=keys_num, unroll=unroll...]
    slice x28 -> x2, local copies, waits for them, and re-layouts: 89.5 us -> 0.07 us  [the longest x1 0.04 us: body(): after = lax.ppermute(kv[:face], 'slab', down)]
    convert_element_type x24 -> x1, other arithmetic: 40 us -> 0.13 us  [body(): first = (faces[:face] + to_after.astype(jnp.float32)).astype(mid.dtype)]
    all_to_all x8 -> x4, starting transfers between devices: 40.1 us -> 20.7 us  [exchange(): return lax.all_to_all(x, 'seq', split_axis=0, concat_axis=0, tiled=True)]
    while x16 -> x0, matrix products: 18.5 us -> none
    all_to_all x9 -> x0, local copies, waits for them, and re-layouts: 16 us -> none  [the longest x2 4.79 us: body(): lax.all_to_all(dq_heads, 'seq', split_axis=0, concat_axis=1, tiled=True)]
    unnamed x29 -> x21, local copies, waits for them, and re-layouts: 21.6 us -> 6.4 us
  transfers between devices with their start and end apart: 12 -> 8, of which waited for: 7 -> 6; matrix products, arithmetic and copies ran while one was open for 8% -> 1% of each run, Pallas kernels for 0% -> 5%
where the time goes in v1:
time: 240 us; the launch traced here: 239 us
  Pallas kernels  102 us (42%)
  waiting for transfers between devices  95.2 us (40%)
  starting transfers between devices  32 us (13%)
  local copies, waits for them, and re-layouts  6.56 us (3%)
    all_to_all x4, waiting for transfers between devices, exchange(): return lax.all_to_all(x, 'seq', split_axis=0, concat_axis=0, tiled=True)  91.3 us
    pallas_call x1, Pallas kernels, attention(): pl.pallas_call(partial(attention_kernel, keys_num=keys_num, unroll=unroll...  78.2 us
    all_to_all x4, starting transfers between devices, exchange(): return lax.all_to_all(x, 'seq', split_axis=0, concat_axis=0, tiled=True)  20.7 us
    pallas_call x2, Pallas kernels, pack_heads(): pl.pallas_call(pack_kernel, out_shape=jax.ShapeDtypeStruct((heads, rows,...  12.4 us
    pallas_call x2, Pallas kernels, unpack_heads(): pl.pallas_call(unpack_kernel, out_shape=(full, full), grid=(heads // 2,),...  11.9 us
    unnamed x21, local copies, waits for them, and re-layouts  6.4 us
  transfers between devices with their start and end apart: 8, of which 6 were waited for; matrix products, arithmetic and copies ran while one was open for 1% of the time, Pallas kernels for 5%

profile of v1, /device:TPU:2, one launch (start us, length us, event | category | flops | bytes accessed | tf_op | source)
XLA Modules:
  0.0 238.7 jit_solution(17028729147355948816)
XLA Ops:
  0.6 6.2 %pack_heads.3 = bf16[16,512,128]{2,1,0:T(8,128)(2,1)} custom-call(bf16[512,1024]{1,0:T(8,128)(2,1)} %a_ref.3, bf16[512,1024]{1,0:T(8,128)(2,1)} %b_ref.3), custom_call_target="tpu_custom_call" | custom-call | tf_op jit(solution)/shard_map/pack_heads/pallas_call | solution.py:30
  6.9 8.0 %all-to-all-start.1 = ((bf16[16,512,128]{2,1,0:T(8,128)(2,1)}), bf16[16,512,128]{2,1,0:T(8,128)(2,1)S(1)}, u32[]{:S(2)}, u32[]{:S(2)}) async-start(bf16[16,512,128]{2,1,0:T(8,128)(2,1)} %pack_heads.3), calls=%async_computation.1 | async-start | bytes 4194304 | tf_op jit(solution)/shard_map/all_to_all | solution.py:178
  14.9 6.2 %pack_heads.2 = bf16[16,512,128]{2,1,0:T(8,128)(2,1)} custom-call(bf16[512,1024]{1,0:T(8,128)(2,1)} %a_ref.2, bf16[512,1024]{1,0:T(8,128)(2,1)} %b_ref.2), custom_call_target="tpu_custom_call" | custom-call | tf_op jit(solution)/shard_map/pack_heads/pallas_call | solution.py:30
  21.1 0.0 copy-start.9
  21.1 0.0 copy-start.7
  21.1 25.5 %all-to-all-done.1 = bf16[16,512,128]{2,1,0:T(8,128)(2,1)S(1)} async-done(((bf16[16,512,128]{2,1,0:T(8,128)(2,1)}), bf16[16,512,128]{2,1,0:T(8,128)(2,1)S(1)}, u32[]{:S(2)}, u32[]{:S(2)}) %all-to-all-start.1) | async-done | bytes 2097184 | tf_op jit(solution)/shard_map/all_to_all | solution.py:178
  46.6 4.4 %all-to-all-start = ((bf16[16,512,128]{2,1,0:T(8,128)(2,1)}), bf16[16,512,128]{2,1,0:T(8,128)(2,1)}, u32[]{:S(2)}, u32[]{:S(2)}) async-start(bf16[16,512,128]{2,1,0:T(8,128)(2,1)} %pack_heads.2), calls=%async_computation | async-start | bytes 4194304 | tf_op jit(solution)/shard_map/all_to_all | solution.py:178
  51.0 1.9 collective-permute-start
  53.0 3.6 %collective-permute-start.1 = (bf16[1024,128]{1,0:T(8,128)(2,1)S(1)}, bf16[1024,128]{1,0:T(8,128)(2,1)S(1)}, u32[]{:S(2)}, u32[]{:S(2)}) collective-permute-start(bf16[1024,128]{1,0:T(8,128)(2,1)S(1)} %bitcast.9), channel_id=1, source_target_pairs={{16,0},{32,16},{48,32},{64,48},{80,64},{96,80},{112,96},{17,1},{33... | collective-permute-start | bytes 786440 | tf_op jit(solution)/shard_map/ppermute | solution.py:190
  56.6 0.0 copy-done.9
  56.6 0.1 copy.10
  56.7 0.1 reshape.28.pattern_ref
  56.8 23.5 %all-to-all-done = bf16[16,512,128]{2,1,0:T(8,128)(2,1)} async-done(((bf16[16,512,128]{2,1,0:T(8,128)(2,1)}), bf16[16,512,128]{2,1,0:T(8,128)(2,1)}, u32[]{:S(2)}, u32[]{:S(2)}) %all-to-all-start) | async-done | bytes 2097184 | tf_op jit(solution)/shard_map/all_to_all | solution.py:178
  80.4 0.0 collective-permute-done.before_hbm
  80.4 0.0 collective-permute-done.1.after_hbm
  80.4 0.0 copy-start.5
  80.4 0.7 copy-done.5
  81.1 0.0 copy-done.7
  81.1 0.0 copy-start.6
  81.1 0.9 copy-done.6
  82.0 78.2 %block_attention.1 = (bf16[8192,128]{1,0:T(8,128)(2,1)S(1)}, bf16[6144,128]{1,0:T(8,128)(2,1)S(1)}, f32[2048,128]{1,0:T(8,128)S(1)}, bf16[2048,128]{1,0:T(8,128)(2,1)S(1)}) custom-call(s32[1024]{0:T(1024)S(1)} %reshape.28.pattern_ref, s32[1024]{0:T(1024)S(1)} %copy-done.7, s32[1]{0:T(128)} %bitcast.start_ref, bf16[8192,128]{1,0:T(8,128)(2,1)} %bitcast.1.qg_ref, ...), custom_call_target="tpu_custom_call" | custom-call | tf_op jit(solution)/shard_map/block_attention/pallas_call | solution.py:155
  160.2 0.0 copy-start
  160.2 1.3 copy-done
  161.6 0.0 copy-start.1
  161.6 1.2 copy-done.1
  162.7 0.0 copy-start.3
  162.7 0.8 copy-done.3
  163.5 0.0 copy-start.4
  163.5 4.6 %all-to-all-start.2 = ((bf16[16,512,128]{2,1,0:T(8,128)(2,1)}), bf16[16,512,128]{2,1,0:T(8,128)(2,1)}, u32[]{:S(2)}, u32[]{:S(2)}) async-start(bf16[16,512,128]{2,1,0:T(8,128)(2,1)} %bitcast.8), calls=%async_computation.2 | async-start | bytes 4194304 | tf_op jit(solution)/shard_map/all_to_all | solution.py:178
  168.1 0.0 copy-start.2
  168.1 0.0 copy-done.4
  168.2 2.1 collective-permute-start.2
  170.2 3.6 %collective-permute-start.3 = (bf16[1024,128]{1,0:T(8,128)(2,1)S(1)}, bf16[1024,128]{1,0:T(8,128)(2,1)S(1)}, u32[]{:S(2)}, u32[]{:S(2)}) collective-permute-start(bf16[1024,128]{1,0:T(8,128)(2,1)S(1)} %get-tuple-element.25), channel_id=1, source_target_pairs={{16,0},{32,16},{48,32},{64,48},{80,64},{96,80},{112,96},{17,1},{33... | collective-permute-start | bytes 786440 | tf_op jit(solution)/shard_map/ppermute | solution.py:194
  173.9 2.1 collective-permute-done.2
  176.0 1.8 collective-permute-done.3
  177.7 0.1 add_convert_fusion.1
  177.9 0.0 copy-done.2
  177.9 1.5 pad_maximum_fusion
  179.4 18.0 %all-to-all-done.2.x_ref = bf16[16,512,128]{2,1,0:T(8,128)(2,1)} async-done(((bf16[16,512,128]{2,1,0:T(8,128)(2,1)}), bf16[16,512,128]{2,1,0:T(8,128)(2,1)}, u32[]{:S(2)}, u32[]{:S(2)}) %all-to-all-start.2) | async-done | bytes 2097184 | tf_op jit(solution)/shard_map/all_to_all | solution.py:178
  197.4 3.7 %all-to-all-start.3 = ((bf16[16,512,128]{2,1,0:T(8,128)(2,1)}), bf16[16,512,128]{2,1,0:T(8,128)(2,1)S(1)}, u32[]{:S(2)}, u32[]{:S(2)}) async-start(bf16[16,512,128]{2,1,0:T(8,128)(2,1)} %bitcast.6), calls=%async_computation.3 | async-start | bytes 4194304 | tf_op jit(solution)/shard_map/all_to_all | solution.py:178
  201.1 5.9 %unpack_heads.2 = (bf16[512,1024]{1,0:T(8,128)(2,1)}, bf16[512,1024]{1,0:T(8,128)(2,1)}) custom-call(bf16[16,512,128]{2,1,0:T(8,128)(2,1)} %all-to-all-done.2.x_ref), custom_call_target="tpu_custom_call" | custom-call | tf_op jit(solution)/shard_map/unpack_heads/pallas_call | solution.py:50
  207.0 24.3 %all-to-all-done.3.x_ref = bf16[16,512,128]{2,1,0:T(8,128)(2,1)S(1)} async-done(((bf16[16,512,128]{2,1,0:T(8,128)(2,1)}), bf16[16,512,128]{2,1,0:T(8,128)(2,1)S(1)}, u32[]{:S(2)}, u32[]{:S(2)}) %all-to-all-start.3) | async-done | bytes 2097184 | tf_op jit(solution)/shard_map/all_to_all | solution.py:178
  231.4 0.0 copy-start.8
  231.4 1.3 copy-done.8
  232.7 5.9 %unpack_heads.3 = (bf16[512,1024]{1,0:T(8,128)(2,1)}, bf16[512,1024]{1,0:T(8,128)(2,1)}) custom-call(bf16[16,512,128]{2,1,0:T(8,128)(2,1)} %copy-done.8), custom_call_target="tpu_custom_call" | custom-call | tf_op jit(solution)/shard_map/unpack_heads/pallas_call | solution.py:50
  (2 shorter events, 0.1 us)
Async XLA Ops:
  6.9 39.7 %all-to-all-start.1 = ((bf16[16,512,128]{2,1,0:T(8,128)(2,1)}), bf16[16,512,128]{2,1,0:T(8,128)(2,1)S(1)}, u32[]{:S(2)}, u32[]{:S(2)}) async-start(bf16[16,512,128]{2,1,0:T(8,128)(2,1)} %pack_heads.3), calls=%async_computation.1 | async-start | bytes 4194304 | tf_op jit(solution)/shard_map/all_to_all | solution.py:178
  21.1 35.5 %copy-start.9 = (s32[128,8]{0,1:T(8,128)S(1)}, s32[128,8]{0,1:T(8,128)}, u32[]{:S(2)}) copy-start(s32[128,8]{0,1:T(8,128)} %param.10) | copy-start | bytes 12292
  21.1 60.0 %copy-start.7 = (s32[1024]{0:T(1024)S(1)}, s32[1024]{0:T(1024)}, u32[]{:S(2)}) copy-start(s32[1024]{0:T(1024)} %valid_ref.1) | copy-start | bytes 12292
  46.6 33.8 %all-to-all-start = ((bf16[16,512,128]{2,1,0:T(8,128)(2,1)}), bf16[16,512,128]{2,1,0:T(8,128)(2,1)}, u32[]{:S(2)}, u32[]{:S(2)}) async-start(bf16[16,512,128]{2,1,0:T(8,128)(2,1)} %pack_heads.2), calls=%async_computation | async-start | bytes 4194304 | tf_op jit(solution)/shard_map/all_to_all | solution.py:178
  51.0 29.3 %collective-permute-start = (bf16[1024,128]{1,0:T(8,128)(2,1)S(1)}, bf16[1024,128]{1,0:T(8,128)(2,1)S(1)}, u32[]{:S(2)}, u32[]{:S(2)}) collective-permute-start(bf16[1024,128]{1,0:T(8,128)(2,1)S(1)} %bitcast.10), channel_id=1, source_target_pairs={{0,16},{16,32},{32,48},{48,64},{64,80},{80,96},{96,112},{1,17},{17... | collective-permute-start | bytes 786440 | tf_op jit(solution)/shard_map/ppermute | solution.py:189
  53.0 27.4 %collective-permute-start.1 = (bf16[1024,128]{1,0:T(8,128)(2,1)S(1)}, bf16[1024,128]{1,0:T(8,128)(2,1)S(1)}, u32[]{:S(2)}, u32[]{:S(2)}) collective-permute-start(bf16[1024,128]{1,0:T(8,128)(2,1)S(1)} %bitcast.9), channel_id=1, source_target_pairs={{16,0},{32,16},{48,32},{64,48},{80,64},{96,80},{112,96},{17,1},{33... | collective-permute-start | bytes 786440 | tf_op jit(solution)/shard_map/ppermute | solution.py:190
  80.4 0.7 copy-start.5
  81.1 1.0 copy-start.6
  160.2 1.3 copy-start
  161.6 1.2 copy-start.1
  162.7 0.8 copy-start.3
  163.5 4.6 %copy-start.4 = (bf16[2048,128]{1,0:T(8,128)(2,1)S(1)}, bf16[2048,128]{1,0:T(8,128)(2,1)}, u32[]{:S(2)}) copy-start(bf16[2048,128]{1,0:T(8,128)(2,1)} %copy-done.3) | copy-start | bytes 1572868
  163.5 33.8 %all-to-all-start.2 = ((bf16[16,512,128]{2,1,0:T(8,128)(2,1)}), bf16[16,512,128]{2,1,0:T(8,128)(2,1)}, u32[]{:S(2)}, u32[]{:S(2)}) async-start(bf16[16,512,128]{2,1,0:T(8,128)(2,1)} %bitcast.8), calls=%async_computation.2 | async-start | bytes 4194304 | tf_op jit(solution)/shard_map/all_to_all | solution.py:178
  168.1 9.8 %copy-start.2 = (bf16[6144,128]{1,0:T(8,128)(2,1)S(1)}, bf16[6144,128]{1,0:T(8,128)(2,1)}, u32[]{:S(2)}) copy-start(bf16[6144,128]{1,0:T(8,128)(2,1)} %copy-done.1) | copy-start | bytes 4718596
  168.2 7.8 %collective-permute-start.2 = (bf16[1024,128]{1,0:T(8,128)(2,1)S(1)}, bf16[1024,128]{1,0:T(8,128)(2,1)S(1)}, u32[]{:S(2)}, u32[]{:S(2)}) collective-permute-start(bf16[1024,128]{1,0:T(8,128)(2,1)S(1)} %get-tuple-element.24), channel_id=1, source_target_pairs={{0,16},{16,32},{32,48},{48,64},{64,80},{80,96},{96,112},{1,17},{17... | collective-permute-start | bytes 786440 | tf_op jit(solution)/shard_map/ppermute | solution.py:195
  170.2 7.5 %collective-permute-start.3 = (bf16[1024,128]{1,0:T(8,128)(2,1)S(1)}, bf16[1024,128]{1,0:T(8,128)(2,1)S(1)}, u32[]{:S(2)}, u32[]{:S(2)}) collective-permute-start(bf16[1024,128]{1,0:T(8,128)(2,1)S(1)} %get-tuple-element.25), channel_id=1, source_target_pairs={{16,0},{32,16},{48,32},{64,48},{80,64},{96,80},{112,96},{17,1},{33... | collective-permute-start | bytes 786440 | tf_op jit(solution)/shard_map/ppermute | solution.py:194
  197.4 34.0 %all-to-all-start.3 = ((bf16[16,512,128]{2,1,0:T(8,128)(2,1)}), bf16[16,512,128]{2,1,0:T(8,128)(2,1)S(1)}, u32[]{:S(2)}, u32[]{:S(2)}) async-start(bf16[16,512,128]{2,1,0:T(8,128)(2,1)} %bitcast.6), calls=%async_computation.3 | async-start | bytes 4194304 | tf_op jit(solution)/shard_map/all_to_all | solution.py:178
  231.4 1.3 copy-start.8

commit v2 on v1

v2 whole, which is shorter than its diff:
```python
from functools import partial
import math

import jax
import jax.numpy as jnp
from jax import lax
from jax.experimental import pallas as pl
from jax.experimental.pallas import tpu as pltpu
from jax.sharding import PartitionSpec as P

HEAD_DIM = 64
BLOCK = 64
FACE = 16
PAIR = 2 * HEAD_DIM
WIDE = 4

score_scale = 0.125
exp2_scale = score_scale * math.log2(math.e)


def swap_halves(a, b):
    low = jnp.concatenate([a[:, :HEAD_DIM], b[:, :HEAD_DIM]], axis=1)
    high = jnp.concatenate([a[:, HEAD_DIM:], b[:, HEAD_DIM:]], axis=1)
    return low, high


def pack_kernel(k_ref, v_ref, q_ref, g_ref, out_ref):
    rows = k_ref.shape[0]
    for p in range(k_ref.shape[1] // PAIR):
        cols = slice(p * PAIR, (p + 1) * PAIR)
        for at, (a_ref, b_ref) in enumerate(((k_ref, v_ref), (q_ref, g_ref))):
            low, high = swap_halves(a_ref[:, cols], b_ref[:, cols])
            out_ref[2 * p, at * rows : (at + 1) * rows] = low
            out_ref[2 * p + 1, at * rows : (at + 1) * rows] = high


def pack_heads(k, v, q, g):
    rows, cols = k.shape
    width = WIDE * PAIR
    part = pl.BlockSpec((rows, width), lambda i: (0, i))
    return pl.pallas_call(
        pack_kernel,
        out_shape=jax.ShapeDtypeStruct((cols // HEAD_DIM, 2 * rows, PAIR), k.dtype),
        grid=(cols // width,),
        in_specs=[part] * 4,
        out_specs=pl.BlockSpec((2 * WIDE, 2 * rows, PAIR), lambda i: (i, 0, 0)),
        compiler_params=pltpu.CompilerParams(vmem_limit_bytes=40 << 20),
        name="pack_heads",
    )(k, v, q, g)


def unpack_kernel(x_ref, k_ref, v_ref, q_ref, o_ref):
    rows = k_ref.shape[0]
    for p in range(k_ref.shape[1] // PAIR):
        cols = slice(p * PAIR, (p + 1) * PAIR)
        for at, (a_ref, b_ref) in enumerate(((k_ref, v_ref), (q_ref, o_ref))):
            part = slice(at * rows, (at + 1) * rows)
            a_ref[:, cols], b_ref[:, cols] = swap_halves(x_ref[2 * p, part], x_ref[2 * p + 1, part])


def unpack_heads(x):
    heads, rows, _ = x.shape
    rows //= 2
    width = WIDE * PAIR
    part = pl.BlockSpec((rows, width), lambda i: (0, i))
    return pl.pallas_call(
        unpack_kernel,
        out_shape=(jax.ShapeDtypeStruct((rows, heads * HEAD_DIM), x.dtype),) * 4,
        grid=(heads * HEAD_DIM // width,),
        in_specs=[pl.BlockSpec((2 * WIDE, 2 * rows, PAIR), lambda i: (i, 0, 0))],
        out_specs=(part,) * 4,
        compiler_params=pltpu.CompilerParams(vmem_limit_bytes=40 << 20),
        name="unpack_heads",
    )(x)


def attention_kernel(
    pattern_ref, valid_ref, start_ref, x_hbm, before_hbm, after_hbm,
    z_hbm, first_ref, last_ref, down_ref, up_ref,
    kv_ref, qg_ref, acc_ref, od_ref, dkv_ref, both_ref, pd_ref, in_sems, od_sems, dkv_sems,
    *, keys_num, group, lines,
):
    shards, rows = qg_ref.shape[:2]
    edge = before_hbm.shape[0]
    each = rows // BLOCK

    def fetch(source, i):
        return pltpu.make_async_copy(source, kv_ref.at[pl.ds(i * rows, rows)], in_sems.at[i])

    copies = [fetch(x_hbm.at[t, pl.ds(0, rows)], edge + t) for t in range(shards)]
    copies += [fetch(before_hbm.at[t], t) for t in range(edge)]
    copies += [fetch(after_hbm.at[t], edge + shards + t) for t in range(edge)]
    copies += [
        pltpu.make_async_copy(x_hbm.at[:, pl.ds(rows, rows)], qg_ref, in_sems.at[len(copies)])
    ]
    for copy in copies:
        copy.start()
    acc_ref[...] = jnp.zeros_like(acc_ref)
    for copy in copies:
        copy.wait()

    start = start_ref[0]
    low = lax.broadcasted_iota(jnp.int32, (BLOCK, PAIR), 1) < HEAD_DIM
    lane = lax.broadcasted_iota(jnp.int32, (1, PAIR), 1)

    def send_od(t):
        return pltpu.make_async_copy(od_ref.at[t], z_hbm.at[t, pl.ds(rows, rows)], od_sems.at[t])

    def send_dkv(t):
        return pltpu.make_async_copy(dkv_ref.at[t], z_hbm.at[t, pl.ds(0, rows)], dkv_sems.at[t])

    def one_group(t, _):
        meta = []
        for u in range(group):
            base = (t * group + u) * keys_num
            slots = [pattern_ref[base + j] for j in range(keys_num)]
            counts = [valid_ref[start + slot] for slot in slots]
            meta.append((u // each, slice(u % each * BLOCK, (u % each + 1) * BLOCK), slots, counts))
        shard = t * (group // each)

        def gathered(slots):
            return jnp.concatenate(
                [kv_ref[pl.ds(pl.multiple_of(slot * BLOCK, BLOCK), BLOCK), :] for slot in slots],
                axis=0,
            )

        def spread(s, part):
            qg = qg_ref[shard + s, part, :]
            zero = jnp.zeros_like(qg)
            return jnp.concatenate([jnp.where(low, zero, qg), jnp.where(low, qg, zero)], axis=0)

        for u, (s, part, slots, counts) in enumerate(meta):
            both_ref[u] = lax.dot_general(
                spread(s, part), gathered(slots), (((1,), (1,)), ((), ())),
                preferred_element_type=jnp.float32,
            )
        for u, (s, part, slots, counts) in enumerate(meta):
            bias = jnp.concatenate(
                [
                    jnp.where(
                        lane < jnp.where(lane < HEAD_DIM, counts[j], counts[j + 1] + HEAD_DIM),
                        0.0,
                        -jnp.inf,
                    )
                    for j in range(0, keys_num, 2)
                ],
                axis=1,
            )
            for r in range(0, BLOCK, lines):
                scores = both_ref[u, BLOCK + r : BLOCK + r + lines, :] + bias
                top = jnp.max(scores, axis=1, keepdims=True)
                weight = jnp.exp2((scores - top) * exp2_scale)
                total = jnp.sum(weight, axis=1, keepdims=True)
                prob = (weight * (1.0 / total)).astype(jnp.bfloat16)
                prob_wide = prob.astype(jnp.float32)
                grad_prob = both_ref[u, r : r + lines, :]
                delta = jnp.sum(prob_wide * grad_prob, axis=1, keepdims=True)
                dscore = (prob_wide * (grad_prob - delta)).astype(jnp.bfloat16)
                pd_ref[u, r : r + lines, :] = prob
                pd_ref[u, BLOCK + r : BLOCK + r + lines, :] = dscore
        for u, (s, part, slots, counts) in enumerate(meta):
            od = jnp.dot(pd_ref[u], gathered(slots), preferred_element_type=jnp.float32)
            od_ref[shard + s, part, :] = jnp.where(
                low, od[BLOCK:] * score_scale, od[:BLOCK]
            ).astype(od_ref.dtype)
        for s in range(group // each):
            send_od(shard + s).start()
        for u, (s, part, slots, counts) in enumerate(meta):
            dkv = lax.dot_general(
                pd_ref[u], spread(s, part), (((0,), (0,)), ((), ())),
                preferred_element_type=jnp.float32,
            )
            for j, slot in enumerate(slots):
                span = pl.ds(pl.multiple_of(slot * BLOCK, BLOCK), BLOCK)
                acc_ref[span, :] += dkv[j * BLOCK : (j + 1) * BLOCK]
        return 0

    lax.fori_loop(0, shards * each // group, one_group, 0)

    wide_low = lax.broadcasted_iota(jnp.int32, (rows, PAIR), 1) < HEAD_DIM

    def scaled(s):
        tile = acc_ref[s * rows : (s + 1) * rows, :]
        return jnp.where(wide_low, tile * score_scale, tile)

    for s in range(edge):
        down_ref[s] = scaled(s).astype(down_ref.dtype)
        up_ref[s] = scaled(edge + shards + s).astype(up_ref.dtype)
        first_ref[s] = scaled(edge + s)
        last_ref[s] = scaled(shards + s)
    for t in range(edge, shards - edge):
        dkv_ref[t] = scaled(edge + t).astype(dkv_ref.dtype)
        send_dkv(t).start()
    for t in range(shards):
        send_od(t).wait()
    for t in range(edge, shards - edge):
        send_dkv(t).wait()


def attention(pattern, valid_rows, start, x, before, after, group=16, lines=16):
    keys_num = pattern.shape[1]
    shards, rows = x.shape[0], x.shape[1] // 2
    edge = before.shape[0]
    ext = shards + 2 * edge
    smem = pl.BlockSpec(memory_space=pltpu.SMEM)
    raw = pl.BlockSpec(memory_space=pl.ANY)
    vmem = pl.BlockSpec(memory_space=pltpu.VMEM)
    face = (edge, rows, PAIR)
    return pl.pallas_call(
        partial(attention_kernel, keys_num=keys_num, group=group, lines=lines),
        out_shape=(jax.ShapeDtypeStruct(x.shape, x.dtype),)
        + (jax.ShapeDtypeStruct(face, jnp.float32),) * 2
        + (jax.ShapeDtypeStruct(face, x.dtype),) * 2,
        in_specs=[smem, smem, smem, raw, raw, raw],
        out_specs=(raw, vmem, vmem, vmem, vmem),
        scratch_shapes=[
            pltpu.VMEM((ext * rows, PAIR), x.dtype),
            pltpu.VMEM((shards, rows, PAIR), x.dtype),
            pltpu.VMEM((ext * rows, PAIR), jnp.float32),
            pltpu.VMEM((shards, rows, PAIR), x.dtype),
            pltpu.VMEM((shards, rows, PAIR), x.dtype),
            pltpu.VMEM((group, PAIR, keys_num * BLOCK), jnp.float32),
            pltpu.VMEM((group, PAIR, keys_num * BLOCK), x.dtype),
            pltpu.SemaphoreType.DMA((ext + 1,)),
            pltpu.SemaphoreType.DMA((shards,)),
            pltpu.SemaphoreType.DMA((shards,)),
        ],
        compiler_params=pltpu.CompilerParams(vmem_limit_bytes=40 << 20),
        name="block_attention",
    )(pattern.reshape(-1), valid_rows, start, x, before, after)


def join_kernel(z_in, first_ref, last_ref, low_ref, high_ref, z_hbm, sum_ref, sems):
    edge, rows = first_ref.shape[:2]
    shards = z_hbm.shape[0]
    sum_ref[0] = (first_ref[...] + low_ref[...].astype(jnp.float32)).astype(sum_ref.dtype)
    sum_ref[1] = (last_ref[...] + high_ref[...].astype(jnp.float32)).astype(sum_ref.dtype)
    copies = [
        pltpu.make_async_copy(
            sum_ref.at[i], z_hbm.at[pl.ds(at, edge), pl.ds(0, rows)], sems.at[i]
        )
        for i, at in enumerate((0, shards - edge))
    ]
    for copy in copies:
        copy.start()
    for copy in copies:
        copy.wait()


def join_faces(z, first, last, low, high):
    raw = pl.BlockSpec(memory_space=pl.ANY)
    vmem = pl.BlockSpec(memory_space=pltpu.VMEM)
    return pl.pallas_call(
        join_kernel,
        out_shape=jax.ShapeDtypeStruct(z.shape, z.dtype),
        in_specs=[raw, vmem, vmem, vmem, vmem],
        out_specs=raw,
        scratch_shapes=[pltpu.VMEM((2, *low.shape), z.dtype), pltpu.SemaphoreType.DMA((2,))],
        input_output_aliases={0: 0},
        name="join_faces",
    )(z, first, last, low, high)


def body(query, key, value, grad_out, pattern, valid_rows):
    def exchange(x):
        return lax.all_to_all(x, "seq", split_axis=0, concat_axis=0, tiled=True)

    size = lax.axis_size("slab")
    up = [(i, i + 1) for i in range(size - 1)]
    down = [(i + 1, i) for i in range(size - 1)]
    rows = query.shape[0]
    edge = FACE * BLOCK // rows
    x = exchange(pack_heads(key, value, query, grad_out))
    before = lax.ppermute(x[x.shape[0] - edge :, :rows], "slab", up)
    after = lax.ppermute(x[:edge, :rows], "slab", down)
    start = (lax.axis_index("slab") * pattern.shape[0] - FACE).astype(jnp.int32).reshape(1)
    z, first, last, to_before, to_after = attention(pattern, valid_rows, start, x, before, after)
    high = lax.ppermute(to_before, "slab", down)
    low = lax.ppermute(to_after, "slab", up)
    z = exchange(join_faces(z, first, last, low, high))
    grad_key, grad_value, grad_query, attn_out = unpack_heads(z)
    return (attn_out, grad_query, grad_key, grad_value)


def solution(mesh):
    rows = P(("slab", "seq"), None)
    return jax.shard_map(
        body,
        mesh=mesh,
        in_specs=(rows, rows, rows, rows, P("slab", None), P()),
        out_specs=(rows, rows, rows, rows),
        check_vma=False,
    )
```

time: 240 us -> 190 us (0.79)
  blocking collectives: 0 us -> 114 us
  waiting for transfers between devices: 95.2 us -> 8.93 us
  Pallas kernels: 102 us -> 41.3 us
  starting transfers between devices: 32 us -> 9.87 us
  local copies, waits for them, and re-layouts: 6.56 us -> 13.5 us
    all_to_all x0 -> x2, blocking collectives: none -> 114 us  [exchange(): return lax.all_to_all(x, 'seq', split_axis=0, concat_axis=0, tiled=True)]
    all_to_all x4 -> x0, waiting for transfers between devices: 91.3 us -> none  [exchange(): return lax.all_to_all(x, 'seq', split_axis=0, concat_axis=0, tiled=True)]
    pallas_call x5 -> x4, Pallas kernels: 102 us -> 41.3 us  [the longest x1 34.9 us: attention(): pl.pallas_call(partial(attention_kernel, keys_num=keys_num, group=group,...]
    all_to_all x4 -> x0, starting transfers between devices: 20.7 us -> none  [exchange(): return lax.all_to_all(x, 'seq', split_axis=0, concat_axis=0, tiled=True)]
    unnamed x21 -> x27, local copies, waits for them, and re-layouts: 6.4 us -> 13.4 us
    ppermute x4, waiting for transfers between devices: 3.87 us -> 8.93 us  [the longest x1 3.82 us: body(): before = lax.ppermute(x[x.shape[0] - edge:, :rows], 'slab', up)]
  transfers between devices with their start and end apart: 8 -> 4, of which waited for: 6 -> 4; matrix products, arithmetic and copies ran while one was open for 1% -> 0% of each run, Pallas kernels for 5% -> 0%
where the time goes in v2:
time: 190 us; the launch traced here: 189 us
  blocking collectives  114 us (60%)
  Pallas kernels  41.3 us (22%)
  local copies, waits for them, and re-layouts  13.5 us (7%)
  starting transfers between devices  9.87 us (5%)
  waiting for transfers between devices  8.93 us (5%)
    all_to_all x2, blocking collectives, exchange(): return lax.all_to_all(x, 'seq', split_axis=0, concat_axis=0, tiled=True)  114 us
    pallas_call x1, Pallas kernels, attention(): pl.pallas_call(partial(attention_kernel, keys_num=keys_num, group=group,...  34.9 us
    unnamed x27, local copies, waits for them, and re-layouts  13.4 us
    ppermute x1, waiting for transfers between devices, body(): before = lax.ppermute(x[x.shape[0] - edge:, :rows], 'slab', up)  3.82 us
  transfers between devices with their start and end apart: 4, of which 4 were waited for; matrix products, arithmetic and copies ran while one was open for 0% of the time, Pallas kernels for 0%

profile of v2, /device:TPU:2, one launch (start us, length us, event | category | flops | bytes accessed | tf_op | source)
XLA Modules:
  0.0 188.6 jit_solution(17132984760389770544)
XLA Ops:
  0.6 0.0 copy-start.3
  0.6 1.2 copy-done.3
  1.9 0.0 copy-start.4
  1.9 1.2 copy-done.4
  3.1 0.0 copy-start.5
  3.1 1.2 copy-done.5
  4.3 0.0 copy-start.6
  4.3 1.2 copy-done.6
  5.5 1.5 pack_heads.1
  7.1 0.0 copy-start.12
  7.1 0.0 copy-start.9
  7.1 58.7 %all_to_all.10.x_hbm = bf16[16,1024,128]{2,1,0:T(8,128)(2,1)S(1)} all-to-all(bf16[16,1024,128]{2,1,0:T(8,128)(2,1)S(1)} %pack_heads.1), channel_id=1, replica_groups=mesh['slab'=8,'seq'=16] {'seq'}, dimensions={0} | all-to-all | bytes 8388608 | tf_op jit(solution)/shard_map/all_to_all | solution.py:266
  65.9 0.0 copy-start
  65.9 1.9 %copy-done = bf16[16,1024,128]{2,1,0:T(8,128)(2,1)} copy-done((bf16[16,1024,128]{2,1,0:T(8,128)(2,1)}, bf16[16,1024,128]{2,1,0:T(8,128)(2,1)S(1)}, u32[]{:S(2)}) %copy-start) | copy-done | bytes 4194328
  67.8 1.9 %collective-permute-start.1 = (bf16[2,512,128]{2,1,0:T(8,128)(2,1)S(1)}, bf16[2,512,128]{2,1,0:T(8,128)(2,1)S(1)}, u32[]{:S(2)}, u32[]{:S(2)}) collective-permute-start(bf16[2,512,128]{2,1,0:T(8,128)(2,1)S(1)} %get-tuple-element.22), channel_id=1, source_target_pairs={{16,0},{32,16},{48,32},{64,48},{80,64},{96,80},{112,96},{17,1},{33... | collective-permute-start | bytes 786440 | tf_op jit(solution)/shard_map/ppermute | solution.py:275
  69.7 2.4 %collective-permute-start = (bf16[2,512,128]{2,1,0:T(8,128)(2,1)S(1)}, bf16[2,512,128]{2,1,0:T(8,128)(2,1)S(1)}, u32[]{:S(2)}, u32[]{:S(2)}) collective-permute-start(bf16[2,512,128]{2,1,0:T(8,128)(2,1)S(1)} %get-tuple-element.23), channel_id=1, source_target_pairs={{0,16},{16,32},{32,48},{48,64},{64,80},{80,96},{96,112},{1,17},{17... | collective-permute-start | bytes 786440 | tf_op jit(solution)/shard_map/ppermute | solution.py:274
  72.1 0.0 copy-done.12
  72.2 0.1 copy.11
  72.3 0.1 reshape.14.pattern_ref
  72.3 1.2 collective-permute-done.1.after_hbm
  73.6 3.8 %collective-permute-done.before_hbm = bf16[2,512,128]{2,1,0:T(8,128)(2,1)S(1)} collective-permute-done((bf16[2,512,128]{2,1,0:T(8,128)(2,1)S(1)}, bf16[2,512,128]{2,1,0:T(8,128)(2,1)S(1)}, u32[]{:S(2)}, u32[]{:S(2)}) %collective-permute-start) | collective-permute-done | bytes 262176 | tf_op jit(solution)/shard_map/ppermute | solution.py:274
  77.4 0.0 copy-done.9
  77.4 0.0 copy-start.1
  77.4 2.2 %copy-done.1 = bf16[16,1024,128]{2,1,0:T(8,128)(2,1)S(1)} copy-done((bf16[16,1024,128]{2,1,0:T(8,128)(2,1)S(1)}, bf16[16,1024,128]{2,1,0:T(8,128)(2,1)}, u32[]{:S(2)}) %copy-start.1) | copy-done | bytes 4194328
  79.6 34.9 %block_attention.1 = (bf16[16,1024,128]{2,1,0:T(8,128)(2,1)S(1)}, f32[2,512,128]{2,1,0:T(8,128)S(1)}, f32[2,512,128]{2,1,0:T(8,128)S(1)}, bf16[2,512,128]{2,1,0:T(8,128)(2,1)S(1)}, bf16[2,512,128]{2,1,0:T(8,128)(2,1)S(1)}) custom-call(s32[1024]{0:T(1024)S(1)} %reshape.14.pattern_ref, s32[1024]{0:T(1024)S(1)} %copy-done.9, s32[1]{0:T(128)} %bitcast.start_ref, ...), custom_call_target="tpu_custom_call" | custom-call | tf_op jit(solution)/shard_map/block_attention/pallas_call | solution.py:209
  114.5 0.0 copy-start.2
  114.5 1.9 %copy-done.2 = bf16[16,1024,128]{2,1,0:T(8,128)(2,1)} copy-done((bf16[16,1024,128]{2,1,0:T(8,128)(2,1)}, bf16[16,1024,128]{2,1,0:T(8,128)(2,1)S(1)}, u32[]{:S(2)}) %copy-start.2) | copy-done | bytes 4194328
  116.5 0.0 copy-start.7
  116.5 0.8 copy-done.7
  117.3 0.0 copy-start.8
  117.3 0.8 copy-done.8
  118.1 1.9 %collective-permute-start.2 = (bf16[2,512,128]{2,1,0:T(8,128)(2,1)S(1)}, bf16[2,512,128]{2,1,0:T(8,128)(2,1)S(1)}, u32[]{:S(2)}, u32[]{:S(2)}) collective-permute-start(bf16[2,512,128]{2,1,0:T(8,128)(2,1)S(1)} %get-tuple-element.16), channel_id=1, source_target_pairs={{0,16},{16,32},{32,48},{48,64},{64,80},{80,96},{96,112},{1,17},{17... | collective-permute-start | bytes 786440 | tf_op jit(solution)/shard_map/ppermute | solution.py:279
  120.0 3.6 %collective-permute-start.3 = (bf16[2,512,128]{2,1,0:T(8,128)(2,1)S(1)}, bf16[2,512,128]{2,1,0:T(8,128)(2,1)S(1)}, u32[]{:S(2)}, u32[]{:S(2)}) collective-permute-start(bf16[2,512,128]{2,1,0:T(8,128)(2,1)S(1)} %get-tuple-element.17), channel_id=1, source_target_pairs={{16,0},{32,16},{48,32},{64,48},{80,64},{96,80},{112,96},{17,1},{33... | collective-permute-start | bytes 786440 | tf_op jit(solution)/shard_map/ppermute | solution.py:278
  123.6 2.1 %collective-permute-done.2.low_ref = bf16[2,512,128]{2,1,0:T(8,128)(2,1)S(1)} collective-permute-done((bf16[2,512,128]{2,1,0:T(8,128)(2,1)S(1)}, bf16[2,512,128]{2,1,0:T(8,128)(2,1)S(1)}, u32[]{:S(2)}, u32[]{:S(2)}) %collective-permute-start.2) | collective-permute-done | bytes 262176 | tf_op jit(solution)/shard_map/ppermute | solution.py:279
  125.8 0.0 copy-start.10
  125.8 1.8 collective-permute-done.3.high_ref
  127.5 0.0 copy-start.11
  127.5 0.0 copy-done.10
  127.5 0.7 copy-done.11
  128.2 2.3 %join_faces.1 = bf16[16,1024,128]{2,1,0:T(8,128)(2,1)} custom-call(bf16[16,1024,128]{2,1,0:T(8,128)(2,1)} %copy-done.2, f32[2,512,128]{2,1,0:T(8,128)} %copy-done.7, f32[2,512,128]{2,1,0:T(8,128)} %copy-done.8, bf16[2,512,128]{2,1,0:T(8,128)(2,1)} %copy-done.10, bf16[2,512,128]{2,1,0:T(8,128)(2,1)} %copy-done.11), custom_call_target="tpu_custom_call", output_to_operand_aliasing={{}: (0, {})} | custom-call | tf_op jit(solution)/shard_map/join_faces/pallas_call | solution.py:253
  130.5 55.5 %all_to_all.11.x_ref = bf16[16,1024,128]{2,1,0:T(8,128)(2,1)S(1)} all-to-all(bf16[16,1024,128]{2,1,0:T(8,128)(2,1)} %join_faces.1), channel_id=1, replica_groups=mesh['slab'=8,'seq'=16] {'seq'}, dimensions={0} | all-to-all | bytes 8388608 | tf_op jit(solution)/shard_map/all_to_all | solution.py:266
  186.0 2.5 %unpack_heads.1 = (bf16[512,1024]{1,0:T(8,128)(2,1)}, bf16[512,1024]{1,0:T(8,128)(2,1)}, bf16[512,1024]{1,0:T(8,128)(2,1)}, bf16[512,1024]{1,0:T(8,128)(2,1)}) custom-call(bf16[16,1024,128]{2,1,0:T(8,128)(2,1)S(1)} %all_to_all.11.x_ref), custom_call_target="tpu_custom_call" | custom-call | tf_op jit(solution)/shard_map/unpack_heads/pallas_call | solution.py:66
  (1 shorter events, 0.0 us)
Async XLA Ops:
  0.6 1.2 copy-start.3
  1.9 1.2 copy-start.4
  3.1 1.2 copy-start.5
  4.3 1.2 copy-start.6
  7.1 65.1 %copy-start.12 = (s32[128,8]{0,1:T(8,128)S(1)}, s32[128,8]{0,1:T(8,128)}, u32[]{:S(2)}) copy-start(s32[128,8]{0,1:T(8,128)} %param.10) | copy-start | bytes 12292
  7.1 70.3 %copy-start.9 = (s32[1024]{0:T(1024)S(1)}, s32[1024]{0:T(1024)}, u32[]{:S(2)}) copy-start(s32[1024]{0:T(1024)} %valid_ref.1) | copy-start | bytes 12292
  65.9 2.0 %copy-start = (bf16[16,1024,128]{2,1,0:T(8,128)(2,1)}, bf16[16,1024,128]{2,1,0:T(8,128)(2,1)S(1)}, u32[]{:S(2)}) copy-start(bf16[16,1024,128]{2,1,0:T(8,128)(2,1)S(1)} %all_to_all.10.x_hbm) | copy-start | bytes 12582916
  67.8 5.8 %collective-permute-start.1 = (bf16[2,512,128]{2,1,0:T(8,128)(2,1)S(1)}, bf16[2,512,128]{2,1,0:T(8,128)(2,1)S(1)}, u32[]{:S(2)}, u32[]{:S(2)}) collective-permute-start(bf16[2,512,128]{2,1,0:T(8,128)(2,1)S(1)} %get-tuple-element.22), channel_id=1, source_target_pairs={{16,0},{32,16},{48,32},{64,48},{80,64},{96,80},{112,96},{17,1},{33... | collective-permute-start | bytes 786440 | tf_op jit(solution)/shard_map/ppermute | solution.py:275
  69.7 7.7 %collective-permute-start = (bf16[2,512,128]{2,1,0:T(8,128)(2,1)S(1)}, bf16[2,512,128]{2,1,0:T(8,128)(2,1)S(1)}, u32[]{:S(2)}, u32[]{:S(2)}) collective-permute-start(bf16[2,512,128]{2,1,0:T(8,128)(2,1)S(1)} %get-tuple-element.23), channel_id=1, source_target_pairs={{0,16},{16,32},{32,48},{48,64},{64,80},{80,96},{96,112},{1,17},{17... | collective-permute-start | bytes 786440 | tf_op jit(solution)/shard_map/ppermute | solution.py:274
  77.4 2.2 %copy-start.1 = (bf16[16,1024,128]{2,1,0:T(8,128)(2,1)S(1)}, bf16[16,1024,128]{2,1,0:T(8,128)(2,1)}, u32[]{:S(2)}) copy-start(bf16[16,1024,128]{2,1,0:T(8,128)(2,1)} %copy-done) | copy-start | bytes 12582916
  114.5 2.0 %copy-start.2 = (bf16[16,1024,128]{2,1,0:T(8,128)(2,1)}, bf16[16,1024,128]{2,1,0:T(8,128)(2,1)S(1)}, u32[]{:S(2)}) copy-start(bf16[16,1024,128]{2,1,0:T(8,128)(2,1)S(1)} %get-tuple-element.13.z_in) | copy-start | bytes 12582916
  116.5 0.8 copy-start.7
  117.3 0.8 copy-start.8
  118.1 7.7 %collective-permute-start.2 = (bf16[2,512,128]{2,1,0:T(8,128)(2,1)S(1)}, bf16[2,512,128]{2,1,0:T(8,128)(2,1)S(1)}, u32[]{:S(2)}, u32[]{:S(2)}) collective-permute-start(bf16[2,512,128]{2,1,0:T(8,128)(2,1)S(1)} %get-tuple-element.16), channel_id=1, source_target_pairs={{0,16},{16,32},{32,48},{48,64},{64,80},{80,96},{96,112},{1,17},{17... | collective-permute-start | bytes 786440 | tf_op jit(solution)/shard_map/ppermute | solution.py:279
  120.0 7.5 %collective-permute-start.3 = (bf16[2,512,128]{2,1,0:T(8,128)(2,1)S(1)}, bf16[2,512,128]{2,1,0:T(8,128)(2,1)S(1)}, u32[]{:S(2)}, u32[]{:S(2)}) collective-permute-start(bf16[2,512,128]{2,1,0:T(8,128)(2,1)S(1)} %get-tuple-element.17), channel_id=1, source_target_pairs={{16,0},{32,16},{48,32},{64,48},{80,64},{96,80},{112,96},{17,1},{33... | collective-permute-start | bytes 786440 | tf_op jit(solution)/shard_map/ppermute | solution.py:278
  125.8 1.8 copy-start.10
  127.5 0.7 copy-start.11

commit v3 on v2

--- a/solution.py
+++ b/solution.py
@@ -16,6 +16,39 @@
 
 score_scale = 0.125
 exp2_scale = score_scale * math.log2(math.e)
+
+
+def on_chip(x):
+    return pltpu.with_memory_space_constraint(x, pltpu.VMEM)
+
+
+def off_chip(x):
+    return pltpu.with_memory_space_constraint(x, pltpu.HBM)
+
+
+def faces_kernel(x_hbm, first_ref, last_ref, sems):
+    edge, rows = first_ref.shape[:2]
+    copies = [
+        pltpu.make_async_copy(x_hbm.at[pl.ds(at, edge), pl.ds(0, rows)], ref, sems.at[i])
+        for i, (at, ref) in enumerate(((0, first_ref), (x_hbm.shape[0] - edge, last_ref)))
+    ]
+    for copy in copies:
+        copy.start()
+    for copy in copies:
+        copy.wait()
+
+
+def take_faces(x, edge, rows):
+    vmem = pl.BlockSpec(memory_space=pltpu.VMEM)
+    return pl.pallas_call(
+        faces_kernel,
+        out_shape=(pltpu.VMEM((edge, rows, PAIR), x.dtype),) * 2,
+        in_specs=[pl.BlockSpec(memory_space=pltpu.HBM)],
+        out_specs=(vmem, vmem),
+        scratch_shapes=[pltpu.SemaphoreType.DMA((2,))],
+        compiler_params=pltpu.CompilerParams(vmem_limit_bytes=4 << 20),
+        name="take_faces",
+    )(off_chip(x))
 
 
 def swap_halves(a, b):
@@ -44,7 +77,7 @@
         grid=(cols // width,),
         in_specs=[part] * 4,
         out_specs=pl.BlockSpec((2 * WIDE, 2 * rows, PAIR), lambda i: (i, 0, 0)),
-        compiler_params=pltpu.CompilerParams(vmem_limit_bytes=40 << 20),
+        compiler_params=pltpu.CompilerParams(vmem_limit_bytes=60 << 20),
         name="pack_heads",
     )(k, v, q, g)
 
@@ -69,27 +102,27 @@
         grid=(heads * HEAD_DIM // width,),
         in_specs=[pl.BlockSpec((2 * WIDE, 2 * rows, PAIR), lambda i: (i, 0, 0))],
         out_specs=(part,) * 4,
-        compiler_params=pltpu.CompilerParams(vmem_limit_bytes=40 << 20),
+        compiler_params=pltpu.CompilerParams(vmem_limit_bytes=60 << 20),
         name="unpack_heads",
     )(x)
 
 
 def attention_kernel(
-    pattern_ref, valid_ref, start_ref, x_hbm, before_hbm, after_hbm,
+    pattern_ref, valid_ref, start_ref, x_hbm, before_ref, after_ref,
     z_hbm, first_ref, last_ref, down_ref, up_ref,
     kv_ref, qg_ref, acc_ref, od_ref, dkv_ref, both_ref, pd_ref, in_sems, od_sems, dkv_sems,
     *, keys_num, group, lines,
 ):
-    shards, rows = qg_ref.shape[:2]
-    edge = before_hbm.shape[0]
+    shards, rows = od_ref.shape[:2]
+    edge = before_ref.shape[0]
     each = rows // BLOCK
 
     def fetch(source, i):
         return pltpu.make_async_copy(source, kv_ref.at[pl.ds(i * rows, rows)], in_sems.at[i])
 
     copies = [fetch(x_hbm.at[t, pl.ds(0, rows)], edge + t) for t in range(shards)]
-    copies += [fetch(before_hbm.at[t], t) for t in range(edge)]
-    copies += [fetch(after_hbm.at[t], edge + shards + t) for t in range(edge)]
+    copies += [fetch(before_ref.at[t], t) for t in range(edge)]
+    copies += [fetch(after_ref.at[t], edge + shards + t) for t in range(edge)]
     copies += [
         pltpu.make_async_copy(x_hbm.at[:, pl.ds(rows, rows)], qg_ref, in_sems.at[len(copies)])
     ]
@@ -203,16 +236,16 @@
     edge = before.shape[0]
     ext = shards + 2 * edge
     smem = pl.BlockSpec(memory_space=pltpu.SMEM)
-    raw = pl.BlockSpec(memory_space=pl.ANY)
+    hbm = pl.BlockSpec(memory_space=pltpu.HBM)
     vmem = pl.BlockSpec(memory_space=pltpu.VMEM)
     face = (edge, rows, PAIR)
     return pl.pallas_call(
         partial(attention_kernel, keys_num=keys_num, group=group, lines=lines),
-        out_shape=(jax.ShapeDtypeStruct(x.shape, x.dtype),)
-        + (jax.ShapeDtypeStruct(face, jnp.float32),) * 2
-        + (jax.ShapeDtypeStruct(face, x.dtype),) * 2,
-        in_specs=[smem, smem, smem, raw, raw, raw],
-        out_specs=(raw, vmem, vmem, vmem, vmem),
+        out_shape=(pltpu.HBM(x.shape, x.dtype),)
+        + (pltpu.VMEM(face, jnp.float32),) * 2
+        + (pltpu.VMEM(face, x.dtype),) * 2,
+        in_specs=[smem, smem, smem, hbm, vmem, vmem],
+        out_specs=(hbm, vmem, vmem, vmem, vmem),
         scratch_shapes=[
             pltpu.VMEM((ext * rows, PAIR), x.dtype),
             pltpu.VMEM((shards, rows, PAIR), x.dtype),
@@ -225,9 +258,9 @@
             pltpu.SemaphoreType.DMA((shards,)),
             pltpu.SemaphoreType.DMA((shards,)),
         ],
-        compiler_params=pltpu.CompilerParams(vmem_limit_bytes=40 << 20),
+        compiler_params=pltpu.CompilerParams(vmem_limit_bytes=32 << 20),
         name="block_attention",
-    )(pattern.reshape(-1), valid_rows, start, x, before, after)
+    )(pattern.reshape(-1), valid_rows, start, off_chip(x), on_chip(before), on_chip(after))
 
 
 def join_kernel(z_in, first_ref, last_ref, low_ref, high_ref, z_hbm, sum_ref, sems):
@@ -248,17 +281,18 @@
 
 
 def join_faces(z, first, last, low, high):
-    raw = pl.BlockSpec(memory_space=pl.ANY)
+    hbm = pl.BlockSpec(memory_space=pltpu.HBM)
     vmem = pl.BlockSpec(memory_space=pltpu.VMEM)
     return pl.pallas_call(
         join_kernel,
-        out_shape=jax.ShapeDtypeStruct(z.shape, z.dtype),
-        in_specs=[raw, vmem, vmem, vmem, vmem],
-        out_specs=raw,
+        out_shape=pltpu.HBM(z.shape, z.dtype),
+        in_specs=[hbm, vmem, vmem, vmem, vmem],
+        out_specs=hbm,
         scratch_shapes=[pltpu.VMEM((2, *low.shape), z.dtype), pltpu.SemaphoreType.DMA((2,))],
         input_output_aliases={0: 0},
+        compiler_params=pltpu.CompilerParams(vmem_limit_bytes=8 << 20),
         name="join_faces",
-    )(z, first, last, low, high)
+    )(z, *(on_chip(a) for a in (first, last, low, high)))
 
 
 def body(query, key, value, grad_out, pattern, valid_rows):
@@ -271,8 +305,9 @@
     rows = query.shape[0]
     edge = FACE * BLOCK // rows
     x = exchange(pack_heads(key, value, query, grad_out))
-    before = lax.ppermute(x[x.shape[0] - edge :, :rows], "slab", up)
-    after = lax.ppermute(x[:edge, :rows], "slab", down)
+    first, last = take_faces(x, edge, rows)
+    before = lax.ppermute(last, "slab", up)
+    after = lax.ppermute(first, "slab", down)
     start = (lax.axis_index("slab") * pattern.shape[0] - FACE).astype(jnp.int32).reshape(1)
     z, first, last, to_before, to_after = attention(pattern, valid_rows, start, x, before, after)
     high = lax.ppermute(to_before, "slab", down)

time: 190 us -> 173 us (0.911)
  local copies, waits for them, and re-layouts: 13.5 us -> 0.2 us
  Pallas kernels: 41.3 us -> 37 us
    unnamed x27 -> x5, local copies, waits for them, and re-layouts: 13.4 us -> 0.11 us
    pallas_call x1, Pallas kernels: 34.9 us -> 26.7 us  [attention(): pl.pallas_call(partial(attention_kernel, keys_num=keys_num, group=group,...]
    pallas_call x1, Pallas kernels: 1.54 us -> 4.13 us  [pack_heads(): pl.pallas_call(pack_kernel, out_shape=jax.ShapeDtypeStruct((cols // HEAD_...]
where the time goes in v3:
time: 173 us; the launch traced here: 172 us
  blocking collectives  115 us (66%)
  Pallas kernels  37 us (21%)
  starting transfers between devices  11.3 us (7%)
  waiting for transfers between devices  7.52 us (4%)
    all_to_all x2, blocking collectives, exchange(): return lax.all_to_all(x, 'seq', split_axis=0, concat_axis=0, tiled=True)  115 us
    pallas_call x1, Pallas kernels, attention(): pl.pallas_call(partial(attention_kernel, keys_num=keys_num, group=group,...  26.7 us
    pallas_call x1, Pallas kernels, pack_heads(): pl.pallas_call(pack_kernel, out_shape=jax.ShapeDtypeStruct((cols // HEAD_...  4.13 us
    pallas_call x1, Pallas kernels, unpack_heads(): pl.pallas_call(unpack_kernel, out_shape=(jax.ShapeDtypeStruct((rows, head...  4.13 us
    ppermute x1, starting transfers between devices, body(): low = lax.ppermute(to_after, 'slab', up)  3.73 us
    ppermute x1, starting transfers between devices, body(): after = lax.ppermute(first, 'slab', down)  3.64 us
  transfers between devices with their start and end apart: 4, of which 4 were waited for; matrix products, arithmetic and copies ran while one was open for 0% of the time, Pallas kernels for 0%

profile of v3, /device:TPU:2, one launch (start us, length us, event | category | flops | bytes accessed | tf_op | source)
XLA Modules:
  0.0 172.0 jit_solution(8515948237066853233)
XLA Ops:
  0.6 4.1 %pack_heads.1 = bf16[16,1024,128]{2,1,0:T(8,128)(2,1)} custom-call(bf16[512,1024]{1,0:T(8,128)(2,1)} %k_ref.1, bf16[512,1024]{1,0:T(8,128)(2,1)} %v_ref.1, bf16[512,1024]{1,0:T(8,128)(2,1)} %q_ref.1, bf16[512,1024]{1,0:T(8,128)(2,1)} %g_ref.1), custom_call_target="tpu_custom_call" | custom-call | tf_op jit(solution)/shard_map/pack_heads/pallas_call | solution.py:74
  4.8 59.0 %all_to_all.10.x_hbm = bf16[16,1024,128]{2,1,0:T(8,128)(2,1)} all-to-all(bf16[16,1024,128]{2,1,0:T(8,128)(2,1)} %pack_heads.1), channel_id=1, replica_groups=mesh['slab'=8,'seq'=16] {'seq'}, dimensions={0} | all-to-all | bytes 8388608 | tf_op jit(solution)/shard_map/all_to_all | solution.py:300
  63.8 0.0 copy-start.1
  63.8 0.0 copy-start
  63.8 1.1 take_faces.1
  64.9 1.9 %collective-permute-start = (bf16[2,512,128]{2,1,0:T(8,128)(2,1)S(1)}, bf16[2,512,128]{2,1,0:T(8,128)(2,1)S(1)}, u32[]{:S(2)}, u32[]{:S(2)}) collective-permute-start(bf16[2,512,128]{2,1,0:T(8,128)(2,1)S(1)} %get-tuple-element.15), channel_id=1, source_target_pairs={{0,16},{16,32},{32,48},{48,64},{64,80},{80,96},{96,112},{1,17},{17... | collective-permute-start | bytes 786440 | tf_op jit(solution)/shard_map/ppermute | solution.py:309
  66.8 3.6 %collective-permute-start.1 = (bf16[2,512,128]{2,1,0:T(8,128)(2,1)S(1)}, bf16[2,512,128]{2,1,0:T(8,128)(2,1)S(1)}, u32[]{:S(2)}, u32[]{:S(2)}) collective-permute-start(bf16[2,512,128]{2,1,0:T(8,128)(2,1)S(1)} %get-tuple-element.16), channel_id=1, source_target_pairs={{16,0},{32,16},{48,32},{64,48},{80,64},{96,80},{112,96},{17,1},{33... | collective-permute-start | bytes 786440 | tf_op jit(solution)/shard_map/ppermute | solution.py:310
  70.4 0.0 copy-done.1
  70.5 0.1 copy.11
  70.6 0.1 reshape.14.pattern_ref
  70.7 1.9 %collective-permute-done.before_ref = bf16[2,512,128]{2,1,0:T(8,128)(2,1)S(1)} collective-permute-done((bf16[2,512,128]{2,1,0:T(8,128)(2,1)S(1)}, bf16[2,512,128]{2,1,0:T(8,128)(2,1)S(1)}, u32[]{:S(2)}, u32[]{:S(2)}) %collective-permute-start) | collective-permute-done | bytes 262176 | tf_op jit(solution)/shard_map/ppermute | solution.py:309
  72.6 1.8 %collective-permute-done.1.after_ref = bf16[2,512,128]{2,1,0:T(8,128)(2,1)S(1)} collective-permute-done((bf16[2,512,128]{2,1,0:T(8,128)(2,1)S(1)}, bf16[2,512,128]{2,1,0:T(8,128)(2,1)S(1)}, u32[]{:S(2)}, u32[]{:S(2)}) %collective-permute-start.1) | collective-permute-done | bytes 262176 | tf_op jit(solution)/shard_map/ppermute | solution.py:310
  74.3 0.0 copy-done
  74.3 26.7 %block_attention.1 = (bf16[16,1024,128]{2,1,0:T(8,128)(2,1)}, f32[2,512,128]{2,1,0:T(8,128)S(1)}, f32[2,512,128]{2,1,0:T(8,128)S(1)}, bf16[2,512,128]{2,1,0:T(8,128)(2,1)S(1)}, bf16[2,512,128]{2,1,0:T(8,128)(2,1)S(1)}) custom-call(s32[1024]{0:T(1024)S(1)} %reshape.14.pattern_ref, s32[1024]{0:T(1024)S(1)} %copy-done, s32[1]{0:T(128)} %bitcast.start_ref, ...), custom_call_target="tpu_custom_call" | custom-call | tf_op jit(solution)/shard_map/block_attention/pallas_call | solution.py:242
  101.0 3.7 %collective-permute-start.2 = (bf16[2,512,128]{2,1,0:T(8,128)(2,1)S(1)}, bf16[2,512,128]{2,1,0:T(8,128)(2,1)S(1)}, u32[]{:S(2)}, u32[]{:S(2)}) collective-permute-start(bf16[2,512,128]{2,1,0:T(8,128)(2,1)S(1)} %get-tuple-element.20), channel_id=1, source_target_pairs={{0,16},{16,32},{32,48},{48,64},{64,80},{80,96},{96,112},{1,17},{17... | collective-permute-start | bytes 786440 | tf_op jit(solution)/shard_map/ppermute | solution.py:314
  104.8 2.0 %collective-permute-start.3 = (bf16[2,512,128]{2,1,0:T(8,128)(2,1)S(1)}, bf16[2,512,128]{2,1,0:T(8,128)(2,1)S(1)}, u32[]{:S(2)}, u32[]{:S(2)}) collective-permute-start(bf16[2,512,128]{2,1,0:T(8,128)(2,1)S(1)} %get-tuple-element.21), channel_id=1, source_target_pairs={{16,0},{32,16},{48,32},{64,48},{80,64},{96,80},{112,96},{17,1},{33... | collective-permute-start | bytes 786440 | tf_op jit(solution)/shard_map/ppermute | solution.py:313
  106.8 2.1 %collective-permute-done.2.low_ref = bf16[2,512,128]{2,1,0:T(8,128)(2,1)S(1)} collective-permute-done((bf16[2,512,128]{2,1,0:T(8,128)(2,1)S(1)}, bf16[2,512,128]{2,1,0:T(8,128)(2,1)S(1)}, u32[]{:S(2)}, u32[]{:S(2)}) %collective-permute-start.2) | collective-permute-done | bytes 262176 | tf_op jit(solution)/shard_map/ppermute | solution.py:314
  108.9 1.8 %collective-permute-done.3.high_ref = bf16[2,512,128]{2,1,0:T(8,128)(2,1)S(1)} collective-permute-done((bf16[2,512,128]{2,1,0:T(8,128)(2,1)S(1)}, bf16[2,512,128]{2,1,0:T(8,128)(2,1)S(1)}, u32[]{:S(2)}, u32[]{:S(2)}) %collective-permute-start.3) | collective-permute-done | bytes 262176 | tf_op jit(solution)/shard_map/ppermute | solution.py:313
  110.7 0.9 join_faces.1
  111.6 56.3 %all_to_all.11.x_ref = bf16[16,1024,128]{2,1,0:T(8,128)(2,1)} all-to-all(bf16[16,1024,128]{2,1,0:T(8,128)(2,1)} %join_faces.1), channel_id=1, replica_groups=mesh['slab'=8,'seq'=16] {'seq'}, dimensions={0} | all-to-all | bytes 8388608 | tf_op jit(solution)/shard_map/all_to_all | solution.py:300
  167.9 4.1 %unpack_heads.1 = (bf16[512,1024]{1,0:T(8,128)(2,1)}, bf16[512,1024]{1,0:T(8,128)(2,1)}, bf16[512,1024]{1,0:T(8,128)(2,1)}, bf16[512,1024]{1,0:T(8,128)(2,1)}) custom-call(bf16[16,1024,128]{2,1,0:T(8,128)(2,1)} %all_to_all.11.x_ref), custom_call_target="tpu_custom_call" | custom-call | tf_op jit(solution)/shard_map/unpack_heads/pallas_call | solution.py:99
Async XLA Ops:
  63.8 6.7 %copy-start.1 = (s32[128,8]{0,1:T(8,128)S(1)}, s32[128,8]{0,1:T(8,128)}, u32[]{:S(2)}) copy-start(s32[128,8]{0,1:T(8,128)} %param.10) | copy-start | bytes 12292
  63.8 10.5 %copy-start = (s32[1024]{0:T(1024)S(1)}, s32[1024]{0:T(1024)}, u32[]{:S(2)}) copy-start(s32[1024]{0:T(1024)} %valid_ref.1) | copy-start | bytes 12292
  64.9 7.7 %collective-permute-start = (bf16[2,512,128]{2,1,0:T(8,128)(2,1)S(1)}, bf16[2,512,128]{2,1,0:T(8,128)(2,1)S(1)}, u32[]{:S(2)}, u32[]{:S(2)}) collective-permute-start(bf16[2,512,128]{2,1,0:T(8,128)(2,1)S(1)} %get-tuple-element.15), channel_id=1, source_target_pairs={{0,16},{16,32},{32,48},{48,64},{64,80},{80,96},{96,112},{1,17},{17... | collective-permute-start | bytes 786440 | tf_op jit(solution)/shard_map/ppermute | solution.py:309
  66.8 7.5 %collective-permute-start.1 = (bf16[2,512,128]{2,1,0:T(8,128)(2,1)S(1)}, bf16[2,512,128]{2,1,0:T(8,128)(2,1)S(1)}, u32[]{:S(2)}, u32[]{:S(2)}) collective-permute-start(bf16[2,512,128]{2,1,0:T(8,128)(2,1)S(1)} %get-tuple-element.16), channel_id=1, source_target_pairs={{16,0},{32,16},{48,32},{64,48},{80,64},{96,80},{112,96},{17,1},{33... | collective-permute-start | bytes 786440 | tf_op jit(solution)/shard_map/ppermute | solution.py:310
  101.0 7.9 %collective-permute-start.2 = (bf16[2,512,128]{2,1,0:T(8,128)(2,1)S(1)}, bf16[2,512,128]{2,1,0:T(8,128)(2,1)S(1)}, u32[]{:S(2)}, u32[]{:S(2)}) collective-permute-start(bf16[2,512,128]{2,1,0:T(8,128)(2,1)S(1)} %get-tuple-element.20), channel_id=1, source_target_pairs={{0,16},{16,32},{32,48},{48,64},{64,80},{80,96},{96,112},{1,17},{17... | collective-permute-start | bytes 786440 | tf_op jit(solution)/shard_map/ppermute | solution.py:314
  104.8 5.9 %collective-permute-start.3 = (bf16[2,512,128]{2,1,0:T(8,128)(2,1)S(1)}, bf16[2,512,128]{2,1,0:T(8,128)(2,1)S(1)}, u32[]{:S(2)}, u32[]{:S(2)}) collective-permute-start(bf16[2,512,128]{2,1,0:T(8,128)(2,1)S(1)} %get-tuple-element.21), channel_id=1, source_target_pairs={{16,0},{32,16},{48,32},{64,48},{80,64},{96,80},{112,96},{17,1},{33... | collective-permute-start | bytes 786440 | tf_op jit(solution)/shard_map/ppermute | solution.py:313

commit v4 on v3

--- a/solution.py
+++ b/solution.py
@@ -57,99 +57,81 @@
     return low, high
 
 
-def pack_kernel(k_ref, v_ref, q_ref, g_ref, out_ref):
-    rows = k_ref.shape[0]
+def pack_kernel(k_ref, v_ref, q_ref, g_ref, one_ref, two_ref):
+    rows, half = k_ref.shape[0], two_ref.shape[1]
     for p in range(k_ref.shape[1] // PAIR):
         cols = slice(p * PAIR, (p + 1) * PAIR)
-        for at, (a_ref, b_ref) in enumerate(((k_ref, v_ref), (q_ref, g_ref))):
-            low, high = swap_halves(a_ref[:, cols], b_ref[:, cols])
-            out_ref[2 * p, at * rows : (at + 1) * rows] = low
-            out_ref[2 * p + 1, at * rows : (at + 1) * rows] = high
+        for i, pair in enumerate(swap_halves(k_ref[:, cols], v_ref[:, cols])):
+            one_ref[2 * p + i, :rows] = pair
+        for i, pair in enumerate(swap_halves(q_ref[:, cols], g_ref[:, cols])):
+            one_ref[2 * p + i, rows:] = pair[:half]
+            two_ref[2 * p + i] = pair[half:]
 
 
 def pack_heads(k, v, q, g):
     rows, cols = k.shape
+    heads, half = cols // HEAD_DIM, rows // 2
     width = WIDE * PAIR
     part = pl.BlockSpec((rows, width), lambda i: (0, i))
+    sizes = (rows + half, half)
     return pl.pallas_call(
         pack_kernel,
-        out_shape=jax.ShapeDtypeStruct((cols // HEAD_DIM, 2 * rows, PAIR), k.dtype),
+        out_shape=tuple(pltpu.HBM((heads, size, PAIR), k.dtype) for size in sizes),
         grid=(cols // width,),
         in_specs=[part] * 4,
-        out_specs=pl.BlockSpec((2 * WIDE, 2 * rows, PAIR), lambda i: (i, 0, 0)),
+        out_specs=tuple(pl.BlockSpec((2 * WIDE, size, PAIR), lambda i: (i, 0, 0)) for size in sizes),
         compiler_params=pltpu.CompilerParams(vmem_limit_bytes=60 << 20),
         name="pack_heads",
     )(k, v, q, g)
 
 
-def unpack_kernel(x_ref, k_ref, v_ref, q_ref, o_ref):
-    rows = k_ref.shape[0]
+def unpack_kernel(one_ref, two_ref, k_ref, v_ref, q_ref, o_ref):
+    rows, half = k_ref.shape[0], two_ref.shape[1]
     for p in range(k_ref.shape[1] // PAIR):
         cols = slice(p * PAIR, (p + 1) * PAIR)
-        for at, (a_ref, b_ref) in enumerate(((k_ref, v_ref), (q_ref, o_ref))):
-            part = slice(at * rows, (at + 1) * rows)
-            a_ref[:, cols], b_ref[:, cols] = swap_halves(x_ref[2 * p, part], x_ref[2 * p + 1, part])
-
-
-def unpack_heads(x):
-    heads, rows, _ = x.shape
-    rows //= 2
+        h, i = 2 * p, 2 * p + 1
+        k_ref[:, cols], v_ref[:, cols] = swap_halves(one_ref[h, :rows], one_ref[i, :rows])
+        q_ref[:half, cols], o_ref[:half, cols] = swap_halves(two_ref[h], two_ref[i])
+        q_ref[half:, cols], o_ref[half:, cols] = swap_halves(one_ref[h, rows:], one_ref[i, rows:])
+
+
+def unpack_heads(one, two):
+    heads, half, _ = two.shape
+    rows = 2 * half
     width = WIDE * PAIR
     part = pl.BlockSpec((rows, width), lambda i: (0, i))
     return pl.pallas_call(
         unpack_kernel,
-        out_shape=(jax.ShapeDtypeStruct((rows, heads * HEAD_DIM), x.dtype),) * 4,
+        out_shape=(jax.ShapeDtypeStruct((rows, heads * HEAD_DIM), one.dtype),) * 4,
         grid=(heads * HEAD_DIM // width,),
-        in_specs=[pl.BlockSpec((2 * WIDE, 2 * rows, PAIR), lambda i: (i, 0, 0))],
+        in_specs=[
+            pl.BlockSpec((2 * WIDE, x.shape[1], PAIR), lambda i: (i, 0, 0)) for x in (one, two)
+        ],
         out_specs=(part,) * 4,
         compiler_params=pltpu.CompilerParams(vmem_limit_bytes=60 << 20),
         name="unpack_heads",
-    )(x)
-
-
-def attention_kernel(
-    pattern_ref, valid_ref, start_ref, x_hbm, before_ref, after_ref,
-    z_hbm, first_ref, last_ref, down_ref, up_ref,
-    kv_ref, qg_ref, acc_ref, od_ref, dkv_ref, both_ref, pd_ref, in_sems, od_sems, dkv_sems,
-    *, keys_num, group, lines,
+    )(off_chip(one), off_chip(two))
+
+
+def query_blocks(
+    pattern_ref, valid_ref, start_ref, kv_ref, qg_ref, acc_ref, od_ref, both_ref, pd_ref, send_od,
+    *, keys_num, chunk, group, lines, ready=None,
 ):
-    shards, rows = od_ref.shape[:2]
-    edge = before_ref.shape[0]
+    shards, rows = qg_ref.shape[:2]
     each = rows // BLOCK
-
-    def fetch(source, i):
-        return pltpu.make_async_copy(source, kv_ref.at[pl.ds(i * rows, rows)], in_sems.at[i])
-
-    copies = [fetch(x_hbm.at[t, pl.ds(0, rows)], edge + t) for t in range(shards)]
-    copies += [fetch(before_ref.at[t], t) for t in range(edge)]
-    copies += [fetch(after_ref.at[t], edge + shards + t) for t in range(edge)]
-    copies += [
-        pltpu.make_async_copy(x_hbm.at[:, pl.ds(rows, rows)], qg_ref, in_sems.at[len(copies)])
-    ]
-    for copy in copies:
-        copy.start()
-    acc_ref[...] = jnp.zeros_like(acc_ref)
-    for copy in copies:
-        copy.wait()
-
     start = start_ref[0]
     low = lax.broadcasted_iota(jnp.int32, (BLOCK, PAIR), 1) < HEAD_DIM
     lane = lax.broadcasted_iota(jnp.int32, (1, PAIR), 1)
 
-    def send_od(t):
-        return pltpu.make_async_copy(od_ref.at[t], z_hbm.at[t, pl.ds(rows, rows)], od_sems.at[t])
-
-    def send_dkv(t):
-        return pltpu.make_async_copy(dkv_ref.at[t], z_hbm.at[t, pl.ds(0, rows)], dkv_sems.at[t])
-
     def one_group(t, _):
+        shard = t * (group // each)
         meta = []
         for u in range(group):
-            base = (t * group + u) * keys_num
+            s, i = u // each, u % each
+            base = ((shard + s) * 2 * each + chunk * each + i) * keys_num
             slots = [pattern_ref[base + j] for j in range(keys_num)]
             counts = [valid_ref[start + slot] for slot in slots]
-            meta.append((u // each, slice(u % each * BLOCK, (u % each + 1) * BLOCK), slots, counts))
-        shard = t * (group // each)
+            meta.append((s, slice(i * BLOCK, (i + 1) * BLOCK), slots, counts))
 
         def gathered(slots):
             return jnp.concatenate(
@@ -198,6 +180,8 @@
             ).astype(od_ref.dtype)
         for s in range(group // each):
             send_od(shard + s).start()
+        if ready is not None:
+            pl.when(t == 0)(ready)
         for u, (s, part, slots, counts) in enumerate(meta):
             dkv = lax.dot_general(
                 pd_ref[u], spread(s, part), (((0,), (0,)), ((), ())),
@@ -210,57 +194,164 @@
 
     lax.fori_loop(0, shards * each // group, one_group, 0)
 
-    wide_low = lax.broadcasted_iota(jnp.int32, (rows, PAIR), 1) < HEAD_DIM
+
+def first_kernel(
+    pattern_ref, valid_ref, start_ref, x_hbm, before_ref, after_ref,
+    od_hbm, kv_hbm, acc_hbm,
+    kv_ref, acc_ref, qg_ref, od_ref, both_ref, pd_ref, in_sems, od_sems, out_sems, **sizes,
+):
+    shards, half = qg_ref.shape[:2]
+    rows = x_hbm.shape[1] - half
+    edge = before_ref.shape[0]
+
+    def fetch(source, i):
+        return pltpu.make_async_copy(source, kv_ref.at[pl.ds(i * rows, rows)], in_sems.at[i])
+
+    copies = [fetch(x_hbm.at[t, pl.ds(0, rows)], edge + t) for t in range(shards)]
+    copies += [fetch(before_ref.at[t], t) for t in range(edge)]
+    copies += [fetch(after_ref.at[t], edge + shards + t) for t in range(edge)]
+    copies += [
+        pltpu.make_async_copy(x_hbm.at[:, pl.ds(rows, half)], qg_ref, in_sems.at[len(copies)])
+    ]
+    for copy in copies:
+        copy.start()
+    acc_ref[...] = jnp.zeros_like(acc_ref)
+    for copy in copies:
+        copy.wait()
+    keep = pltpu.make_async_copy(kv_ref, kv_hbm, out_sems.at[0])
+    keep.start()
+
+    def send_od(t):
+        return pltpu.make_async_copy(od_ref.at[t], od_hbm.at[t], od_sems.at[t])
+
+    query_blocks(
+        pattern_ref, valid_ref, start_ref, kv_ref, qg_ref, acc_ref, od_ref, both_ref, pd_ref,
+        send_od, chunk=0, **sizes,
+    )
+    total = pltpu.make_async_copy(acc_ref, acc_hbm, out_sems.at[1])
+    total.start()
+    for t in range(shards):
+        send_od(t).wait()
+    keep.wait()
+    total.wait()
+
+
+def second_kernel(
+    pattern_ref, valid_ref, start_ref, x_hbm, kv_hbm, acc_hbm,
+    z_hbm, first_ref, last_ref, down_ref, up_ref,
+    kv_ref, acc_ref, qg_ref, od_ref, dkv_ref, both_ref, pd_ref, in_sems, od_sems, dkv_sems, **sizes,
+):
+    shards, half = qg_ref.shape[:2]
+    rows = 2 * half
+    edge = first_ref.shape[0]
+    copies = [
+        pltpu.make_async_copy(source, target, in_sems.at[i])
+        for i, (source, target) in enumerate(((x_hbm, qg_ref), (kv_hbm, kv_ref), (acc_hbm, acc_ref)))
+    ]
+    for copy in copies:
+        copy.start()
+    copies[0].wait()
+    copies[1].wait()
+
+    def send_od(t):
+        return pltpu.make_async_copy(od_ref.at[t], z_hbm.at[t, pl.ds(rows, half)], od_sems.at[t])
+
+    def send_dkv(t):
+        return pltpu.make_async_copy(dkv_ref.at[t], z_hbm.at[t, pl.ds(0, rows)], dkv_sems.at[t])
+
+    query_blocks(
+        pattern_ref, valid_ref, start_ref, kv_ref, qg_ref, acc_ref, od_ref, both_ref, pd_ref,
+        send_od, chunk=1, ready=copies[2].wait, **sizes,
+    )
+    low = lax.broadcasted_iota(jnp.int32, (rows, PAIR), 1) < HEAD_DIM
 
     def scaled(s):
         tile = acc_ref[s * rows : (s + 1) * rows, :]
-        return jnp.where(wide_low, tile * score_scale, tile)
-
+        return jnp.where(low, tile * score_scale, tile)
+
+    for t in range(edge, shards - edge):
+        dkv_ref[t] = scaled(edge + t).astype(dkv_ref.dtype)
+        send_dkv(t).start()
     for s in range(edge):
         down_ref[s] = scaled(s).astype(down_ref.dtype)
         up_ref[s] = scaled(edge + shards + s).astype(up_ref.dtype)
         first_ref[s] = scaled(edge + s)
         last_ref[s] = scaled(shards + s)
-    for t in range(edge, shards - edge):
-        dkv_ref[t] = scaled(edge + t).astype(dkv_ref.dtype)
-        send_dkv(t).start()
     for t in range(shards):
         send_od(t).wait()
     for t in range(edge, shards - edge):
         send_dkv(t).wait()
 
 
-def attention(pattern, valid_rows, start, x, before, after, group=16, lines=16):
-    keys_num = pattern.shape[1]
-    shards, rows = x.shape[0], x.shape[1] // 2
-    edge = before.shape[0]
-    ext = shards + 2 * edge
+def cost(tokens, keys_num):
+    work = tokens * keys_num * BLOCK
+    return pl.CostEstimate(flops=12 * PAIR * work, transcendentals=work, bytes_accessed=16 << 20)
+
+
+def first_half(pattern, valid_rows, start, x, before, after, group=16, lines=16):
+    keys_num = pattern.shape[0] * BLOCK // (x.shape[0] * before.shape[1])
+    shards, edge, rows = x.shape[0], before.shape[0], before.shape[1]
+    half, ext = rows // 2, shards + 2 * edge
+    smem = pl.BlockSpec(memory_space=pltpu.SMEM)
+    hbm = pl.BlockSpec(memory_space=pltpu.HBM)
+    vmem = pl.BlockSpec(memory_space=pltpu.VMEM)
+    return pl.pallas_call(
+        partial(first_kernel, keys_num=keys_num, group=group, lines=lines),
+        out_shape=(
+            pltpu.HBM((shards, half, PAIR), x.dtype),
+            pltpu.HBM((ext * rows, PAIR), x.dtype),
+            pltpu.HBM((ext * rows, PAIR), jnp.float32),
+        ),
+        in_specs=[smem, smem, smem, hbm, vmem, vmem],
+        out_specs=(hbm, hbm, hbm),
+        scratch_shapes=[
+            pltpu.VMEM((ext * rows, PAIR), x.dtype),
+            pltpu.VMEM((ext * rows, PAIR), jnp.float32),
+            pltpu.VMEM((shards, half, PAIR), x.dtype),
+            pltpu.VMEM((shards, half, PAIR), x.dtype),
+            pltpu.VMEM((group, PAIR, keys_num * BLOCK), jnp.float32),
+            pltpu.VMEM((group, PAIR, keys_num * BLOCK), x.dtype),
+            pltpu.SemaphoreType.DMA((ext + 1,)),
+            pltpu.SemaphoreType.DMA((shards,)),
+            pltpu.SemaphoreType.DMA((2,)),
+        ],
+        compiler_params=pltpu.CompilerParams(vmem_limit_bytes=32 << 20),
+        cost_estimate=cost(shards * half, keys_num),
+        name="first_half",
+    )(pattern, valid_rows, start, off_chip(x), on_chip(before), on_chip(after))
+
+
+def second_half(pattern, valid_rows, start, x, kv, acc, edge, group=16, lines=16):
+    shards, half = x.shape[:2]
+    rows = 2 * half
+    keys_num = pattern.shape[0] * BLOCK // (shards * rows)
     smem = pl.BlockSpec(memory_space=pltpu.SMEM)
     hbm = pl.BlockSpec(memory_space=pltpu.HBM)
     vmem = pl.BlockSpec(memory_space=pltpu.VMEM)
     face = (edge, rows, PAIR)
     return pl.pallas_call(
-        partial(attention_kernel, keys_num=keys_num, group=group, lines=lines),
-        out_shape=(pltpu.HBM(x.shape, x.dtype),)
+        partial(second_kernel, keys_num=keys_num, group=group, lines=lines),
+        out_shape=(pltpu.HBM((shards, rows + half, PAIR), x.dtype),)
         + (pltpu.VMEM(face, jnp.float32),) * 2
         + (pltpu.VMEM(face, x.dtype),) * 2,
-        in_specs=[smem, smem, smem, hbm, vmem, vmem],
+        in_specs=[smem, smem, smem, hbm, hbm, hbm],
         out_specs=(hbm, vmem, vmem, vmem, vmem),
         scratch_shapes=[
-            pltpu.VMEM((ext * rows, PAIR), x.dtype),
-            pltpu.VMEM((shards, rows, PAIR), x.dtype),
-            pltpu.VMEM((ext * rows, PAIR), jnp.float32),
-            pltpu.VMEM((shards, rows, PAIR), x.dtype),
+            pltpu.VMEM(kv.shape, kv.dtype),
+            pltpu.VMEM(acc.shape, acc.dtype),
+            pltpu.VMEM((shards, half, PAIR), x.dtype),
+            pltpu.VMEM((shards, half, PAIR), x.dtype),
             pltpu.VMEM((shards, rows, PAIR), x.dtype),
             pltpu.VMEM((group, PAIR, keys_num * BLOCK), jnp.float32),
             pltpu.VMEM((group, PAIR, keys_num * BLOCK), x.dtype),
-            pltpu.SemaphoreType.DMA((ext + 1,)),
+            pltpu.SemaphoreType.DMA((3,)),
             pltpu.SemaphoreType.DMA((shards,)),
             pltpu.SemaphoreType.DMA((shards,)),
         ],
         compiler_params=pltpu.CompilerParams(vmem_limit_bytes=32 << 20),
-        name="block_attention",
-    )(pattern.reshape(-1), valid_rows, start, off_chip(x), on_chip(before), on_chip(after))
+        cost_estimate=cost(shards * half, keys_num),
+        name="second_half",
+    )(pattern, valid_rows, start, off_chip(x), off_chip(kv), off_chip(acc))
 
 
 def join_kernel(z_in, first_ref, last_ref, low_ref, high_ref, z_hbm, sum_ref, sems):
@@ -304,16 +395,21 @@
     down = [(i + 1, i) for i in range(size - 1)]
     rows = query.shape[0]
     edge = FACE * BLOCK // rows
-    x = exchange(pack_heads(key, value, query, grad_out))
-    first, last = take_faces(x, edge, rows)
+    one, two = pack_heads(key, value, query, grad_out)
+    one = exchange(one)
+    first, last = take_faces(one, edge, rows)
     before = lax.ppermute(last, "slab", up)
     after = lax.ppermute(first, "slab", down)
+    two = exchange(two)
     start = (lax.axis_index("slab") * pattern.shape[0] - FACE).astype(jnp.int32).reshape(1)
-    z, first, last, to_before, to_after = attention(pattern, valid_rows, start, x, before, after)
+    scalars = (pattern.reshape(-1), valid_rows, start)
+    od, kv, acc = first_half(*scalars, one, before, after)
+    od = exchange(od)
+    z, first, last, to_before, to_after = second_half(*scalars, two, kv, acc, edge)
     high = lax.ppermute(to_before, "slab", down)
     low = lax.ppermute(to_after, "slab", up)
     z = exchange(join_faces(z, first, last, low, high))
-    grad_key, grad_value, grad_query, attn_out = unpack_heads(z)
+    grad_key, grad_value, grad_query, attn_out = unpack_heads(z, od)
     return (attn_out, grad_query, grad_key, grad_value)
 
 

time: 173 us -> 173 us (level)
  blocking collectives: 115 us -> 95.9 us
  starting transfers between devices: 11.3 us -> 22.1 us
  Pallas kernels: 37 us -> 44.3 us
    all_to_all x2, blocking collectives: 115 us -> 95.9 us  [exchange(): return lax.all_to_all(x, 'seq', split_axis=0, concat_axis=0, tiled=True)]
    all_to_all x0 -> x2, starting transfers between devices: none -> 10.9 us  [exchange(): return lax.all_to_all(x, 'seq', split_axis=0, concat_axis=0, tiled=True)]
    pallas_call x2 -> x3, Pallas kernels: 30.8 us -> 38.2 us  [the longest x1 17.1 us: first_half(): pl.pallas_call(partial(first_kernel, keys_num=keys_num, group=group, line...]
  transfers between devices with their start and end apart: 4 -> 6, of which waited for: 4 -> 4; matrix products, arithmetic and copies ran while one was open for 0% -> 0% of each run, Pallas kernels for 0% -> 21%
where the time goes in v4:
time: 173 us; the launch traced here: 171 us
  blocking collectives  95.9 us (55%)
  Pallas kernels  44.3 us (26%)
  starting transfers between devices  22.1 us (13%)
  waiting for transfers between devices  7.53 us (4%)
    all_to_all x2, blocking collectives, exchange(): return lax.all_to_all(x, 'seq', split_axis=0, concat_axis=0, tiled=True)  95.9 us
    pallas_call x1, Pallas kernels, first_half(): pl.pallas_call(partial(first_kernel, keys_num=keys_num, group=group, line...  17.1 us
    pallas_call x1, Pallas kernels, second_half(): pl.pallas_call(partial(second_kernel, keys_num=keys_num, group=group, lin...  17 us
    all_to_all x2, starting transfers between devices, exchange(): return lax.all_to_all(x, 'seq', split_axis=0, concat_axis=0, tiled=True)  10.9 us
    pallas_call x1, Pallas kernels, pack_heads(): pl.pallas_call(pack_kernel, out_shape=tuple((pltpu.HBM((heads, size, PAIR...  4.13 us
    pallas_call x1, Pallas kernels, unpack_heads(): pl.pallas_call(unpack_kernel, out_shape=(jax.ShapeDtypeStruct((rows, head...  4.05 us
    ppermute x1, starting transfers between devices, body(): after = lax.ppermute(first, 'slab', down)  3.64 us
  transfers between devices with their start and end apart: 6, of which 4 were waited for; matrix products, arithmetic and copies ran while one was open for 0% of the time, Pallas kernels for 21%

profile of v4, /device:TPU:2, one launch (start us, length us, event | category | flops | bytes accessed | tf_op | source)
XLA Modules:
  0.0 170.8 jit_solution(15201607186142133878)
XLA Ops:
  0.6 4.1 %pack_heads.1 = (bf16[16,768,128]{2,1,0:T(8,128)(2,1)}, bf16[16,256,128]{2,1,0:T(8,128)(2,1)}) custom-call(bf16[512,1024]{1,0:T(8,128)(2,1)} %k_ref.1, bf16[512,1024]{1,0:T(8,128)(2,1)} %v_ref.1, bf16[512,1024]{1,0:T(8,128)(2,1)} %q_ref.1, bf16[512,1024]{1,0:T(8,128)(2,1)} %g_ref.1), custom_call_target="tpu_custom_call" | custom-call | tf_op jit(solution)/shard_map/pack_heads/pallas_call | solution.py:77
  4.8 47.8 %all_to_all.20.x_hbm = bf16[16,768,128]{2,1,0:T(8,128)(2,1)} all-to-all(bf16[16,768,128]{2,1,0:T(8,128)(2,1)} %get-tuple-element.21), channel_id=1, replica_groups=mesh['slab'=8,'seq'=16] {'seq'}, dimensions={0} | all-to-all | bytes 6291456 | tf_op jit(solution)/shard_map/all_to_all | solution.py:391
  52.5 0.0 copy-start.3
  52.5 0.0 copy-start
  52.5 3.8 %all-to-all-start = ((bf16[16,256,128]{2,1,0:T(8,128)(2,1)}), bf16[16,256,128]{2,1,0:T(8,128)(2,1)S(1)}, u32[]{:S(2)}, u32[]{:S(2)}) async-start(bf16[16,256,128]{2,1,0:T(8,128)(2,1)} %get-tuple-element.20), calls=%async_computation | async-start | bytes 2097152 | tf_op jit(solution)/shard_map/all_to_all | solution.py:391
  56.3 1.0 take_faces.1
  57.4 1.9 %collective-permute-start = (bf16[2,512,128]{2,1,0:T(8,128)(2,1)S(1)}, bf16[2,512,128]{2,1,0:T(8,128)(2,1)S(1)}, u32[]{:S(2)}, u32[]{:S(2)}) collective-permute-start(bf16[2,512,128]{2,1,0:T(8,128)(2,1)S(1)} %get-tuple-element.22), channel_id=1, source_target_pairs={{0,16},{16,32},{32,48},{48,64},{64,80},{80,96},{96,112},{1,17},{17... | collective-permute-start | bytes 786440 | tf_op jit(solution)/shard_map/ppermute | solution.py:401
  59.3 3.6 %collective-permute-start.1 = (bf16[2,512,128]{2,1,0:T(8,128)(2,1)S(1)}, bf16[2,512,128]{2,1,0:T(8,128)(2,1)S(1)}, u32[]{:S(2)}, u32[]{:S(2)}) collective-permute-start(bf16[2,512,128]{2,1,0:T(8,128)(2,1)S(1)} %get-tuple-element.23), channel_id=1, source_target_pairs={{16,0},{32,16},{48,32},{64,48},{80,64},{96,80},{112,96},{17,1},{33... | collective-permute-start | bytes 786440 | tf_op jit(solution)/shard_map/ppermute | solution.py:402
  63.0 0.0 copy-done.3
  63.0 0.1 copy.11
  63.1 0.1 reshape.14.pattern_ref
  63.2 1.9 %collective-permute-done.before_ref = bf16[2,512,128]{2,1,0:T(8,128)(2,1)S(1)} collective-permute-done((bf16[2,512,128]{2,1,0:T(8,128)(2,1)S(1)}, bf16[2,512,128]{2,1,0:T(8,128)(2,1)S(1)}, u32[]{:S(2)}, u32[]{:S(2)}) %collective-permute-start) | collective-permute-done | bytes 262176 | tf_op jit(solution)/shard_map/ppermute | solution.py:401
  65.1 1.8 %collective-permute-done.1.after_ref = bf16[2,512,128]{2,1,0:T(8,128)(2,1)S(1)} collective-permute-done((bf16[2,512,128]{2,1,0:T(8,128)(2,1)S(1)}, bf16[2,512,128]{2,1,0:T(8,128)(2,1)S(1)}, u32[]{:S(2)}, u32[]{:S(2)}) %collective-permute-start.1) | collective-permute-done | bytes 262176 | tf_op jit(solution)/shard_map/ppermute | solution.py:402
  66.8 0.0 copy-done
  66.8 17.1 %first_half.1 = (bf16[16,256,128]{2,1,0:T(8,128)(2,1)}, bf16[10240,128]{1,0:T(8,128)(2,1)}, f32[10240,128]{1,0:T(8,128)}) custom-call(s32[1024]{0:T(1024)S(1)} %reshape.14.pattern_ref, s32[1024]{0:T(1024)S(1)} %copy-done, s32[1]{0:T(128)} %bitcast.start_ref, bf16[16,768,128]{2,1,0:T(8,128)(2,1)} %all_to_all.20.x_hbm, ...), custom_call_target="tpu_custom_call" | custom-call | flops 3221225472 | bytes 16777216 | tf_op jit(solution)/shard_map/first_half/pallas_call | solution.py:298
  83.9 0.0 all-to-all-done.x_hbm
  84.0 0.0 copy-start.2
  84.0 7.2 %all-to-all-start.3 = ((bf16[16,256,128]{2,1,0:T(8,128)(2,1)}), bf16[16,256,128]{2,1,0:T(8,128)(2,1)S(1)}, u32[]{:S(2)}, u32[]{:S(2)}) async-start(bf16[16,256,128]{2,1,0:T(8,128)(2,1)} %get-tuple-element.31), calls=%async_computation.3 | async-start | bytes 2097152 | tf_op jit(solution)/shard_map/all_to_all | solution.py:391
  91.1 0.0 copy-done.2
  91.1 17.0 %second_half.1 = (bf16[16,768,128]{2,1,0:T(8,128)(2,1)}, f32[2,512,128]{2,1,0:T(8,128)S(1)}, f32[2,512,128]{2,1,0:T(8,128)S(1)}, bf16[2,512,128]{2,1,0:T(8,128)(2,1)S(1)}, bf16[2,512,128]{2,1,0:T(8,128)(2,1)S(1)}) custom-call(s32[1024]{0:T(1024)S(1)} %reshape.14.pattern_ref, s32[1024]{0:T(1024)S(1)} %copy-done, s32[1]{0:T(128)} %bitcast.start_ref, ...), custom_call_target="tpu_custom_call" | custom-call | flops 3221225472 | bytes 16777216 | tf_op jit(solution)/shard_map/second_half/pallas_call | solution.py:332
  108.1 3.4 %collective-permute-start.2 = (bf16[2,512,128]{2,1,0:T(8,128)(2,1)S(1)}, bf16[2,512,128]{2,1,0:T(8,128)(2,1)S(1)}, u32[]{:S(2)}, u32[]{:S(2)}) collective-permute-start(bf16[2,512,128]{2,1,0:T(8,128)(2,1)S(1)} %get-tuple-element.29), channel_id=1, source_target_pairs={{0,16},{16,32},{32,48},{48,64},{64,80},{80,96},{96,112},{1,17},{17... | collective-permute-start | bytes 786440 | tf_op jit(solution)/shard_map/ppermute | solution.py:410
  111.5 2.2 %collective-permute-start.3 = (bf16[2,512,128]{2,1,0:T(8,128)(2,1)S(1)}, bf16[2,512,128]{2,1,0:T(8,128)(2,1)S(1)}, u32[]{:S(2)}, u32[]{:S(2)}) collective-permute-start(bf16[2,512,128]{2,1,0:T(8,128)(2,1)S(1)} %get-tuple-element.30), channel_id=1, source_target_pairs={{16,0},{32,16},{48,32},{64,48},{80,64},{96,80},{112,96},{17,1},{33... | collective-permute-start | bytes 786440 | tf_op jit(solution)/shard_map/ppermute | solution.py:409
  113.7 2.1 %collective-permute-done.2.low_ref = bf16[2,512,128]{2,1,0:T(8,128)(2,1)S(1)} collective-permute-done((bf16[2,512,128]{2,1,0:T(8,128)(2,1)S(1)}, bf16[2,512,128]{2,1,0:T(8,128)(2,1)S(1)}, u32[]{:S(2)}, u32[]{:S(2)}) %collective-permute-start.2) | collective-permute-done | bytes 262176 | tf_op jit(solution)/shard_map/ppermute | solution.py:410
  115.8 1.8 %collective-permute-done.3.high_ref = bf16[2,512,128]{2,1,0:T(8,128)(2,1)S(1)} collective-permute-done((bf16[2,512,128]{2,1,0:T(8,128)(2,1)S(1)}, bf16[2,512,128]{2,1,0:T(8,128)(2,1)S(1)}, u32[]{:S(2)}, u32[]{:S(2)}) %collective-permute-start.3) | collective-permute-done | bytes 262176 | tf_op jit(solution)/shard_map/ppermute | solution.py:409
  117.6 1.0 join_faces.1
  118.6 0.0 all-to-all-done.3.two_ref
  118.6 0.0 copy-start.1
  118.6 48.1 %all_to_all.21.one_ref = bf16[16,768,128]{2,1,0:T(8,128)(2,1)} all-to-all(bf16[16,768,128]{2,1,0:T(8,128)(2,1)} %join_faces.1), channel_id=1, replica_groups=mesh['slab'=8,'seq'=16] {'seq'}, dimensions={0} | all-to-all | bytes 6291456 | tf_op jit(solution)/shard_map/all_to_all | solution.py:391
  166.7 0.0 copy-done.1
  166.7 4.1 %unpack_heads.1 = (bf16[512,1024]{1,0:T(8,128)(2,1)}, bf16[512,1024]{1,0:T(8,128)(2,1)}, bf16[512,1024]{1,0:T(8,128)(2,1)}, bf16[512,1024]{1,0:T(8,128)(2,1)}) custom-call(bf16[16,768,128]{2,1,0:T(8,128)(2,1)} %all_to_all.21.one_ref, bf16[16,256,128]{2,1,0:T(8,128)(2,1)} %copy-done.1), custom_call_target="tpu_custom_call" | custom-call | tf_op jit(solution)/shard_map/unpack_heads/pallas_call | solution.py:103
Async XLA Ops:
  52.5 10.4 %copy-start.3 = (s32[128,8]{0,1:T(8,128)S(1)}, s32[128,8]{0,1:T(8,128)}, u32[]{:S(2)}) copy-start(s32[128,8]{0,1:T(8,128)} %param.10) | copy-start | bytes 12292
  52.5 14.3 %copy-start = (s32[1024]{0:T(1024)S(1)}, s32[1024]{0:T(1024)}, u32[]{:S(2)}) copy-start(s32[1024]{0:T(1024)} %valid_ref.3) | copy-start | bytes 12292
  52.5 31.4 %all-to-all-start = ((bf16[16,256,128]{2,1,0:T(8,128)(2,1)}), bf16[16,256,128]{2,1,0:T(8,128)(2,1)S(1)}, u32[]{:S(2)}, u32[]{:S(2)}) async-start(bf16[16,256,128]{2,1,0:T(8,128)(2,1)} %get-tuple-element.20), calls=%async_computation | async-start | bytes 2097152 | tf_op jit(solution)/shard_map/all_to_all | solution.py:391
  57.4 7.7 %collective-permute-start = (bf16[2,512,128]{2,1,0:T(8,128)(2,1)S(1)}, bf16[2,512,128]{2,1,0:T(8,128)(2,1)S(1)}, u32[]{:S(2)}, u32[]{:S(2)}) collective-permute-start(bf16[2,512,128]{2,1,0:T(8,128)(2,1)S(1)} %get-tuple-element.22), channel_id=1, source_target_pairs={{0,16},{16,32},{32,48},{48,64},{64,80},{80,96},{96,112},{1,17},{17... | collective-permute-start | bytes 786440 | tf_op jit(solution)/shard_map/ppermute | solution.py:401
  59.3 7.5 %collective-permute-start.1 = (bf16[2,512,128]{2,1,0:T(8,128)(2,1)S(1)}, bf16[2,512,128]{2,1,0:T(8,128)(2,1)S(1)}, u32[]{:S(2)}, u32[]{:S(2)}) collective-permute-start(bf16[2,512,128]{2,1,0:T(8,128)(2,1)S(1)} %get-tuple-element.23), channel_id=1, source_target_pairs={{16,0},{32,16},{48,32},{64,48},{80,64},{96,80},{112,96},{17,1},{33... | collective-permute-start | bytes 786440 | tf_op jit(solution)/shard_map/ppermute | solution.py:402
  84.0 7.2 %copy-start.2 = (bf16[16,256,128]{2,1,0:T(8,128)(2,1)}, bf16[16,256,128]{2,1,0:T(8,128)(2,1)S(1)}, u32[]{:S(2)}) copy-start(bf16[16,256,128]{2,1,0:T(8,128)(2,1)S(1)} %all-to-all-done.x_hbm) | copy-start | bytes 3145732
  84.0 34.6 %all-to-all-start.3 = ((bf16[16,256,128]{2,1,0:T(8,128)(2,1)}), bf16[16,256,128]{2,1,0:T(8,128)(2,1)S(1)}, u32[]{:S(2)}, u32[]{:S(2)}) async-start(bf16[16,256,128]{2,1,0:T(8,128)(2,1)} %get-tuple-element.31), calls=%async_computation.3 | async-start | bytes 2097152 | tf_op jit(solution)/shard_map/all_to_all | solution.py:391
  108.1 7.7 %collective-permute-start.2 = (bf16[2,512,128]{2,1,0:T(8,128)(2,1)S(1)}, bf16[2,512,128]{2,1,0:T(8,128)(2,1)S(1)}, u32[]{:S(2)}, u32[]{:S(2)}) collective-permute-start(bf16[2,512,128]{2,1,0:T(8,128)(2,1)S(1)} %get-tuple-element.29), channel_id=1, source_target_pairs={{0,16},{16,32},{32,48},{48,64},{64,80},{80,96},{96,112},{1,17},{17... | collective-permute-start | bytes 786440 | tf_op jit(solution)/shard_map/ppermute | solution.py:410
  111.5 6.1 %collective-permute-start.3 = (bf16[2,512,128]{2,1,0:T(8,128)(2,1)S(1)}, bf16[2,512,128]{2,1,0:T(8,128)(2,1)S(1)}, u32[]{:S(2)}, u32[]{:S(2)}) collective-permute-start(bf16[2,512,128]{2,1,0:T(8,128)(2,1)S(1)} %get-tuple-element.30), channel_id=1, source_target_pairs={{16,0},{32,16},{48,32},{64,48},{80,64},{96,80},{112,96},{17,1},{33... | collective-permute-start | bytes 786440 | tf_op jit(solution)/shard_map/ppermute | solution.py:409
  118.6 48.1 %copy-start.1 = (bf16[16,256,128]{2,1,0:T(8,128)(2,1)}, bf16[16,256,128]{2,1,0:T(8,128)(2,1)S(1)}, u32[]{:S(2)}) copy-start(bf16[16,256,128]{2,1,0:T(8,128)(2,1)S(1)} %all-to-all-done.3.two_ref) | copy-start | bytes 3145732

commit v5 on v4

--- a/solution.py
+++ b/solution.py
@@ -12,7 +12,7 @@
 BLOCK = 64
 FACE = 16
 PAIR = 2 * HEAD_DIM
-WIDE = 4
+CHUNKS = 4
 
 score_scale = 0.125
 exp2_scale = score_scale * math.log2(math.e)
@@ -57,60 +57,140 @@
     return low, high
 
 
-def pack_kernel(k_ref, v_ref, q_ref, g_ref, one_ref, two_ref):
-    rows, half = k_ref.shape[0], two_ref.shape[1]
-    for p in range(k_ref.shape[1] // PAIR):
-        cols = slice(p * PAIR, (p + 1) * PAIR)
-        for i, pair in enumerate(swap_halves(k_ref[:, cols], v_ref[:, cols])):
-            one_ref[2 * p + i, :rows] = pair
-        for i, pair in enumerate(swap_halves(q_ref[:, cols], g_ref[:, cols])):
-            one_ref[2 * p + i, rows:] = pair[:half]
-            two_ref[2 * p + i] = pair[half:]
+def pack_kernel(
+    k_hbm, v_hbm, q_hbm, g_hbm, one_hbm, two_hbm, in_refs, out_refs, in_sems, one_sems, two_sems,
+):
+    rows, half = k_hbm.shape[0], two_hbm.shape[1]
+    chunk = rows // CHUNKS
+    pairs = ((k_hbm, v_hbm), (q_hbm, g_hbm))
+
+    def span(c):
+        return pl.ds(c * chunk, chunk)
+
+    def load(n, i, c):
+        return pltpu.make_async_copy(
+            pairs[n][i].at[span(c)], in_refs.at[2 * n + i, span(c)], in_sems.at[2 * n + i, c]
+        )
+
+    def store(n, c):
+        if n == 0 or c * chunk < half:
+            target = one_hbm.at[:, pl.ds(n * rows + c * chunk, chunk)]
+        else:
+            target = two_hbm.at[:, pl.ds(c * chunk - half, chunk)]
+        return pltpu.make_async_copy(
+            out_refs.at[n, :, span(c)], target, (one_sems if n == 0 else two_sems).at[c]
+        )
+
+    order = [(n, c) for n in range(2) for c in range(CHUNKS)]
+    for n, c in order:
+        for i in range(2):
+            load(n, i, c).start()
+    for n, c in order:
+        for i in range(2):
+            load(n, i, c).wait()
+        part = slice(c * chunk, (c + 1) * chunk)
+        for p in range(k_hbm.shape[1] // PAIR):
+            cols = slice(p * PAIR, (p + 1) * PAIR)
+            halves = swap_halves(in_refs[2 * n, part, cols], in_refs[2 * n + 1, part, cols])
+            out_refs[n, 2 * p, part], out_refs[n, 2 * p + 1, part] = halves
+        store(n, c).start()
+    for n, c in order:
+        store(n, c).wait()
 
 
 def pack_heads(k, v, q, g):
     rows, cols = k.shape
     heads, half = cols // HEAD_DIM, rows // 2
-    width = WIDE * PAIR
-    part = pl.BlockSpec((rows, width), lambda i: (0, i))
-    sizes = (rows + half, half)
+    hbm = pl.BlockSpec(memory_space=pltpu.HBM)
     return pl.pallas_call(
         pack_kernel,
-        out_shape=tuple(pltpu.HBM((heads, size, PAIR), k.dtype) for size in sizes),
-        grid=(cols // width,),
-        in_specs=[part] * 4,
-        out_specs=tuple(pl.BlockSpec((2 * WIDE, size, PAIR), lambda i: (i, 0, 0)) for size in sizes),
+        out_shape=tuple(pltpu.HBM((heads, size, PAIR), k.dtype) for size in (rows + half, half)),
+        in_specs=[hbm] * 4,
+        out_specs=(hbm, hbm),
+        scratch_shapes=[
+            pltpu.VMEM((4, rows, cols), k.dtype),
+            pltpu.VMEM((2, heads, rows, PAIR), k.dtype),
+            pltpu.SemaphoreType.DMA((4, CHUNKS)),
+            pltpu.SemaphoreType.DMA((CHUNKS,)),
+            pltpu.SemaphoreType.DMA((CHUNKS,)),
+        ],
         compiler_params=pltpu.CompilerParams(vmem_limit_bytes=60 << 20),
         name="pack_heads",
-    )(k, v, q, g)
-
-
-def unpack_kernel(one_ref, two_ref, k_ref, v_ref, q_ref, o_ref):
-    rows, half = k_ref.shape[0], two_ref.shape[1]
-    for p in range(k_ref.shape[1] // PAIR):
-        cols = slice(p * PAIR, (p + 1) * PAIR)
-        h, i = 2 * p, 2 * p + 1
-        k_ref[:, cols], v_ref[:, cols] = swap_halves(one_ref[h, :rows], one_ref[i, :rows])
-        q_ref[:half, cols], o_ref[:half, cols] = swap_halves(two_ref[h], two_ref[i])
-        q_ref[half:, cols], o_ref[half:, cols] = swap_halves(one_ref[h, rows:], one_ref[i, rows:])
+    )(*(off_chip(x) for x in (k, v, q, g)))
+
+
+def unpack_kernel(
+    one_hbm, two_hbm, k_hbm, v_hbm, q_hbm, o_hbm, in_refs, out_refs, one_sems, two_sems, out_sems,
+):
+    rows, half = k_hbm.shape[0], two_hbm.shape[1]
+    chunk = rows // CHUNKS
+    pairs = ((k_hbm, v_hbm), (q_hbm, o_hbm))
+
+    def span(c):
+        return pl.ds(c * chunk, chunk)
+
+    def load(n, c):
+        if n == 0:
+            source = one_hbm.at[:, span(c)]
+        elif c * chunk < half:
+            source = two_hbm.at[:, span(c)]
+        else:
+            source = one_hbm.at[:, pl.ds(rows + c * chunk - half, chunk)]
+        return pltpu.make_async_copy(
+            source, in_refs.at[n, :, span(c)], (one_sems if n == 0 else two_sems).at[c]
+        )
+
+    def store(n, i, c):
+        return pltpu.make_async_copy(
+            out_refs.at[2 * n + i, span(c)], pairs[n][i].at[span(c)], out_sems.at[2 * n + i, c]
+        )
+
+    order = [(n, c) for n in range(2) for c in range(CHUNKS)]
+    for n, c in order:
+        load(n, c).start()
+    for n, c in order:
+        load(n, c).wait()
+        part = slice(c * chunk, (c + 1) * chunk)
+        for p in range(k_hbm.shape[1] // PAIR):
+            cols = slice(p * PAIR, (p + 1) * PAIR)
+            halves = swap_halves(in_refs[n, 2 * p, part], in_refs[n, 2 * p + 1, part])
+            out_refs[2 * n, part, cols], out_refs[2 * n + 1, part, cols] = halves
+        for i in range(2):
+            store(n, i, c).start()
+    for n, c in order:
+        for i in range(2):
+            store(n, i, c).wait()
 
 
 def unpack_heads(one, two):
     heads, half, _ = two.shape
-    rows = 2 * half
-    width = WIDE * PAIR
-    part = pl.BlockSpec((rows, width), lambda i: (0, i))
+    rows, cols = 2 * half, heads * HEAD_DIM
+    hbm = pl.BlockSpec(memory_space=pltpu.HBM)
     return pl.pallas_call(
         unpack_kernel,
-        out_shape=(jax.ShapeDtypeStruct((rows, heads * HEAD_DIM), one.dtype),) * 4,
-        grid=(heads * HEAD_DIM // width,),
-        in_specs=[
-            pl.BlockSpec((2 * WIDE, x.shape[1], PAIR), lambda i: (i, 0, 0)) for x in (one, two)
+        out_shape=(pltpu.HBM((rows, cols), one.dtype),) * 4,
+        in_specs=[hbm, hbm],
+        out_specs=(hbm,) * 4,
+        scratch_shapes=[
+            pltpu.VMEM((2, heads, rows, PAIR), one.dtype),
+            pltpu.VMEM((4, rows, cols), one.dtype),
+            pltpu.SemaphoreType.DMA((CHUNKS,)),
+            pltpu.SemaphoreType.DMA((CHUNKS,)),
+            pltpu.SemaphoreType.DMA((4, CHUNKS)),
         ],
-        out_specs=(part,) * 4,
         compiler_params=pltpu.CompilerParams(vmem_limit_bytes=60 << 20),
         name="unpack_heads",
     )(off_chip(one), off_chip(two))
+
+
+def in_turn(*tasks):
+    def steps(stage, blocks):
+        for u in blocks:
+            yield from stage(u)
+
+    running = [steps(*task) for task in tasks]
+    while running:
+        running = [task for task in running if next(task, True) is None]
 
 
 def query_blocks(
@@ -144,12 +224,18 @@
             zero = jnp.zeros_like(qg)
             return jnp.concatenate([jnp.where(low, zero, qg), jnp.where(low, qg, zero)], axis=0)
 
-        for u, (s, part, slots, counts) in enumerate(meta):
-            both_ref[u] = lax.dot_general(
-                spread(s, part), gathered(slots), (((1,), (1,)), ((), ())),
-                preferred_element_type=jnp.float32,
-            )
-        for u, (s, part, slots, counts) in enumerate(meta):
+        def probe(u):
+            s, part, slots, counts = meta[u]
+            kv, gq = gathered(slots), spread(s, part)
+            for n in range(0, keys_num * BLOCK, 2 * PAIR):
+                both_ref[u, :, n : n + 2 * PAIR] = lax.dot_general(
+                    gq, kv[n : n + 2 * PAIR], (((1,), (1,)), ((), ())),
+                    preferred_element_type=jnp.float32,
+                )
+                yield
+
+        def weigh(u):
+            s, part, slots, counts = meta[u]
             bias = jnp.concatenate(
                 [
                     jnp.where(
@@ -173,23 +259,39 @@
                 dscore = (prob_wide * (grad_prob - delta)).astype(jnp.bfloat16)
                 pd_ref[u, r : r + lines, :] = prob
                 pd_ref[u, BLOCK + r : BLOCK + r + lines, :] = dscore
-        for u, (s, part, slots, counts) in enumerate(meta):
+                yield
+
+        def rows_out(u):
+            s, part, slots, counts = meta[u]
             od = jnp.dot(pd_ref[u], gathered(slots), preferred_element_type=jnp.float32)
             od_ref[shard + s, part, :] = jnp.where(
                 low, od[BLOCK:] * score_scale, od[:BLOCK]
             ).astype(od_ref.dtype)
-        for s in range(group // each):
-            send_od(shard + s).start()
-        if ready is not None:
-            pl.when(t == 0)(ready)
-        for u, (s, part, slots, counts) in enumerate(meta):
+            yield
+
+        def keys_out(u):
+            s, part, slots, counts = meta[u]
             dkv = lax.dot_general(
                 pd_ref[u], spread(s, part), (((0,), (0,)), ((), ())),
                 preferred_element_type=jnp.float32,
             )
+            yield
             for j, slot in enumerate(slots):
                 span = pl.ds(pl.multiple_of(slot * BLOCK, BLOCK), BLOCK)
                 acc_ref[span, :] += dkv[j * BLOCK : (j + 1) * BLOCK]
+                if j % 2:
+                    yield
+
+        near, far = range(group // 2), range(group // 2, group)
+        in_turn((probe, near))
+        in_turn((probe, far), (weigh, near))
+        if ready is not None:
+            pl.when(t == 0)(ready)
+        in_turn((keys_out, near), (weigh, far))
+        in_turn((rows_out, range(group)))
+        for s in range(group // each):
+            send_od(shard + s).start()
+        in_turn((keys_out, far))
         return 0
 
     lax.fori_loop(0, shards * each // group, one_group, 0)

time: 173 us -> 171 us (0.988)
  no operation moved by 1% of the time
where the time goes in v5:
time: 171 us; the launch traced here: 169 us
  blocking collectives  95.9 us (56%)
  Pallas kernels  42.6 us (25%)
  starting transfers between devices  22.1 us (13%)
  waiting for transfers between devices  7.53 us (4%)
    all_to_all x2, blocking collectives, exchange(): return lax.all_to_all(x, 'seq', split_axis=0, concat_axis=0, tiled=True)  95.9 us
    pallas_call x1, Pallas kernels, second_half(): pl.pallas_call(partial(second_kernel, keys_num=keys_num, group=group, lin...  16.8 us
    pallas_call x1, Pallas kernels, first_half(): pl.pallas_call(partial(first_kernel, keys_num=keys_num, group=group, line...  16.3 us
    all_to_all x2, starting transfers between devices, exchange(): return lax.all_to_all(x, 'seq', split_axis=0, concat_axis=0, tiled=True)  10.9 us
    pallas_call x1, Pallas kernels, unpack_heads(): pl.pallas_call(unpack_kernel, out_shape=(pltpu.HBM((rows, cols), one.dtyp...  3.83 us
    pallas_call x1, Pallas kernels, pack_heads(): pl.pallas_call(pack_kernel, out_shape=tuple((pltpu.HBM((heads, size, PAIR...  3.7 us
    ppermute x1, starting transfers between devices, body(): after = lax.ppermute(first, 'slab', down)  3.64 us
  transfers between devices with their start and end apart: 6, of which 4 were waited for; matrix products, arithmetic and copies ran while one was open for 0% of the time, Pallas kernels for 21%

profile of v5, /device:TPU:2, one launch (start us, length us, event | category | flops | bytes accessed | tf_op | source)
XLA Modules:
  0.0 169.2 jit_solution(2186059007197626653)
XLA Ops:
  0.6 3.7 %pack_heads.1 = (bf16[16,768,128]{2,1,0:T(8,128)(2,1)}, bf16[16,256,128]{2,1,0:T(8,128)(2,1)}) custom-call(bf16[512,1024]{1,0:T(8,128)(2,1)} %k_hbm.1, bf16[512,1024]{1,0:T(8,128)(2,1)} %v_hbm.1, bf16[512,1024]{1,0:T(8,128)(2,1)} %q_hbm.1, bf16[512,1024]{1,0:T(8,128)(2,1)} %g_hbm.1), custom_call_target="tpu_custom_call" | custom-call | tf_op jit(solution)/shard_map/pack_heads/pallas_call | solution.py:105
  4.3 47.8 %all_to_all.20.x_hbm = bf16[16,768,128]{2,1,0:T(8,128)(2,1)} all-to-all(bf16[16,768,128]{2,1,0:T(8,128)(2,1)} %get-tuple-element.21), channel_id=1, replica_groups=mesh['slab'=8,'seq'=16] {'seq'}, dimensions={0} | all-to-all | bytes 6291456 | tf_op jit(solution)/shard_map/all_to_all | solution.py:493
  52.1 0.0 copy-start.3
  52.1 0.0 copy-start
  52.1 3.8 %all-to-all-start = ((bf16[16,256,128]{2,1,0:T(8,128)(2,1)}), bf16[16,256,128]{2,1,0:T(8,128)(2,1)S(1)}, u32[]{:S(2)}, u32[]{:S(2)}) async-start(bf16[16,256,128]{2,1,0:T(8,128)(2,1)} %get-tuple-element.20), calls=%async_computation | async-start | bytes 2097152 | tf_op jit(solution)/shard_map/all_to_all | solution.py:493
  55.9 1.0 take_faces.1
  57.0 1.9 %collective-permute-start = (bf16[2,512,128]{2,1,0:T(8,128)(2,1)S(1)}, bf16[2,512,128]{2,1,0:T(8,128)(2,1)S(1)}, u32[]{:S(2)}, u32[]{:S(2)}) collective-permute-start(bf16[2,512,128]{2,1,0:T(8,128)(2,1)S(1)} %get-tuple-element.22), channel_id=1, source_target_pairs={{0,16},{16,32},{32,48},{48,64},{64,80},{80,96},{96,112},{1,17},{17... | collective-permute-start | bytes 786440 | tf_op jit(solution)/shard_map/ppermute | solution.py:503
  58.9 3.6 %collective-permute-start.1 = (bf16[2,512,128]{2,1,0:T(8,128)(2,1)S(1)}, bf16[2,512,128]{2,1,0:T(8,128)(2,1)S(1)}, u32[]{:S(2)}, u32[]{:S(2)}) collective-permute-start(bf16[2,512,128]{2,1,0:T(8,128)(2,1)S(1)} %get-tuple-element.23), channel_id=1, source_target_pairs={{16,0},{32,16},{48,32},{64,48},{80,64},{96,80},{112,96},{17,1},{33... | collective-permute-start | bytes 786440 | tf_op jit(solution)/shard_map/ppermute | solution.py:504
  62.6 0.0 copy-done.3
  62.6 0.1 copy.11
  62.7 0.1 reshape.14.pattern_ref
  62.8 1.9 %collective-permute-done.before_ref = bf16[2,512,128]{2,1,0:T(8,128)(2,1)S(1)} collective-permute-done((bf16[2,512,128]{2,1,0:T(8,128)(2,1)S(1)}, bf16[2,512,128]{2,1,0:T(8,128)(2,1)S(1)}, u32[]{:S(2)}, u32[]{:S(2)}) %collective-permute-start) | collective-permute-done | bytes 262176 | tf_op jit(solution)/shard_map/ppermute | solution.py:503
  64.7 1.8 %collective-permute-done.1.after_ref = bf16[2,512,128]{2,1,0:T(8,128)(2,1)S(1)} collective-permute-done((bf16[2,512,128]{2,1,0:T(8,128)(2,1)S(1)}, bf16[2,512,128]{2,1,0:T(8,128)(2,1)S(1)}, u32[]{:S(2)}, u32[]{:S(2)}) %collective-permute-start.1) | collective-permute-done | bytes 262176 | tf_op jit(solution)/shard_map/ppermute | solution.py:504
  66.4 0.0 copy-done
  66.4 16.3 %first_half.1 = (bf16[16,256,128]{2,1,0:T(8,128)(2,1)}, bf16[10240,128]{1,0:T(8,128)(2,1)}, f32[10240,128]{1,0:T(8,128)}) custom-call(s32[1024]{0:T(1024)S(1)} %reshape.14.pattern_ref, s32[1024]{0:T(1024)S(1)} %copy-done, s32[1]{0:T(128)} %bitcast.start_ref, bf16[16,768,128]{2,1,0:T(8,128)(2,1)} %all_to_all.20.x_hbm, ...), custom_call_target="tpu_custom_call" | custom-call | flops 3221225472 | bytes 16777216 | tf_op jit(solution)/shard_map/first_half/pallas_call | solution.py:400
  82.7 0.0 all-to-all-done.x_hbm
  82.7 0.0 copy-start.2
  82.8 7.2 %all-to-all-start.3 = ((bf16[16,256,128]{2,1,0:T(8,128)(2,1)}), bf16[16,256,128]{2,1,0:T(8,128)(2,1)S(1)}, u32[]{:S(2)}, u32[]{:S(2)}) async-start(bf16[16,256,128]{2,1,0:T(8,128)(2,1)} %get-tuple-element.31), calls=%async_computation.3 | async-start | bytes 2097152 | tf_op jit(solution)/shard_map/all_to_all | solution.py:493
  89.9 0.0 copy-done.2
  89.9 16.8 %second_half.1 = (bf16[16,768,128]{2,1,0:T(8,128)(2,1)}, f32[2,512,128]{2,1,0:T(8,128)S(1)}, f32[2,512,128]{2,1,0:T(8,128)S(1)}, bf16[2,512,128]{2,1,0:T(8,128)(2,1)S(1)}, bf16[2,512,128]{2,1,0:T(8,128)(2,1)S(1)}) custom-call(s32[1024]{0:T(1024)S(1)} %reshape.14.pattern_ref, s32[1024]{0:T(1024)S(1)} %copy-done, s32[1]{0:T(128)} %bitcast.start_ref, ...), custom_call_target="tpu_custom_call" | custom-call | flops 3221225472 | bytes 16777216 | tf_op jit(solution)/shard_map/second_half/pallas_call | solution.py:434
  106.7 3.4 %collective-permute-start.2 = (bf16[2,512,128]{2,1,0:T(8,128)(2,1)S(1)}, bf16[2,512,128]{2,1,0:T(8,128)(2,1)S(1)}, u32[]{:S(2)}, u32[]{:S(2)}) collective-permute-start(bf16[2,512,128]{2,1,0:T(8,128)(2,1)S(1)} %get-tuple-element.29), channel_id=1, source_target_pairs={{0,16},{16,32},{32,48},{48,64},{64,80},{80,96},{96,112},{1,17},{17... | collective-permute-start | bytes 786440 | tf_op jit(solution)/shard_map/ppermute | solution.py:512
  110.1 2.2 %collective-permute-start.3 = (bf16[2,512,128]{2,1,0:T(8,128)(2,1)S(1)}, bf16[2,512,128]{2,1,0:T(8,128)(2,1)S(1)}, u32[]{:S(2)}, u32[]{:S(2)}) collective-permute-start(bf16[2,512,128]{2,1,0:T(8,128)(2,1)S(1)} %get-tuple-element.30), channel_id=1, source_target_pairs={{16,0},{32,16},{48,32},{64,48},{80,64},{96,80},{112,96},{17,1},{33... | collective-permute-start | bytes 786440 | tf_op jit(solution)/shard_map/ppermute | solution.py:511
  112.3 2.1 %collective-permute-done.2.low_ref = bf16[2,512,128]{2,1,0:T(8,128)(2,1)S(1)} collective-permute-done((bf16[2,512,128]{2,1,0:T(8,128)(2,1)S(1)}, bf16[2,512,128]{2,1,0:T(8,128)(2,1)S(1)}, u32[]{:S(2)}, u32[]{:S(2)}) %collective-permute-start.2) | collective-permute-done | bytes 262176 | tf_op jit(solution)/shard_map/ppermute | solution.py:512
  114.4 1.8 %collective-permute-done.3.high_ref = bf16[2,512,128]{2,1,0:T(8,128)(2,1)S(1)} collective-permute-done((bf16[2,512,128]{2,1,0:T(8,128)(2,1)S(1)}, bf16[2,512,128]{2,1,0:T(8,128)(2,1)S(1)}, u32[]{:S(2)}, u32[]{:S(2)}) %collective-permute-start.3) | collective-permute-done | bytes 262176 | tf_op jit(solution)/shard_map/ppermute | solution.py:511
  116.2 1.0 join_faces.1
  117.2 0.0 all-to-all-done.3.two_hbm
  117.2 0.0 copy-start.1
  117.2 48.1 %all_to_all.21.one_hbm = bf16[16,768,128]{2,1,0:T(8,128)(2,1)} all-to-all(bf16[16,768,128]{2,1,0:T(8,128)(2,1)} %join_faces.1), channel_id=1, replica_groups=mesh['slab'=8,'seq'=16] {'seq'}, dimensions={0} | all-to-all | bytes 6291456 | tf_op jit(solution)/shard_map/all_to_all | solution.py:493
  165.3 0.0 copy-done.1
  165.3 3.8 %unpack_heads.1 = (bf16[512,1024]{1,0:T(8,128)(2,1)}, bf16[512,1024]{1,0:T(8,128)(2,1)}, bf16[512,1024]{1,0:T(8,128)(2,1)}, bf16[512,1024]{1,0:T(8,128)(2,1)}) custom-call(bf16[16,768,128]{2,1,0:T(8,128)(2,1)} %all_to_all.21.one_hbm, bf16[16,256,128]{2,1,0:T(8,128)(2,1)} %copy-done.1), custom_call_target="tpu_custom_call" | custom-call | tf_op jit(solution)/shard_map/unpack_heads/pallas_call | solution.py:169
Async XLA Ops:
  52.1 10.4 %copy-start.3 = (s32[128,8]{0,1:T(8,128)S(1)}, s32[128,8]{0,1:T(8,128)}, u32[]{:S(2)}) copy-start(s32[128,8]{0,1:T(8,128)} %param.10) | copy-start | bytes 12292
  52.1 14.3 %copy-start = (s32[1024]{0:T(1024)S(1)}, s32[1024]{0:T(1024)}, u32[]{:S(2)}) copy-start(s32[1024]{0:T(1024)} %valid_ref.3) | copy-start | bytes 12292
  52.1 30.6 %all-to-all-start = ((bf16[16,256,128]{2,1,0:T(8,128)(2,1)}), bf16[16,256,128]{2,1,0:T(8,128)(2,1)S(1)}, u32[]{:S(2)}, u32[]{:S(2)}) async-start(bf16[16,256,128]{2,1,0:T(8,128)(2,1)} %get-tuple-element.20), calls=%async_computation | async-start | bytes 2097152 | tf_op jit(solution)/shard_map/all_to_all | solution.py:493
  57.0 7.7 %collective-permute-start = (bf16[2,512,128]{2,1,0:T(8,128)(2,1)S(1)}, bf16[2,512,128]{2,1,0:T(8,128)(2,1)S(1)}, u32[]{:S(2)}, u32[]{:S(2)}) collective-permute-start(bf16[2,512,128]{2,1,0:T(8,128)(2,1)S(1)} %get-tuple-element.22), channel_id=1, source_target_pairs={{0,16},{16,32},{32,48},{48,64},{64,80},{80,96},{96,112},{1,17},{17... | collective-permute-start | bytes 786440 | tf_op jit(solution)/shard_map/ppermute | solution.py:503
  58.9 7.5 %collective-permute-start.1 = (bf16[2,512,128]{2,1,0:T(8,128)(2,1)S(1)}, bf16[2,512,128]{2,1,0:T(8,128)(2,1)S(1)}, u32[]{:S(2)}, u32[]{:S(2)}) collective-permute-start(bf16[2,512,128]{2,1,0:T(8,128)(2,1)S(1)} %get-tuple-element.23), channel_id=1, source_target_pairs={{16,0},{32,16},{48,32},{64,48},{80,64},{96,80},{112,96},{17,1},{33... | collective-permute-start | bytes 786440 | tf_op jit(solution)/shard_map/ppermute | solution.py:504
  82.7 7.2 %copy-start.2 = (bf16[16,256,128]{2,1,0:T(8,128)(2,1)}, bf16[16,256,128]{2,1,0:T(8,128)(2,1)S(1)}, u32[]{:S(2)}) copy-start(bf16[16,256,128]{2,1,0:T(8,128)(2,1)S(1)} %all-to-all-done.x_hbm) | copy-start | bytes 3145732
  82.8 34.4 %all-to-all-start.3 = ((bf16[16,256,128]{2,1,0:T(8,128)(2,1)}), bf16[16,256,128]{2,1,0:T(8,128)(2,1)S(1)}, u32[]{:S(2)}, u32[]{:S(2)}) async-start(bf16[16,256,128]{2,1,0:T(8,128)(2,1)} %get-tuple-element.31), calls=%async_computation.3 | async-start | bytes 2097152 | tf_op jit(solution)/shard_map/all_to_all | solution.py:493
  106.7 7.7 %collective-permute-start.2 = (bf16[2,512,128]{2,1,0:T(8,128)(2,1)S(1)}, bf16[2,512,128]{2,1,0:T(8,128)(2,1)S(1)}, u32[]{:S(2)}, u32[]{:S(2)}) collective-permute-start(bf16[2,512,128]{2,1,0:T(8,128)(2,1)S(1)} %get-tuple-element.29), channel_id=1, source_target_pairs={{0,16},{16,32},{32,48},{48,64},{64,80},{80,96},{96,112},{1,17},{17... | collective-permute-start | bytes 786440 | tf_op jit(solution)/shard_map/ppermute | solution.py:512
  110.1 6.0 %collective-permute-start.3 = (bf16[2,512,128]{2,1,0:T(8,128)(2,1)S(1)}, bf16[2,512,128]{2,1,0:T(8,128)(2,1)S(1)}, u32[]{:S(2)}, u32[]{:S(2)}) collective-permute-start(bf16[2,512,128]{2,1,0:T(8,128)(2,1)S(1)} %get-tuple-element.30), channel_id=1, source_target_pairs={{16,0},{32,16},{48,32},{64,48},{80,64},{96,80},{112,96},{17,1},{33... | collective-permute-start | bytes 786440 | tf_op jit(solution)/shard_map/ppermute | solution.py:511
  117.2 48.1 %copy-start.1 = (bf16[16,256,128]{2,1,0:T(8,128)(2,1)}, bf16[16,256,128]{2,1,0:T(8,128)(2,1)S(1)}, u32[]{:S(2)}) copy-start(bf16[16,256,128]{2,1,0:T(8,128)(2,1)S(1)} %all-to-all-done.3.two_hbm) | copy-start | bytes 3145732

commit v6 on v5

--- a/solution.py
+++ b/solution.py
@@ -502,6 +502,7 @@
     first, last = take_faces(one, edge, rows)
     before = lax.ppermute(last, "slab", up)
     after = lax.ppermute(first, "slab", down)
+    before, two = lax.optimization_barrier((before, two))
     two = exchange(two)
     start = (lax.axis_index("slab") * pattern.shape[0] - FACE).astype(jnp.int32).reshape(1)
     scalars = (pattern.reshape(-1), valid_rows, start)

time: 171 us -> 175 us (1.023)
  waiting for transfers between devices: 7.53 us -> 13.3 us
  starting transfers between devices: 22.1 us -> 20.3 us
    ppermute x1, waiting for transfers between devices: 1.9 us -> 5.76 us  [body(): before = lax.ppermute(last, 'slab', up)]
    ppermute x1, waiting for transfers between devices: 1.76 us -> 3.65 us  [body(): after = lax.ppermute(first, 'slab', down)]
  transfers between devices with their start and end apart: 6 -> 6, of which waited for: 4 -> 4; matrix products, arithmetic and copies ran while one was open for 0% -> 0% of each run, Pallas kernels for 21% -> 20%
where the time goes in v6:
time: 175 us; the launch traced here: 173 us
  blocking collectives  95.9 us (55%)
  Pallas kernels  42.6 us (24%)
  starting transfers between devices  20.3 us (12%)
  waiting for transfers between devices  13.3 us (8%)
    all_to_all x2, blocking collectives, exchange(): return lax.all_to_all(x, 'seq', split_axis=0, concat_axis=0, tiled=True)  95.9 us
    pallas_call x1, Pallas kernels, second_half(): pl.pallas_call(partial(second_kernel, keys_num=keys_num, group=group, lin...  16.8 us
    pallas_call x1, Pallas kernels, first_half(): pl.pallas_call(partial(first_kernel, keys_num=keys_num, group=group, line...  16.3 us
    all_to_all x2, starting transfers between devices, exchange(): return lax.all_to_all(x, 'seq', split_axis=0, concat_axis=0, tiled=True)  10.8 us
    ppermute x1, waiting for transfers between devices, body(): before = lax.ppermute(last, 'slab', up)  5.76 us
    pallas_call x1, Pallas kernels, unpack_heads(): pl.pallas_call(unpack_kernel, out_shape=(pltpu.HBM((rows, cols), one.dtyp...  3.83 us
    pallas_call x1, Pallas kernels, pack_heads(): pl.pallas_call(pack_kernel, out_shape=tuple((pltpu.HBM((heads, size, PAIR...  3.7 us
    ppermute x1, starting transfers between devices, body(): low = lax.ppermute(to_after, 'slab', up)  3.69 us
  transfers between devices with their start and end apart: 6, of which 4 were waited for; matrix products, arithmetic and copies ran while one was open for 0% of the time, Pallas kernels for 20%

profile of v6, /device:TPU:2, one launch (start us, length us, event | category | flops | bytes accessed | tf_op | source)
XLA Modules:
  0.0 173.1 jit_solution(4426357436665617476)
XLA Ops:
  0.6 3.7 %pack_heads.1 = (bf16[16,768,128]{2,1,0:T(8,128)(2,1)}, bf16[16,256,128]{2,1,0:T(8,128)(2,1)}) custom-call(bf16[512,1024]{1,0:T(8,128)(2,1)} %k_hbm.1, bf16[512,1024]{1,0:T(8,128)(2,1)} %v_hbm.1, bf16[512,1024]{1,0:T(8,128)(2,1)} %q_hbm.1, bf16[512,1024]{1,0:T(8,128)(2,1)} %g_hbm.1), custom_call_target="tpu_custom_call" | custom-call | tf_op jit(solution)/shard_map/pack_heads/pallas_call | solution.py:105
  4.3 47.8 %all_to_all.20.x_hbm = bf16[16,768,128]{2,1,0:T(8,128)(2,1)} all-to-all(bf16[16,768,128]{2,1,0:T(8,128)(2,1)} %get-tuple-element.22), channel_id=1, replica_groups=mesh['slab'=8,'seq'=16] {'seq'}, dimensions={0} | all-to-all | bytes 6291456 | tf_op jit(solution)/shard_map/all_to_all | solution.py:493
  52.1 0.0 copy-start.3
  52.1 0.0 copy-start
  52.1 1.1 take_faces.1
  53.2 1.9 %collective-permute-start = (bf16[2,512,128]{2,1,0:T(8,128)(2,1)S(1)}, bf16[2,512,128]{2,1,0:T(8,128)(2,1)S(1)}, u32[]{:S(2)}, u32[]{:S(2)}) collective-permute-start(bf16[2,512,128]{2,1,0:T(8,128)(2,1)S(1)} %get-tuple-element.23), channel_id=1, source_target_pairs={{0,16},{16,32},{32,48},{48,64},{64,80},{80,96},{96,112},{1,17},{17... | collective-permute-start | bytes 786440 | tf_op jit(solution)/shard_map/ppermute | solution.py:503
  55.1 5.8 %collective-permute-done.before_ref = bf16[2,512,128]{2,1,0:T(8,128)(2,1)S(1)} collective-permute-done((bf16[2,512,128]{2,1,0:T(8,128)(2,1)S(1)}, bf16[2,512,128]{2,1,0:T(8,128)(2,1)S(1)}, u32[]{:S(2)}, u32[]{:S(2)}) %collective-permute-start) | collective-permute-done | bytes 262176 | tf_op jit(solution)/shard_map/ppermute | solution.py:503
  60.9 3.7 %all-to-all-start.1 = ((bf16[16,256,128]{2,1,0:T(8,128)(2,1)}), bf16[16,256,128]{2,1,0:T(8,128)(2,1)S(1)}, u32[]{:S(2)}, u32[]{:S(2)}) async-start(bf16[16,256,128]{2,1,0:T(8,128)(2,1)} %get-tuple-element.25), calls=%async_computation.1 | async-start | bytes 2097152 | tf_op jit(solution)/shard_map/all_to_all | solution.py:493
  64.6 1.9 %collective-permute-start.1 = (bf16[2,512,128]{2,1,0:T(8,128)(2,1)S(1)}, bf16[2,512,128]{2,1,0:T(8,128)(2,1)S(1)}, u32[]{:S(2)}, u32[]{:S(2)}) collective-permute-start(bf16[2,512,128]{2,1,0:T(8,128)(2,1)S(1)} %get-tuple-element.27), channel_id=1, source_target_pairs={{16,0},{32,16},{48,32},{64,48},{80,64},{96,80},{112,96},{17,1},{33... | collective-permute-start | bytes 786440 | tf_op jit(solution)/shard_map/ppermute | solution.py:504
  66.5 0.0 copy-done.3
  66.5 0.1 copy.11
  66.6 0.1 reshape.14.pattern_ref
  66.7 3.7 %collective-permute-done.1.after_ref = bf16[2,512,128]{2,1,0:T(8,128)(2,1)S(1)} collective-permute-done((bf16[2,512,128]{2,1,0:T(8,128)(2,1)S(1)}, bf16[2,512,128]{2,1,0:T(8,128)(2,1)S(1)}, u32[]{:S(2)}, u32[]{:S(2)}) %collective-permute-start.1) | collective-permute-done | bytes 262176 | tf_op jit(solution)/shard_map/ppermute | solution.py:504
  70.4 0.0 copy-done
  70.4 16.3 %first_half.1 = (bf16[16,256,128]{2,1,0:T(8,128)(2,1)}, bf16[10240,128]{1,0:T(8,128)(2,1)}, f32[10240,128]{1,0:T(8,128)}) custom-call(s32[1024]{0:T(1024)S(1)} %reshape.14.pattern_ref, s32[1024]{0:T(1024)S(1)} %copy-done, s32[1]{0:T(128)} %bitcast.start_ref, bf16[16,768,128]{2,1,0:T(8,128)(2,1)} %all_to_all.20.x_hbm, ...), custom_call_target="tpu_custom_call" | custom-call | flops 3221225472 | bytes 16777216 | tf_op jit(solution)/shard_map/first_half/pallas_call | solution.py:400
  86.7 0.0 all-to-all-done.1.x_hbm
  86.7 0.0 copy-start.2
  86.7 7.2 %all-to-all-start.3 = ((bf16[16,256,128]{2,1,0:T(8,128)(2,1)}), bf16[16,256,128]{2,1,0:T(8,128)(2,1)S(1)}, u32[]{:S(2)}, u32[]{:S(2)}) async-start(bf16[16,256,128]{2,1,0:T(8,128)(2,1)} %get-tuple-element.35), calls=%async_computation.3 | async-start | bytes 2097152 | tf_op jit(solution)/shard_map/all_to_all | solution.py:493
  93.8 0.0 copy-done.2
  93.9 16.8 %second_half.1 = (bf16[16,768,128]{2,1,0:T(8,128)(2,1)}, f32[2,512,128]{2,1,0:T(8,128)S(1)}, f32[2,512,128]{2,1,0:T(8,128)S(1)}, bf16[2,512,128]{2,1,0:T(8,128)(2,1)S(1)}, bf16[2,512,128]{2,1,0:T(8,128)(2,1)S(1)}) custom-call(s32[1024]{0:T(1024)S(1)} %reshape.14.pattern_ref, s32[1024]{0:T(1024)S(1)} %copy-done, s32[1]{0:T(128)} %bitcast.start_ref, ...), custom_call_target="tpu_custom_call" | custom-call | flops 3221225472 | bytes 16777216 | tf_op jit(solution)/shard_map/second_half/pallas_call | solution.py:434
  110.6 3.7 %collective-permute-start.2 = (bf16[2,512,128]{2,1,0:T(8,128)(2,1)S(1)}, bf16[2,512,128]{2,1,0:T(8,128)(2,1)S(1)}, u32[]{:S(2)}, u32[]{:S(2)}) collective-permute-start(bf16[2,512,128]{2,1,0:T(8,128)(2,1)S(1)} %get-tuple-element.33), channel_id=1, source_target_pairs={{0,16},{16,32},{32,48},{48,64},{64,80},{80,96},{96,112},{1,17},{17... | collective-permute-start | bytes 786440 | tf_op jit(solution)/shard_map/ppermute | solution.py:513
  114.3 1.9 %collective-permute-start.3 = (bf16[2,512,128]{2,1,0:T(8,128)(2,1)S(1)}, bf16[2,512,128]{2,1,0:T(8,128)(2,1)S(1)}, u32[]{:S(2)}, u32[]{:S(2)}) collective-permute-start(bf16[2,512,128]{2,1,0:T(8,128)(2,1)S(1)} %get-tuple-element.34), channel_id=1, source_target_pairs={{16,0},{32,16},{48,32},{64,48},{80,64},{96,80},{112,96},{17,1},{33... | collective-permute-start | bytes 786440 | tf_op jit(solution)/shard_map/ppermute | solution.py:512
  116.3 2.1 %collective-permute-done.2.low_ref = bf16[2,512,128]{2,1,0:T(8,128)(2,1)S(1)} collective-permute-done((bf16[2,512,128]{2,1,0:T(8,128)(2,1)S(1)}, bf16[2,512,128]{2,1,0:T(8,128)(2,1)S(1)}, u32[]{:S(2)}, u32[]{:S(2)}) %collective-permute-start.2) | collective-permute-done | bytes 262176 | tf_op jit(solution)/shard_map/ppermute | solution.py:513
  118.3 1.8 %collective-permute-done.3.high_ref = bf16[2,512,128]{2,1,0:T(8,128)(2,1)S(1)} collective-permute-done((bf16[2,512,128]{2,1,0:T(8,128)(2,1)S(1)}, bf16[2,512,128]{2,1,0:T(8,128)(2,1)S(1)}, u32[]{:S(2)}, u32[]{:S(2)}) %collective-permute-start.3) | collective-permute-done | bytes 262176 | tf_op jit(solution)/shard_map/ppermute | solution.py:512
  120.1 1.0 join_faces.1
  121.1 0.0 all-to-all-done.3.two_hbm
  121.1 0.0 copy-start.1
  121.1 48.1 %all_to_all.21.one_hbm = bf16[16,768,128]{2,1,0:T(8,128)(2,1)} all-to-all(bf16[16,768,128]{2,1,0:T(8,128)(2,1)} %join_faces.1), channel_id=1, replica_groups=mesh['slab'=8,'seq'=16] {'seq'}, dimensions={0} | all-to-all | bytes 6291456 | tf_op jit(solution)/shard_map/all_to_all | solution.py:493
  169.2 0.0 copy-done.1
  169.2 3.8 %unpack_heads.1 = (bf16[512,1024]{1,0:T(8,128)(2,1)}, bf16[512,1024]{1,0:T(8,128)(2,1)}, bf16[512,1024]{1,0:T(8,128)(2,1)}, bf16[512,1024]{1,0:T(8,128)(2,1)}) custom-call(bf16[16,768,128]{2,1,0:T(8,128)(2,1)} %all_to_all.21.one_hbm, bf16[16,256,128]{2,1,0:T(8,128)(2,1)} %copy-done.1), custom_call_target="tpu_custom_call" | custom-call | tf_op jit(solution)/shard_map/unpack_heads/pallas_call | solution.py:169
Async XLA Ops:
  52.1 14.4 %copy-start.3 = (s32[128,8]{0,1:T(8,128)S(1)}, s32[128,8]{0,1:T(8,128)}, u32[]{:S(2)}) copy-start(s32[128,8]{0,1:T(8,128)} %param.10) | copy-start | bytes 12292
  52.1 18.2 %copy-start = (s32[1024]{0:T(1024)S(1)}, s32[1024]{0:T(1024)}, u32[]{:S(2)}) copy-start(s32[1024]{0:T(1024)} %valid_ref.3) | copy-start | bytes 12292
  53.2 7.7 %collective-permute-start = (bf16[2,512,128]{2,1,0:T(8,128)(2,1)S(1)}, bf16[2,512,128]{2,1,0:T(8,128)(2,1)S(1)}, u32[]{:S(2)}, u32[]{:S(2)}) collective-permute-start(bf16[2,512,128]{2,1,0:T(8,128)(2,1)S(1)} %get-tuple-element.23), channel_id=1, source_target_pairs={{0,16},{16,32},{32,48},{48,64},{64,80},{80,96},{96,112},{1,17},{17... | collective-permute-start | bytes 786440 | tf_op jit(solution)/shard_map/ppermute | solution.py:503
  60.9 25.8 %all-to-all-start.1 = ((bf16[16,256,128]{2,1,0:T(8,128)(2,1)}), bf16[16,256,128]{2,1,0:T(8,128)(2,1)S(1)}, u32[]{:S(2)}, u32[]{:S(2)}) async-start(bf16[16,256,128]{2,1,0:T(8,128)(2,1)} %get-tuple-element.25), calls=%async_computation.1 | async-start | bytes 2097152 | tf_op jit(solution)/shard_map/all_to_all | solution.py:493
  64.6 5.8 %collective-permute-start.1 = (bf16[2,512,128]{2,1,0:T(8,128)(2,1)S(1)}, bf16[2,512,128]{2,1,0:T(8,128)(2,1)S(1)}, u32[]{:S(2)}, u32[]{:S(2)}) collective-permute-start(bf16[2,512,128]{2,1,0:T(8,128)(2,1)S(1)} %get-tuple-element.27), channel_id=1, source_target_pairs={{16,0},{32,16},{48,32},{64,48},{80,64},{96,80},{112,96},{17,1},{33... | collective-permute-start | bytes 786440 | tf_op jit(solution)/shard_map/ppermute | solution.py:504
  86.7 7.2 %copy-start.2 = (bf16[16,256,128]{2,1,0:T(8,128)(2,1)}, bf16[16,256,128]{2,1,0:T(8,128)(2,1)S(1)}, u32[]{:S(2)}) copy-start(bf16[16,256,128]{2,1,0:T(8,128)(2,1)S(1)} %all-to-all-done.1.x_hbm) | copy-start | bytes 3145732
  86.7 34.4 %all-to-all-start.3 = ((bf16[16,256,128]{2,1,0:T(8,128)(2,1)}), bf16[16,256,128]{2,1,0:T(8,128)(2,1)S(1)}, u32[]{:S(2)}, u32[]{:S(2)}) async-start(bf16[16,256,128]{2,1,0:T(8,128)(2,1)} %get-tuple-element.35), calls=%async_computation.3 | async-start | bytes 2097152 | tf_op jit(solution)/shard_map/all_to_all | solution.py:493
  110.6 7.7 %collective-permute-start.2 = (bf16[2,512,128]{2,1,0:T(8,128)(2,1)S(1)}, bf16[2,512,128]{2,1,0:T(8,128)(2,1)S(1)}, u32[]{:S(2)}, u32[]{:S(2)}) collective-permute-start(bf16[2,512,128]{2,1,0:T(8,128)(2,1)S(1)} %get-tuple-element.33), channel_id=1, source_target_pairs={{0,16},{16,32},{32,48},{48,64},{64,80},{80,96},{96,112},{1,17},{17... | collective-permute-start | bytes 786440 | tf_op jit(solution)/shard_map/ppermute | solution.py:513
  114.3 5.8 %collective-permute-start.3 = (bf16[2,512,128]{2,1,0:T(8,128)(2,1)S(1)}, bf16[2,512,128]{2,1,0:T(8,128)(2,1)S(1)}, u32[]{:S(2)}, u32[]{:S(2)}) collective-permute-start(bf16[2,512,128]{2,1,0:T(8,128)(2,1)S(1)} %get-tuple-element.34), channel_id=1, source_target_pairs={{16,0},{32,16},{48,32},{64,48},{80,64},{96,80},{112,96},{17,1},{33... | collective-permute-start | bytes 786440 | tf_op jit(solution)/shard_map/ppermute | solution.py:512
  121.1 48.1 %copy-start.1 = (bf16[16,256,128]{2,1,0:T(8,128)(2,1)}, bf16[16,256,128]{2,1,0:T(8,128)(2,1)S(1)}, u32[]{:S(2)}) copy-start(bf16[16,256,128]{2,1,0:T(8,128)(2,1)S(1)} %all-to-all-done.3.two_hbm) | copy-start | bytes 3145732

commit v7 on v5

--- a/solution.py
+++ b/solution.py
@@ -119,68 +119,53 @@
     )(*(off_chip(x) for x in (k, v, q, g)))
 
 
-def unpack_kernel(
-    one_hbm, two_hbm, k_hbm, v_hbm, q_hbm, o_hbm, in_refs, out_refs, one_sems, two_sems, out_sems,
-):
-    rows, half = k_hbm.shape[0], two_hbm.shape[1]
-    chunk = rows // CHUNKS
-    pairs = ((k_hbm, v_hbm), (q_hbm, o_hbm))
-
-    def span(c):
-        return pl.ds(c * chunk, chunk)
-
-    def load(n, c):
-        if n == 0:
-            source = one_hbm.at[:, span(c)]
-        elif c * chunk < half:
-            source = two_hbm.at[:, span(c)]
-        else:
-            source = one_hbm.at[:, pl.ds(rows + c * chunk - half, chunk)]
+def chunks(source, row, size, to, chunk):
+    return [(source, row + i, chunk, to + i) for i in range(0, size, chunk)]
+
+
+def unpack_kernel(*refs, jobs, count, skip):
+    source, targets = refs[0], refs[1 + skip : 1 + skip + count]
+    out_refs, sems = refs[1 + skip + count :]
+
+    def store(n, i):
+        target, row, size, at = jobs[n]
         return pltpu.make_async_copy(
-            source, in_refs.at[n, :, span(c)], (one_sems if n == 0 else two_sems).at[c]
+            out_refs.at[i, pl.ds(at, size)], targets[target + i].at[pl.ds(row, size)], sems.at[i, n]
         )
 
-    def store(n, i, c):
-        return pltpu.make_async_copy(
-            out_refs.at[2 * n + i, span(c)], pairs[n][i].at[span(c)], out_sems.at[2 * n + i, c]
-        )
-
-    order = [(n, c) for n in range(2) for c in range(CHUNKS)]
-    for n, c in order:
-        load(n, c).start()
-    for n, c in order:
-        load(n, c).wait()
-        part = slice(c * chunk, (c + 1) * chunk)
-        for p in range(k_hbm.shape[1] // PAIR):
+    for n, (_, _, size, at) in enumerate(jobs):
+        part = slice(at, at + size)
+        for p in range(source.shape[0] // 2):
             cols = slice(p * PAIR, (p + 1) * PAIR)
-            halves = swap_halves(in_refs[n, 2 * p, part], in_refs[n, 2 * p + 1, part])
-            out_refs[2 * n, part, cols], out_refs[2 * n + 1, part, cols] = halves
+            halves = swap_halves(source[2 * p, part], source[2 * p + 1, part])
+            out_refs[0, part, cols], out_refs[1, part, cols] = halves
         for i in range(2):
-            store(n, i, c).start()
-    for n, c in order:
+            store(n, i).start()
+    for n in range(len(jobs)):
         for i in range(2):
-            store(n, i, c).wait()
-
-
-def unpack_heads(one, two):
-    heads, half, _ = two.shape
-    rows, cols = 2 * half, heads * HEAD_DIM
+            store(n, i).wait()
+
+
+def unpack_heads(x, full_rows, jobs, count, name, into=()):
+    heads, rows, _ = x.shape
+    cols = heads * HEAD_DIM
     hbm = pl.BlockSpec(memory_space=pltpu.HBM)
     return pl.pallas_call(
-        unpack_kernel,
-        out_shape=(pltpu.HBM((rows, cols), one.dtype),) * 4,
-        in_specs=[hbm, hbm],
-        out_specs=(hbm,) * 4,
+        partial(unpack_kernel, jobs=jobs, count=count, skip=len(into)),
+        out_shape=(pltpu.HBM((full_rows, cols), x.dtype),) * count,
+        in_specs=[pl.BlockSpec(memory_space=pltpu.VMEM)] + [hbm] * len(into),
+        out_specs=(hbm,) * count,
         scratch_shapes=[
-            pltpu.VMEM((2, heads, rows, PAIR), one.dtype),
-            pltpu.VMEM((4, rows, cols), one.dtype),
-            pltpu.SemaphoreType.DMA((CHUNKS,)),
-            pltpu.SemaphoreType.DMA((CHUNKS,)),
-            pltpu.SemaphoreType.DMA((4, CHUNKS)),
+            pltpu.VMEM((2, rows, cols), x.dtype),
+            pltpu.SemaphoreType.DMA((2, len(jobs))),
         ],
-        compiler_params=pltpu.CompilerParams(vmem_limit_bytes=60 << 20),
-        name="unpack_heads",
-    )(off_chip(one), off_chip(two))
+        input_output_aliases={1 + i: count - len(into) + i for i in range(len(into))},
+        compiler_params=pltpu.CompilerParams(vmem_limit_bytes=16 << 20),
+        cost_estimate=pl.CostEstimate(
+            flops=0, transcendentals=0, bytes_accessed=4 * rows * cols * x.dtype.itemsize
+        ),
+        name=name,
+    )(on_chip(x), *(off_chip(a) for a in into))
 
 
 def in_turn(*tasks):
@@ -339,21 +324,20 @@
 
 
 def second_kernel(
-    pattern_ref, valid_ref, start_ref, x_hbm, kv_hbm, acc_hbm,
+    pattern_ref, valid_ref, start_ref, qg_ref, kv_hbm, acc_hbm,
     z_hbm, first_ref, last_ref, down_ref, up_ref,
-    kv_ref, acc_ref, qg_ref, od_ref, dkv_ref, both_ref, pd_ref, in_sems, od_sems, dkv_sems, **sizes,
+    kv_ref, acc_ref, od_ref, dkv_ref, both_ref, pd_ref, in_sems, od_sems, dkv_sems, **sizes,
 ):
     shards, half = qg_ref.shape[:2]
     rows = 2 * half
     edge = first_ref.shape[0]
     copies = [
         pltpu.make_async_copy(source, target, in_sems.at[i])
-        for i, (source, target) in enumerate(((x_hbm, qg_ref), (kv_hbm, kv_ref), (acc_hbm, acc_ref)))
+        for i, (source, target) in enumerate(((kv_hbm, kv_ref), (acc_hbm, acc_ref)))
     ]
     for copy in copies:
         copy.start()
     copies[0].wait()
-    copies[1].wait()
 
     def send_od(t):
         return pltpu.make_async_copy(od_ref.at[t], z_hbm.at[t, pl.ds(rows, half)], od_sems.at[t])
@@ -363,7 +347,7 @@
 
     query_blocks(
         pattern_ref, valid_ref, start_ref, kv_ref, qg_ref, acc_ref, od_ref, both_ref, pd_ref,
-        send_od, chunk=1, ready=copies[2].wait, **sizes,
+        send_od, chunk=1, ready=copies[1].wait, **sizes,
     )
     low = lax.broadcasted_iota(jnp.int32, (rows, PAIR), 1) < HEAD_DIM
 
@@ -390,7 +374,7 @@
     return pl.CostEstimate(flops=12 * PAIR * work, transcendentals=work, bytes_accessed=16 << 20)
 
 
-def first_half(pattern, valid_rows, start, x, before, after, group=16, lines=16):
+def first_half(pattern, valid_rows, start, x, before, after, group=32, lines=16):
     keys_num = pattern.shape[0] * BLOCK // (x.shape[0] * before.shape[1])
     shards, edge, rows = x.shape[0], before.shape[0], before.shape[1]
     half, ext = rows // 2, shards + 2 * edge
@@ -423,7 +407,7 @@
     )(pattern, valid_rows, start, off_chip(x), on_chip(before), on_chip(after))
 
 
-def second_half(pattern, valid_rows, start, x, kv, acc, edge, group=16, lines=16):
+def second_half(pattern, valid_rows, start, x, kv, acc, edge, group=32, lines=16):
     shards, half = x.shape[:2]
     rows = 2 * half
     keys_num = pattern.shape[0] * BLOCK // (shards * rows)
@@ -436,24 +420,23 @@
         out_shape=(pltpu.HBM((shards, rows + half, PAIR), x.dtype),)
         + (pltpu.VMEM(face, jnp.float32),) * 2
         + (pltpu.VMEM(face, x.dtype),) * 2,
-        in_specs=[smem, smem, smem, hbm, hbm, hbm],
+        in_specs=[smem, smem, smem, vmem, hbm, hbm],
         out_specs=(hbm, vmem, vmem, vmem, vmem),
         scratch_shapes=[
             pltpu.VMEM(kv.shape, kv.dtype),
             pltpu.VMEM(acc.shape, acc.dtype),
             pltpu.VMEM((shards, half, PAIR), x.dtype),
-            pltpu.VMEM((shards, half, PAIR), x.dtype),
             pltpu.VMEM((shards, rows, PAIR), x.dtype),
             pltpu.VMEM((group, PAIR, keys_num * BLOCK), jnp.float32),
             pltpu.VMEM((group, PAIR, keys_num * BLOCK), x.dtype),
-            pltpu.SemaphoreType.DMA((3,)),
+            pltpu.SemaphoreType.DMA((2,)),
             pltpu.SemaphoreType.DMA((shards,)),
             pltpu.SemaphoreType.DMA((shards,)),
         ],
         compiler_params=pltpu.CompilerParams(vmem_limit_bytes=32 << 20),
         cost_estimate=cost(shards * half, keys_num),
         name="second_half",
-    )(pattern, valid_rows, start, off_chip(x), off_chip(kv), off_chip(acc))
+    )(pattern, valid_rows, start, on_chip(x), off_chip(kv), off_chip(acc))
 
 
 def join_kernel(z_in, first_ref, last_ref, low_ref, high_ref, z_hbm, sum_ref, sems):
@@ -497,6 +480,7 @@
     down = [(i + 1, i) for i in range(size - 1)]
     rows = query.shape[0]
     edge = FACE * BLOCK // rows
+    half, chunk = rows // 2, rows // CHUNKS
     one, two = pack_heads(key, value, query, grad_out)
     one = exchange(one)
     first, last = take_faces(one, edge, rows)
@@ -510,8 +494,13 @@
     z, first, last, to_before, to_after = second_half(*scalars, two, kv, acc, edge)
     high = lax.ppermute(to_before, "slab", down)
     low = lax.ppermute(to_after, "slab", up)
+    done = unpack_heads(od, rows, chunks(0, 0, half, 0, chunk), 2, "unpack_first")
+    z, *done = lax.optimization_barrier((z, *done))
     z = exchange(join_faces(z, first, last, low, high))
-    grad_key, grad_value, grad_query, attn_out = unpack_heads(z, od)
+    jobs = chunks(0, 0, rows, 0, chunk) + chunks(2, half, half, rows, chunk)
+    grad_key, grad_value, grad_query, attn_out = unpack_heads(
+        z, rows, jobs, 4, "unpack_second", into=done
+    )
     return (attn_out, grad_query, grad_key, grad_value)
 
 

time: 171 us -> 169 us (0.988)
    pallas_call x1 -> x2, Pallas kernels: 3.83 us -> 3.2 us  [unpack_heads(): pl.pallas_call(partial(unpack_kernel, jobs=jobs, count=count, skip=len(in...]
where the time goes in v7:
time: 169 us; the launch traced here: 167 us
  blocking collectives  95.8 us (57%)
  Pallas kernels  41.8 us (25%)
  starting transfers between devices  22.1 us (13%)
  waiting for transfers between devices  6.29 us (4%)
    all_to_all x2, blocking collectives, exchange(): return lax.all_to_all(x, 'seq', split_axis=0, concat_axis=0, tiled=True)  95.8 us
    pallas_call x1, Pallas kernels, first_half(): pl.pallas_call(partial(first_kernel, keys_num=keys_num, group=group, line...  16.6 us
    pallas_call x1, Pallas kernels, second_half(): pl.pallas_call(partial(second_kernel, keys_num=keys_num, group=group, lin...  16.3 us
    all_to_all x2, starting transfers between devices, exchange(): return lax.all_to_all(x, 'seq', split_axis=0, concat_axis=0, tiled=True)  11 us
    pallas_call x1, Pallas kernels, pack_heads(): pl.pallas_call(pack_kernel, out_shape=tuple((pltpu.HBM((heads, size, PAIR...  3.7 us
    ppermute x1, starting transfers between devices, body(): after = lax.ppermute(first, 'slab', down)  3.64 us
    ppermute x1, starting transfers between devices, body(): low = lax.ppermute(to_after, 'slab', up)  3.4 us
  transfers between devices with their start and end apart: 6, of which 4 were waited for; matrix products, arithmetic and copies ran while one was open for 0% of the time, Pallas kernels for 21%

profile of v7, /device:TPU:2, one launch (start us, length us, event | category | flops | bytes accessed | tf_op | source)
XLA Modules:
  0.0 167.1 jit_solution(4883439936698395848)
XLA Ops:
  0.6 3.7 %pack_heads.1 = (bf16[16,768,128]{2,1,0:T(8,128)(2,1)}, bf16[16,256,128]{2,1,0:T(8,128)(2,1)}) custom-call(bf16[512,1024]{1,0:T(8,128)(2,1)} %k_hbm.1, bf16[512,1024]{1,0:T(8,128)(2,1)} %v_hbm.1, bf16[512,1024]{1,0:T(8,128)(2,1)} %q_hbm.1, bf16[512,1024]{1,0:T(8,128)(2,1)} %g_hbm.1), custom_call_target="tpu_custom_call" | custom-call | tf_op jit(solution)/shard_map/pack_heads/pallas_call | solution.py:105
  4.3 47.8 %all_to_all.20.x_hbm = bf16[16,768,128]{2,1,0:T(8,128)(2,1)} all-to-all(bf16[16,768,128]{2,1,0:T(8,128)(2,1)} %get-tuple-element.26), channel_id=1, replica_groups=mesh['slab'=8,'seq'=16] {'seq'}, dimensions={0} | all-to-all | bytes 6291456 | tf_op jit(solution)/shard_map/all_to_all | solution.py:476
  52.1 0.0 copy-start.1
  52.1 0.0 copy-start
  52.1 3.8 %all-to-all-start = ((bf16[16,256,128]{2,1,0:T(8,128)(2,1)}), bf16[16,256,128]{2,1,0:T(8,128)(2,1)S(1)}, u32[]{:S(2)}, u32[]{:S(2)}) async-start(bf16[16,256,128]{2,1,0:T(8,128)(2,1)} %get-tuple-element.25), calls=%async_computation | async-start | bytes 2097152 | tf_op jit(solution)/shard_map/all_to_all | solution.py:476
  55.9 1.0 take_faces.1
  57.0 1.9 %collective-permute-start = (bf16[2,512,128]{2,1,0:T(8,128)(2,1)S(1)}, bf16[2,512,128]{2,1,0:T(8,128)(2,1)S(1)}, u32[]{:S(2)}, u32[]{:S(2)}) collective-permute-start(bf16[2,512,128]{2,1,0:T(8,128)(2,1)S(1)} %get-tuple-element.27), channel_id=1, source_target_pairs={{0,16},{16,32},{32,48},{48,64},{64,80},{80,96},{96,112},{1,17},{17... | collective-permute-start | bytes 786440 | tf_op jit(solution)/shard_map/ppermute | solution.py:487
  58.9 3.6 %collective-permute-start.1 = (bf16[2,512,128]{2,1,0:T(8,128)(2,1)S(1)}, bf16[2,512,128]{2,1,0:T(8,128)(2,1)S(1)}, u32[]{:S(2)}, u32[]{:S(2)}) collective-permute-start(bf16[2,512,128]{2,1,0:T(8,128)(2,1)S(1)} %get-tuple-element.28), channel_id=1, source_target_pairs={{16,0},{32,16},{48,32},{64,48},{80,64},{96,80},{112,96},{17,1},{33... | collective-permute-start | bytes 786440 | tf_op jit(solution)/shard_map/ppermute | solution.py:488
  62.6 0.0 copy-done.1
  62.6 0.1 copy.13
  62.7 0.1 reshape.14.pattern_ref
  62.8 1.9 %collective-permute-done.before_ref = bf16[2,512,128]{2,1,0:T(8,128)(2,1)S(1)} collective-permute-done((bf16[2,512,128]{2,1,0:T(8,128)(2,1)S(1)}, bf16[2,512,128]{2,1,0:T(8,128)(2,1)S(1)}, u32[]{:S(2)}, u32[]{:S(2)}) %collective-permute-start) | collective-permute-done | bytes 262176 | tf_op jit(solution)/shard_map/ppermute | solution.py:487
  64.7 1.8 %collective-permute-done.1.after_ref = bf16[2,512,128]{2,1,0:T(8,128)(2,1)S(1)} collective-permute-done((bf16[2,512,128]{2,1,0:T(8,128)(2,1)S(1)}, bf16[2,512,128]{2,1,0:T(8,128)(2,1)S(1)}, u32[]{:S(2)}, u32[]{:S(2)}) %collective-permute-start.1) | collective-permute-done | bytes 262176 | tf_op jit(solution)/shard_map/ppermute | solution.py:488
  66.4 0.0 copy-done
  66.4 16.6 %first_half.1 = (bf16[16,256,128]{2,1,0:T(8,128)(2,1)}, bf16[10240,128]{1,0:T(8,128)(2,1)}, f32[10240,128]{1,0:T(8,128)}) custom-call(s32[1024]{0:T(1024)S(1)} %reshape.14.pattern_ref, s32[1024]{0:T(1024)S(1)} %copy-done, s32[1]{0:T(128)} %bitcast.start_ref, bf16[16,768,128]{2,1,0:T(8,128)(2,1)} %all_to_all.20.x_hbm, ...), custom_call_target="tpu_custom_call" | custom-call | flops 3221225472 | bytes 16777216 | tf_op jit(solution)/shard_map/first_half/pallas_call | solution.py:384
  83.0 0.0 all-to-all-done.qg_ref
  83.1 7.2 %all-to-all-start.2 = ((bf16[16,256,128]{2,1,0:T(8,128)(2,1)}), bf16[16,256,128]{2,1,0:T(8,128)(2,1)S(1)}, u32[]{:S(2)}, u32[]{:S(2)}) async-start(bf16[16,256,128]{2,1,0:T(8,128)(2,1)} %get-tuple-element.32), calls=%async_computation.2 | async-start | bytes 2097152 | tf_op jit(solution)/shard_map/all_to_all | solution.py:476
  90.2 16.3 %second_half.1 = (bf16[16,768,128]{2,1,0:T(8,128)(2,1)}, f32[2,512,128]{2,1,0:T(8,128)S(1)}, f32[2,512,128]{2,1,0:T(8,128)S(1)}, bf16[2,512,128]{2,1,0:T(8,128)(2,1)S(1)}, bf16[2,512,128]{2,1,0:T(8,128)(2,1)}) custom-call(s32[1024]{0:T(1024)S(1)} %reshape.14.pattern_ref, s32[1024]{0:T(1024)S(1)} %copy-done, s32[1]{0:T(128)} %bitcast.start_ref, ...), custom_call_target="tpu_custom_call" | custom-call | flops 3221225472 | bytes 16777216 | tf_op jit(solution)/shard_map/second_half/pallas_call | solution.py:418
  106.5 3.4 %collective-permute-start.2 = (bf16[2,512,128]{2,1,0:T(8,128)(2,1)}, bf16[2,512,128]{2,1,0:T(8,128)(2,1)S(1)}, u32[]{:S(2)}, u32[]{:S(2)}) collective-permute-start(bf16[2,512,128]{2,1,0:T(8,128)(2,1)} %get-tuple-element.38), channel_id=1, source_target_pairs={{0,16},{16,32},{32,48},{48,64},{64,80},{80,96},{96,112},{1,17},{17... | collective-permute-start | bytes 786440 | tf_op jit(solution)/shard_map/ppermute | solution.py:496
  109.9 2.2 %collective-permute-start.3 = (bf16[2,512,128]{2,1,0:T(8,128)(2,1)S(1)}, bf16[2,512,128]{2,1,0:T(8,128)(2,1)S(1)}, u32[]{:S(2)}, u32[]{:S(2)}) collective-permute-start(bf16[2,512,128]{2,1,0:T(8,128)(2,1)S(1)} %get-tuple-element.39), channel_id=1, source_target_pairs={{16,0},{32,16},{48,32},{64,48},{80,64},{96,80},{112,96},{17,1},{33... | collective-permute-start | bytes 786440 | tf_op jit(solution)/shard_map/ppermute | solution.py:495
  112.1 0.0 all-to-all-done.2.refs_0_
  112.1 1.2 unpack_first.1
  113.3 1.1 collective-permute-done.2.low_ref
  114.4 1.5 collective-permute-done.3.high_ref
  115.9 1.0 join_faces.1
  116.9 48.0 %all_to_all.21.refs_0_ = bf16[16,768,128]{2,1,0:T(8,128)(2,1)S(1)} all-to-all(bf16[16,768,128]{2,1,0:T(8,128)(2,1)} %join_faces.1), channel_id=1, replica_groups=mesh['slab'=8,'seq'=16] {'seq'}, dimensions={0} | all-to-all | bytes 6291456 | tf_op jit(solution)/shard_map/all_to_all | solution.py:476
  164.9 2.0 %unpack_second.1 = (bf16[512,1024]{1,0:T(8,128)(2,1)}, bf16[512,1024]{1,0:T(8,128)(2,1)}, bf16[512,1024]{1,0:T(8,128)(2,1)}, bf16[512,1024]{1,0:T(8,128)(2,1)}) custom-call(bf16[16,768,128]{2,1,0:T(8,128)(2,1)S(1)} %all_to_all.21.refs_0_, bf16[512,1024]{1,0:T(8,128)(2,1)} %get-tuple-element.40.refs_1_, ...), custom_call_target="tpu_custom_call", output_to_operand_aliasing={{2}: (1, {}), {3}: (2, {})} | custom-call | bytes 6291456 | tf_op jit(solution)/shard_map/unpack_second/pallas_call | solution.py:153
Async XLA Ops:
  52.1 10.4 %copy-start.1 = (s32[128,8]{0,1:T(8,128)S(1)}, s32[128,8]{0,1:T(8,128)}, u32[]{:S(2)}) copy-start(s32[128,8]{0,1:T(8,128)} %param.10) | copy-start | bytes 12292
  52.1 14.3 %copy-start = (s32[1024]{0:T(1024)S(1)}, s32[1024]{0:T(1024)}, u32[]{:S(2)}) copy-start(s32[1024]{0:T(1024)} %valid_ref.3) | copy-start | bytes 12292
  52.1 30.9 %all-to-all-start = ((bf16[16,256,128]{2,1,0:T(8,128)(2,1)}), bf16[16,256,128]{2,1,0:T(8,128)(2,1)S(1)}, u32[]{:S(2)}, u32[]{:S(2)}) async-start(bf16[16,256,128]{2,1,0:T(8,128)(2,1)} %get-tuple-element.25), calls=%async_computation | async-start | bytes 2097152 | tf_op jit(solution)/shard_map/all_to_all | solution.py:476
  57.0 7.7 %collective-permute-start = (bf16[2,512,128]{2,1,0:T(8,128)(2,1)S(1)}, bf16[2,512,128]{2,1,0:T(8,128)(2,1)S(1)}, u32[]{:S(2)}, u32[]{:S(2)}) collective-permute-start(bf16[2,512,128]{2,1,0:T(8,128)(2,1)S(1)} %get-tuple-element.27), channel_id=1, source_target_pairs={{0,16},{16,32},{32,48},{48,64},{64,80},{80,96},{96,112},{1,17},{17... | collective-permute-start | bytes 786440 | tf_op jit(solution)/shard_map/ppermute | solution.py:487
  58.9 7.5 %collective-permute-start.1 = (bf16[2,512,128]{2,1,0:T(8,128)(2,1)S(1)}, bf16[2,512,128]{2,1,0:T(8,128)(2,1)S(1)}, u32[]{:S(2)}, u32[]{:S(2)}) collective-permute-start(bf16[2,512,128]{2,1,0:T(8,128)(2,1)S(1)} %get-tuple-element.28), channel_id=1, source_target_pairs={{16,0},{32,16},{48,32},{64,48},{80,64},{96,80},{112,96},{17,1},{33... | collective-permute-start | bytes 786440 | tf_op jit(solution)/shard_map/ppermute | solution.py:488
  83.1 29.0 %all-to-all-start.2 = ((bf16[16,256,128]{2,1,0:T(8,128)(2,1)}), bf16[16,256,128]{2,1,0:T(8,128)(2,1)S(1)}, u32[]{:S(2)}, u32[]{:S(2)}) async-start(bf16[16,256,128]{2,1,0:T(8,128)(2,1)} %get-tuple-element.32), calls=%async_computation.2 | async-start | bytes 2097152 | tf_op jit(solution)/shard_map/all_to_all | solution.py:476
  106.5 7.9 %collective-permute-start.2 = (bf16[2,512,128]{2,1,0:T(8,128)(2,1)}, bf16[2,512,128]{2,1,0:T(8,128)(2,1)S(1)}, u32[]{:S(2)}, u32[]{:S(2)}) collective-permute-start(bf16[2,512,128]{2,1,0:T(8,128)(2,1)} %get-tuple-element.38), channel_id=1, source_target_pairs={{0,16},{16,32},{32,48},{48,64},{64,80},{80,96},{96,112},{1,17},{17... | collective-permute-start | bytes 786440 | tf_op jit(solution)/shard_map/ppermute | solution.py:496
  109.9 6.0 %collective-permute-start.3 = (bf16[2,512,128]{2,1,0:T(8,128)(2,1)S(1)}, bf16[2,512,128]{2,1,0:T(8,128)(2,1)S(1)}, u32[]{:S(2)}, u32[]{:S(2)}) collective-permute-start(bf16[2,512,128]{2,1,0:T(8,128)(2,1)S(1)} %get-tuple-element.39), channel_id=1, source_target_pairs={{16,0},{32,16},{48,32},{64,48},{80,64},{96,80},{112,96},{17,1},{33... | collective-permute-start | bytes 786440 | tf_op jit(solution)/shard_map/ppermute | solution.py:495

commit v8 on v7

--- a/solution.py
+++ b/solution.py
@@ -26,11 +26,13 @@
     return pltpu.with_memory_space_constraint(x, pltpu.HBM)
 
 
-def faces_kernel(x_hbm, first_ref, last_ref, sems):
-    edge, rows = first_ref.shape[:2]
+def faces_kernel(odd_ref, x_hbm, inner_ref, outer_ref, sems):
+    edge, rows = inner_ref.shape[:2]
+    end = x_hbm.shape[0] - edge
+    odd = odd_ref[0]
     copies = [
         pltpu.make_async_copy(x_hbm.at[pl.ds(at, edge), pl.ds(0, rows)], ref, sems.at[i])
-        for i, (at, ref) in enumerate(((0, first_ref), (x_hbm.shape[0] - edge, last_ref)))
+        for i, (at, ref) in enumerate((((1 - odd) * end, inner_ref), (odd * end, outer_ref)))
     ]
     for copy in copies:
         copy.start()
@@ -38,17 +40,17 @@
         copy.wait()
 
 
-def take_faces(x, edge, rows):
+def take_faces(odd, x, edge, rows):
     vmem = pl.BlockSpec(memory_space=pltpu.VMEM)
     return pl.pallas_call(
         faces_kernel,
         out_shape=(pltpu.VMEM((edge, rows, PAIR), x.dtype),) * 2,
-        in_specs=[pl.BlockSpec(memory_space=pltpu.HBM)],
+        in_specs=[pl.BlockSpec(memory_space=pltpu.SMEM), pl.BlockSpec(memory_space=pltpu.HBM)],
         out_specs=(vmem, vmem),
         scratch_shapes=[pltpu.SemaphoreType.DMA((2,))],
         compiler_params=pltpu.CompilerParams(vmem_limit_bytes=4 << 20),
         name="take_faces",
-    )(off_chip(x))
+    )(odd, off_chip(x))
 
 
 def swap_halves(a, b):
@@ -283,20 +285,24 @@
 
 
 def first_kernel(
-    pattern_ref, valid_ref, start_ref, x_hbm, before_ref, after_ref,
+    pattern_ref, valid_ref, start_ref, odd_ref, x_hbm, inner_ref, outer_ref,
     od_hbm, kv_hbm, acc_hbm,
     kv_ref, acc_ref, qg_ref, od_ref, both_ref, pd_ref, in_sems, od_sems, out_sems, **sizes,
 ):
     shards, half = qg_ref.shape[:2]
     rows = x_hbm.shape[1] - half
-    edge = before_ref.shape[0]
-
-    def fetch(source, i):
-        return pltpu.make_async_copy(source, kv_ref.at[pl.ds(i * rows, rows)], in_sems.at[i])
-
-    copies = [fetch(x_hbm.at[t, pl.ds(0, rows)], edge + t) for t in range(shards)]
-    copies += [fetch(before_ref.at[t], t) for t in range(edge)]
-    copies += [fetch(after_ref.at[t], edge + shards + t) for t in range(edge)]
+    edge = inner_ref.shape[0]
+    above = edge + shards
+    odd = odd_ref[0]
+
+    def fetch(source, at, i):
+        span = pl.ds(pl.multiple_of(at * rows, rows), rows)
+        return pltpu.make_async_copy(source, kv_ref.at[span], in_sems.at[i])
+
+    copies = [fetch(x_hbm.at[t, pl.ds(0, rows)], edge + t, t) for t in range(shards)]
+    for t in range(edge):
+        copies += [fetch(inner_ref.at[t], (1 - odd) * above + t, len(copies))]
+        copies += [fetch(outer_ref.at[t], odd * above + t, len(copies))]
     copies += [
         pltpu.make_async_copy(x_hbm.at[:, pl.ds(rows, half)], qg_ref, in_sems.at[len(copies)])
     ]
@@ -324,13 +330,13 @@
 
 
 def second_kernel(
-    pattern_ref, valid_ref, start_ref, qg_ref, kv_hbm, acc_hbm,
-    z_hbm, first_ref, last_ref, down_ref, up_ref,
+    pattern_ref, valid_ref, start_ref, odd_ref, qg_ref, kv_hbm, acc_hbm,
+    z_hbm, inner_own_ref, outer_own_ref, inner_rim_ref, outer_rim_ref,
     kv_ref, acc_ref, od_ref, dkv_ref, both_ref, pd_ref, in_sems, od_sems, dkv_sems, **sizes,
 ):
     shards, half = qg_ref.shape[:2]
     rows = 2 * half
-    edge = first_ref.shape[0]
+    edge = inner_own_ref.shape[0]
     copies = [
         pltpu.make_async_copy(source, target, in_sems.at[i])
         for i, (source, target) in enumerate(((kv_hbm, kv_ref), (acc_hbm, acc_ref)))
@@ -352,17 +358,18 @@
     low = lax.broadcasted_iota(jnp.int32, (rows, PAIR), 1) < HEAD_DIM
 
     def scaled(s):
-        tile = acc_ref[s * rows : (s + 1) * rows, :]
+        tile = acc_ref[pl.ds(pl.multiple_of(s * rows, rows), rows), :]
         return jnp.where(low, tile * score_scale, tile)
 
     for t in range(edge, shards - edge):
         dkv_ref[t] = scaled(edge + t).astype(dkv_ref.dtype)
         send_dkv(t).start()
+    odd, above, end = odd_ref[0], edge + shards, shards - edge
     for s in range(edge):
-        down_ref[s] = scaled(s).astype(down_ref.dtype)
-        up_ref[s] = scaled(edge + shards + s).astype(up_ref.dtype)
-        first_ref[s] = scaled(edge + s)
-        last_ref[s] = scaled(shards + s)
+        inner_rim_ref[s] = scaled((1 - odd) * above + s).astype(inner_rim_ref.dtype)
+        outer_rim_ref[s] = scaled(odd * above + s).astype(outer_rim_ref.dtype)
+        inner_own_ref[s] = scaled(edge + (1 - odd) * end + s)
+        outer_own_ref[s] = scaled(edge + odd * end + s)
     for t in range(shards):
         send_od(t).wait()
     for t in range(edge, shards - edge):
@@ -374,9 +381,9 @@
     return pl.CostEstimate(flops=12 * PAIR * work, transcendentals=work, bytes_accessed=16 << 20)
 
 
-def first_half(pattern, valid_rows, start, x, before, after, group=32, lines=16):
-    keys_num = pattern.shape[0] * BLOCK // (x.shape[0] * before.shape[1])
-    shards, edge, rows = x.shape[0], before.shape[0], before.shape[1]
+def first_half(pattern, valid_rows, start, odd, x, inner, outer, group=16, lines=16):
+    keys_num = pattern.shape[0] * BLOCK // (x.shape[0] * inner.shape[1])
+    shards, edge, rows = x.shape[0], inner.shape[0], inner.shape[1]
     half, ext = rows // 2, shards + 2 * edge
     smem = pl.BlockSpec(memory_space=pltpu.SMEM)
     hbm = pl.BlockSpec(memory_space=pltpu.HBM)
@@ -388,7 +395,7 @@
             pltpu.HBM((ext * rows, PAIR), x.dtype),
             pltpu.HBM((ext * rows, PAIR), jnp.float32),
         ),
-        in_specs=[smem, smem, smem, hbm, vmem, vmem],
+        in_specs=[smem, smem, smem, smem, hbm, vmem, vmem],
         out_specs=(hbm, hbm, hbm),
         scratch_shapes=[
             pltpu.VMEM((ext * rows, PAIR), x.dtype),
@@ -404,10 +411,10 @@
         compiler_params=pltpu.CompilerParams(vmem_limit_bytes=32 << 20),
         cost_estimate=cost(shards * half, keys_num),
         name="first_half",
-    )(pattern, valid_rows, start, off_chip(x), on_chip(before), on_chip(after))
-
-
-def second_half(pattern, valid_rows, start, x, kv, acc, edge, group=32, lines=16):
+    )(pattern, valid_rows, start, odd, off_chip(x), on_chip(inner), on_chip(outer))
+
+
+def second_half(pattern, valid_rows, start, odd, x, kv, acc, edge, group=32, lines=16):
     shards, half = x.shape[:2]
     rows = 2 * half
     keys_num = pattern.shape[0] * BLOCK // (shards * rows)
@@ -420,7 +427,7 @@
         out_shape=(pltpu.HBM((shards, rows + half, PAIR), x.dtype),)
         + (pltpu.VMEM(face, jnp.float32),) * 2
         + (pltpu.VMEM(face, x.dtype),) * 2,
-        in_specs=[smem, smem, smem, vmem, hbm, hbm],
+        in_specs=[smem, smem, smem, smem, vmem, hbm, hbm],
         out_specs=(hbm, vmem, vmem, vmem, vmem),
         scratch_shapes=[
             pltpu.VMEM(kv.shape, kv.dtype),
@@ -436,19 +443,22 @@
         compiler_params=pltpu.CompilerParams(vmem_limit_bytes=32 << 20),
         cost_estimate=cost(shards * half, keys_num),
         name="second_half",
-    )(pattern, valid_rows, start, on_chip(x), off_chip(kv), off_chip(acc))
-
-
-def join_kernel(z_in, first_ref, last_ref, low_ref, high_ref, z_hbm, sum_ref, sems):
-    edge, rows = first_ref.shape[:2]
+    )(pattern, valid_rows, start, odd, on_chip(x), off_chip(kv), off_chip(acc))
+
+
+def join_kernel(
+    odd_ref, z_in, inner_ref, outer_ref, inner_rim_ref, outer_rim_ref, z_hbm, sum_ref, sems,
+):
+    edge, rows = inner_ref.shape[:2]
+    odd = odd_ref[0]
     shards = z_hbm.shape[0]
-    sum_ref[0] = (first_ref[...] + low_ref[...].astype(jnp.float32)).astype(sum_ref.dtype)
-    sum_ref[1] = (last_ref[...] + high_ref[...].astype(jnp.float32)).astype(sum_ref.dtype)
+    sum_ref[0] = (inner_ref[...] + inner_rim_ref[...].astype(jnp.float32)).astype(sum_ref.dtype)
+    sum_ref[1] = (outer_ref[...] + outer_rim_ref[...].astype(jnp.float32)).astype(sum_ref.dtype)
     copies = [
         pltpu.make_async_copy(
             sum_ref.at[i], z_hbm.at[pl.ds(at, edge), pl.ds(0, rows)], sems.at[i]
         )
-        for i, at in enumerate((0, shards - edge))
+        for i, at in enumerate(((1 - odd) * (shards - edge), odd * (shards - edge)))
     ]
     for copy in copies:
         copy.start()
@@ -456,19 +466,19 @@
         copy.wait()
 
 
-def join_faces(z, first, last, low, high):
+def join_faces(odd, z, inner, outer, inner_rim, outer_rim):
     hbm = pl.BlockSpec(memory_space=pltpu.HBM)
     vmem = pl.BlockSpec(memory_space=pltpu.VMEM)
     return pl.pallas_call(
         join_kernel,
         out_shape=pltpu.HBM(z.shape, z.dtype),
-        in_specs=[hbm, vmem, vmem, vmem, vmem],
+        in_specs=[pl.BlockSpec(memory_space=pltpu.SMEM), hbm, vmem, vmem, vmem, vmem],
         out_specs=hbm,
-        scratch_shapes=[pltpu.VMEM((2, *low.shape), z.dtype), pltpu.SemaphoreType.DMA((2,))],
-        input_output_aliases={0: 0},
+        scratch_shapes=[pltpu.VMEM((2, *inner_rim.shape), z.dtype), pltpu.SemaphoreType.DMA((2,))],
+        input_output_aliases={1: 0},
         compiler_params=pltpu.CompilerParams(vmem_limit_bytes=8 << 20),
         name="join_faces",
-    )(z, *(on_chip(a) for a in (first, last, low, high)))
+    )(odd, z, *(on_chip(a) for a in (inner, outer, inner_rim, outer_rim)))
 
 
 def body(query, key, value, grad_out, pattern, valid_rows):
@@ -476,27 +486,28 @@
         return lax.all_to_all(x, "seq", split_axis=0, concat_axis=0, tiled=True)
 
     size = lax.axis_size("slab")
-    up = [(i, i + 1) for i in range(size - 1)]
-    down = [(i + 1, i) for i in range(size - 1)]
+    inside = [(i, i ^ 1) for i in range(size) if i ^ 1 < size]
+    outside = [(i, j) for i in range(size) if 0 <= (j := i - 1 + 2 * (i % 2)) < size]
+    odd = (lax.axis_index("slab") % 2).astype(jnp.int32).reshape(1)
     rows = query.shape[0]
     edge = FACE * BLOCK // rows
     half, chunk = rows // 2, rows // CHUNKS
     one, two = pack_heads(key, value, query, grad_out)
     one = exchange(one)
-    first, last = take_faces(one, edge, rows)
-    before = lax.ppermute(last, "slab", up)
-    after = lax.ppermute(first, "slab", down)
+    inner, outer = take_faces(odd, one, edge, rows)
+    inner = lax.ppermute(inner, "slab", inside)
+    outer = lax.ppermute(outer, "slab", outside)
     two = exchange(two)
     start = (lax.axis_index("slab") * pattern.shape[0] - FACE).astype(jnp.int32).reshape(1)
-    scalars = (pattern.reshape(-1), valid_rows, start)
-    od, kv, acc = first_half(*scalars, one, before, after)
+    scalars = (pattern.reshape(-1), valid_rows, start, odd)
+    od, kv, acc = first_half(*scalars, one, inner, outer)
     od = exchange(od)
-    z, first, last, to_before, to_after = second_half(*scalars, two, kv, acc, edge)
-    high = lax.ppermute(to_before, "slab", down)
-    low = lax.ppermute(to_after, "slab", up)
+    z, inner, outer, inner_rim, outer_rim = second_half(*scalars, two, kv, acc, edge)
+    inner_rim = lax.ppermute(inner_rim, "slab", inside)
+    outer_rim = lax.ppermute(outer_rim, "slab", outside)
     done = unpack_heads(od, rows, chunks(0, 0, half, 0, chunk), 2, "unpack_first")
     z, *done = lax.optimization_barrier((z, *done))
-    z = exchange(join_faces(z, first, last, low, high))
+    z = exchange(join_faces(odd, z, inner, outer, inner_rim, outer_rim))
     jobs = chunks(0, 0, rows, 0, chunk) + chunks(2, half, half, rows, chunk)
     grad_key, grad_value, grad_query, attn_out = unpack_heads(
         z, rows, jobs, 4, "unpack_second", into=done

time: 169 us -> 162 us (0.959)
  starting transfers between devices: 22.1 us -> 16.2 us
  waiting for transfers between devices: 6.29 us -> 9.32 us
    ppermute x4, starting transfers between devices: 11.1 us -> 5.25 us  [the longest x1 2.53 us: body(): outer = lax.ppermute(outer, 'slab', outside)]
    all_to_all x2, waiting for transfers between devices: 0.01 us -> 1.84 us  [exchange(): return lax.all_to_all(x, 'seq', split_axis=0, concat_axis=0, tiled=True)]
  transfers between devices with their start and end apart: 6 -> 6, of which waited for: 4 -> 3; matrix products, arithmetic and copies ran while one was open for 0% -> 0% of each run, Pallas kernels for 21% -> 21%
where the time goes in v8:
time: 162 us; the launch traced here: 161 us
  blocking collectives  94.8 us (59%)
  Pallas kernels  40.2 us (25%)
  starting transfers between devices  16.2 us (10%)
  waiting for transfers between devices  9.32 us (6%)
    all_to_all x2, blocking collectives, exchange(): return lax.all_to_all(x, 'seq', split_axis=0, concat_axis=0, tiled=True)  94.8 us
    pallas_call x1, Pallas kernels, first_half(): pl.pallas_call(partial(first_kernel, keys_num=keys_num, group=group, line...  15.7 us
    pallas_call x1, Pallas kernels, second_half(): pl.pallas_call(partial(second_kernel, keys_num=keys_num, group=group, lin...  15.5 us
    all_to_all x2, starting transfers between devices, exchange(): return lax.all_to_all(x, 'seq', split_axis=0, concat_axis=0, tiled=True)  11 us
    ppermute x1, waiting for transfers between devices, body(): outer = lax.ppermute(outer, 'slab', outside)  4.93 us
    pallas_call x1, Pallas kernels, pack_heads(): pl.pallas_call(pack_kernel, out_shape=tuple((pltpu.HBM((heads, size, PAIR...  3.7 us
  transfers between devices with their start and end apart: 6, of which 3 were waited for; matrix products, arithmetic and copies ran while one was open for 0% of the time, Pallas kernels for 21%

profile of v8, /device:TPU:2, one launch (start us, length us, event | category | flops | bytes accessed | tf_op | source)
XLA Modules:
  0.0 161.5 jit_solution(91084366999313680)
XLA Ops:
  0.6 3.7 %pack_heads.1 = (bf16[16,768,128]{2,1,0:T(8,128)(2,1)}, bf16[16,256,128]{2,1,0:T(8,128)(2,1)}) custom-call(bf16[512,1024]{1,0:T(8,128)(2,1)} %k_hbm.1, bf16[512,1024]{1,0:T(8,128)(2,1)} %v_hbm.1, bf16[512,1024]{1,0:T(8,128)(2,1)} %q_hbm.1, bf16[512,1024]{1,0:T(8,128)(2,1)} %g_hbm.1), custom_call_target="tpu_custom_call" | custom-call | tf_op jit(solution)/shard_map/pack_heads/pallas_call | solution.py:107
  4.3 47.8 %all_to_all.20.x_hbm = bf16[16,768,128]{2,1,0:T(8,128)(2,1)} all-to-all(bf16[16,768,128]{2,1,0:T(8,128)(2,1)} %get-tuple-element.26), channel_id=1, replica_groups=mesh['slab'=8,'seq'=16] {'seq'}, dimensions={0} | all-to-all | bytes 6291456 | tf_op jit(solution)/shard_map/all_to_all | solution.py:486
  52.1 0.0 copy-start.1
  52.1 0.0 copy-start
  52.1 3.8 %all-to-all-start = ((bf16[16,256,128]{2,1,0:T(8,128)(2,1)}), bf16[16,256,128]{2,1,0:T(8,128)(2,1)S(1)}, u32[]{:S(2)}, u32[]{:S(2)}) async-start(bf16[16,256,128]{2,1,0:T(8,128)(2,1)} %get-tuple-element.25), calls=%async_computation | async-start | bytes 2097152 | tf_op jit(solution)/shard_map/all_to_all | solution.py:486
  55.9 1.0 take_faces.1
  57.0 0.1 collective-permute-start
  57.1 2.5 %collective-permute-start.1 = (bf16[2,512,128]{2,1,0:T(8,128)(2,1)S(1)}, bf16[2,512,128]{2,1,0:T(8,128)(2,1)S(1)}, u32[]{:S(2)}, u32[]{:S(2)}) collective-permute-start(bf16[2,512,128]{2,1,0:T(8,128)(2,1)S(1)} %get-tuple-element.28), channel_id=1, source_target_pairs={{16,32},{32,16},{48,64},{64,48},{80,96},{96,80},{17,33},{33,17},{4... | collective-permute-start | bytes 786440 | tf_op jit(solution)/shard_map/ppermute | solution.py:499
  59.6 0.0 copy-done.1
  59.6 0.1 copy.13
  59.7 0.1 reshape.18.pattern_ref
  59.8 0.0 collective-permute-done.inner_ref
  59.8 4.9 %collective-permute-done.1.outer_ref = bf16[2,512,128]{2,1,0:T(8,128)(2,1)S(1)} collective-permute-done((bf16[2,512,128]{2,1,0:T(8,128)(2,1)S(1)}, bf16[2,512,128]{2,1,0:T(8,128)(2,1)S(1)}, u32[]{:S(2)}, u32[]{:S(2)}) %collective-permute-start.1) | collective-permute-done | bytes 262176 | tf_op jit(solution)/shard_map/ppermute | solution.py:499
  64.8 0.0 copy-done
  64.8 15.7 %first_half.1 = (bf16[16,256,128]{2,1,0:T(8,128)(2,1)}, bf16[10240,128]{1,0:T(8,128)(2,1)}, f32[10240,128]{1,0:T(8,128)}) custom-call(s32[1024]{0:T(1024)S(1)} %reshape.18.pattern_ref, s32[1024]{0:T(1024)S(1)} %copy-done, s32[1]{0:T(128)} %bitcast.1.start_ref, s32[1]{0:T(128)} %bitcast.odd_ref, bf16[16,768,128]{2,1,0:T(8,128)(2,1)} %all_to_all.20.x_hbm, ...), custom_call_target="tpu_custom_call" | custom-call | flops 3221225472 | bytes 16777216 | tf_op jit(solution)/shard_map/first_half/pallas_call | solution.py:391
  80.5 0.0 all-to-all-done.qg_ref
  80.5 7.2 %all-to-all-start.2 = ((bf16[16,256,128]{2,1,0:T(8,128)(2,1)}), bf16[16,256,128]{2,1,0:T(8,128)(2,1)S(1)}, u32[]{:S(2)}, u32[]{:S(2)}) async-start(bf16[16,256,128]{2,1,0:T(8,128)(2,1)} %get-tuple-element.32), calls=%async_computation.2 | async-start | bytes 2097152 | tf_op jit(solution)/shard_map/all_to_all | solution.py:486
  87.7 15.5 %second_half.1 = (bf16[16,768,128]{2,1,0:T(8,128)(2,1)}, f32[2,512,128]{2,1,0:T(8,128)S(1)}, f32[2,512,128]{2,1,0:T(8,128)S(1)}, bf16[2,512,128]{2,1,0:T(8,128)(2,1)}, bf16[2,512,128]{2,1,0:T(8,128)(2,1)S(1)}) custom-call(s32[1024]{0:T(1024)S(1)} %reshape.18.pattern_ref, s32[1024]{0:T(1024)S(1)} %copy-done, s32[1]{0:T(128)} %bitcast.1.start_ref, ...), custom_call_target="tpu_custom_call" | custom-call | flops 3221225472 | bytes 16777216 | tf_op jit(solution)/shard_map/second_half/pallas_call | solution.py:425
  103.2 0.6 collective-permute-start.2
  103.8 2.1 %collective-permute-start.3 = (bf16[2,512,128]{2,1,0:T(8,128)(2,1)S(1)}, bf16[2,512,128]{2,1,0:T(8,128)(2,1)S(1)}, u32[]{:S(2)}, u32[]{:S(2)}) collective-permute-start(bf16[2,512,128]{2,1,0:T(8,128)(2,1)S(1)} %get-tuple-element.39), channel_id=1, source_target_pairs={{16,32},{32,16},{48,64},{64,48},{80,96},{96,80},{17,33},{33,17},{4... | collective-permute-start | bytes 786440 | tf_op jit(solution)/shard_map/ppermute | solution.py:507
  105.9 1.8 %all-to-all-done.2.refs_0_ = bf16[16,256,128]{2,1,0:T(8,128)(2,1)S(1)} async-done(((bf16[16,256,128]{2,1,0:T(8,128)(2,1)}), bf16[16,256,128]{2,1,0:T(8,128)(2,1)S(1)}, u32[]{:S(2)}, u32[]{:S(2)}) %all-to-all-start.2) | async-done | bytes 1048608 | tf_op jit(solution)/shard_map/all_to_all | solution.py:486
  107.7 1.2 unpack_first.1
  108.9 0.0 collective-permute-done.2.inner_rim_ref
  108.9 2.5 %collective-permute-done.3.outer_rim_ref = bf16[2,512,128]{2,1,0:T(8,128)(2,1)S(1)} collective-permute-done((bf16[2,512,128]{2,1,0:T(8,128)(2,1)S(1)}, bf16[2,512,128]{2,1,0:T(8,128)(2,1)S(1)}, u32[]{:S(2)}, u32[]{:S(2)}) %collective-permute-start.3) | collective-permute-done | bytes 262176 | tf_op jit(solution)/shard_map/ppermute | solution.py:507
  111.5 1.0 join_faces.1
  112.5 47.0 %all_to_all.21.refs_0_ = bf16[16,768,128]{2,1,0:T(8,128)(2,1)S(1)} all-to-all(bf16[16,768,128]{2,1,0:T(8,128)(2,1)} %join_faces.1), channel_id=1, replica_groups=mesh['slab'=8,'seq'=16] {'seq'}, dimensions={0} | all-to-all | bytes 6291456 | tf_op jit(solution)/shard_map/all_to_all | solution.py:486
  159.5 2.0 %unpack_second.1 = (bf16[512,1024]{1,0:T(8,128)(2,1)}, bf16[512,1024]{1,0:T(8,128)(2,1)}, bf16[512,1024]{1,0:T(8,128)(2,1)}, bf16[512,1024]{1,0:T(8,128)(2,1)}) custom-call(bf16[16,768,128]{2,1,0:T(8,128)(2,1)S(1)} %all_to_all.21.refs_0_, bf16[512,1024]{1,0:T(8,128)(2,1)} %get-tuple-element.40.refs_1_, ...), custom_call_target="tpu_custom_call", output_to_operand_aliasing={{2}: (1, {}), {3}: (2, {})} | custom-call | bytes 6291456 | tf_op jit(solution)/shard_map/unpack_second/pallas_call | solution.py:155
Async XLA Ops:
  52.1 7.5 %copy-start.1 = (s32[128,8]{0,1:T(8,128)S(1)}, s32[128,8]{0,1:T(8,128)}, u32[]{:S(2)}) copy-start(s32[128,8]{0,1:T(8,128)} %param.10) | copy-start | bytes 12292
  52.1 12.7 %copy-start = (s32[1024]{0:T(1024)S(1)}, s32[1024]{0:T(1024)}, u32[]{:S(2)}) copy-start(s32[1024]{0:T(1024)} %valid_ref.3) | copy-start | bytes 12292
  52.1 28.4 %all-to-all-start = ((bf16[16,256,128]{2,1,0:T(8,128)(2,1)}), bf16[16,256,128]{2,1,0:T(8,128)(2,1)S(1)}, u32[]{:S(2)}, u32[]{:S(2)}) async-start(bf16[16,256,128]{2,1,0:T(8,128)(2,1)} %get-tuple-element.25), calls=%async_computation | async-start | bytes 2097152 | tf_op jit(solution)/shard_map/all_to_all | solution.py:486
  57.0 2.8 %collective-permute-start = (bf16[2,512,128]{2,1,0:T(8,128)(2,1)S(1)}, bf16[2,512,128]{2,1,0:T(8,128)(2,1)S(1)}, u32[]{:S(2)}, u32[]{:S(2)}) collective-permute-start(bf16[2,512,128]{2,1,0:T(8,128)(2,1)S(1)} %get-tuple-element.27), channel_id=1, source_target_pairs={{0,16},{16,0},{32,48},{48,32},{64,80},{80,64},{96,112},{112,96},{1... | collective-permute-start | bytes 786440 | tf_op jit(solution)/shard_map/ppermute | solution.py:498
  57.1 7.7 %collective-permute-start.1 = (bf16[2,512,128]{2,1,0:T(8,128)(2,1)S(1)}, bf16[2,512,128]{2,1,0:T(8,128)(2,1)S(1)}, u32[]{:S(2)}, u32[]{:S(2)}) collective-permute-start(bf16[2,512,128]{2,1,0:T(8,128)(2,1)S(1)} %get-tuple-element.28), channel_id=1, source_target_pairs={{16,32},{32,16},{48,64},{64,48},{80,96},{96,80},{17,33},{33,17},{4... | collective-permute-start | bytes 786440 | tf_op jit(solution)/shard_map/ppermute | solution.py:499
  80.5 27.2 %all-to-all-start.2 = ((bf16[16,256,128]{2,1,0:T(8,128)(2,1)}), bf16[16,256,128]{2,1,0:T(8,128)(2,1)S(1)}, u32[]{:S(2)}, u32[]{:S(2)}) async-start(bf16[16,256,128]{2,1,0:T(8,128)(2,1)} %get-tuple-element.32), calls=%async_computation.2 | async-start | bytes 2097152 | tf_op jit(solution)/shard_map/all_to_all | solution.py:486
  103.2 5.7 %collective-permute-start.2 = (bf16[2,512,128]{2,1,0:T(8,128)(2,1)}, bf16[2,512,128]{2,1,0:T(8,128)(2,1)S(1)}, u32[]{:S(2)}, u32[]{:S(2)}) collective-permute-start(bf16[2,512,128]{2,1,0:T(8,128)(2,1)} %get-tuple-element.38), channel_id=1, source_target_pairs={{0,16},{16,0},{32,48},{48,32},{64,80},{80,64},{96,112},{112,96},{1... | collective-permute-start | bytes 786440 | tf_op jit(solution)/shard_map/ppermute | solution.py:506
  103.8 7.7 %collective-permute-start.3 = (bf16[2,512,128]{2,1,0:T(8,128)(2,1)S(1)}, bf16[2,512,128]{2,1,0:T(8,128)(2,1)S(1)}, u32[]{:S(2)}, u32[]{:S(2)}) collective-permute-start(bf16[2,512,128]{2,1,0:T(8,128)(2,1)S(1)} %get-tuple-element.39), channel_id=1, source_target_pairs={{16,32},{32,16},{48,64},{64,48},{80,96},{96,80},{17,33},{33,17},{4... | collective-permute-start | bytes 786440 | tf_op jit(solution)/shard_map/ppermute | solution.py:507

commit v9 on v8

--- a/solution.py
+++ b/solution.py
@@ -486,9 +486,9 @@
         return lax.all_to_all(x, "seq", split_axis=0, concat_axis=0, tiled=True)
 
     size = lax.axis_size("slab")
-    inside = [(i, i ^ 1) for i in range(size) if i ^ 1 < size]
-    outside = [(i, j) for i in range(size) if 0 <= (j := i - 1 + 2 * (i % 2)) < size]
-    odd = (lax.axis_index("slab") % 2).astype(jnp.int32).reshape(1)
+    inside = [(i, j) for i in range(size) if 0 <= (j := i - 1 + 2 * (i % 2)) < size]
+    outside = [(i, i ^ 1) for i in range(size) if i ^ 1 < size]
+    odd = ((lax.axis_index("slab") + 1) % 2).astype(jnp.int32).reshape(1)
     rows = query.shape[0]
     edge = FACE * BLOCK // rows
     half, chunk = rows // 2, rows // CHUNKS

time: 162 us -> 163 us (level)
  waiting for transfers between devices: 9.32 us -> 6.97 us
  starting transfers between devices: 16.2 us -> 18.1 us
    ppermute x1, waiting for transfers between devices: 4.93 us -> 0.01 us  [body(): outer = lax.ppermute(outer, 'slab', outside)]
    ppermute x1, waiting for transfers between devices: 0.01 us -> 3.89 us  [body(): inner = lax.ppermute(inner, 'slab', inside)]
    ppermute x1, waiting for transfers between devices: 0.01 us -> 3.07 us  [body(): inner_rim = lax.ppermute(inner_rim, 'slab', inside)]
    ppermute x1, waiting for transfers between devices: 2.54 us -> 0.01 us  [body(): outer_rim = lax.ppermute(outer_rim, 'slab', outside)]
    ppermute x1, starting transfers between devices: 0.09 us -> 1.92 us  [body(): inner = lax.ppermute(inner, 'slab', inside)]
    all_to_all x2, waiting for transfers between devices: 1.84 us -> 0.01 us  [exchange(): return lax.all_to_all(x, 'seq', split_axis=0, concat_axis=0, tiled=True)]
  transfers between devices with their start and end apart: 6 -> 6, of which waited for: 3 -> 2; matrix products, arithmetic and copies ran while one was open for 0% -> 0% of each run, Pallas kernels for 21% -> 21%
where the time goes in v9:
time: 163 us; the launch traced here: 162 us
  blocking collectives  94.9 us (58%)
  Pallas kernels  41.5 us (25%)
  starting transfers between devices  18.1 us (11%)
  waiting for transfers between devices  6.97 us (4%)
    all_to_all x2, blocking collectives, exchange(): return lax.all_to_all(x, 'seq', split_axis=0, concat_axis=0, tiled=True)  94.9 us
    pallas_call x1, Pallas kernels, first_half(): pl.pallas_call(partial(first_kernel, keys_num=keys_num, group=group, line...  16.3 us
    pallas_call x1, Pallas kernels, second_half(): pl.pallas_call(partial(second_kernel, keys_num=keys_num, group=group, lin...  16.3 us
    all_to_all x2, starting transfers between devices, exchange(): return lax.all_to_all(x, 'seq', split_axis=0, concat_axis=0, tiled=True)  10.9 us
    ppermute x1, waiting for transfers between devices, body(): inner = lax.ppermute(inner, 'slab', inside)  3.89 us
    pallas_call x1, Pallas kernels, pack_heads(): pl.pallas_call(pack_kernel, out_shape=tuple((pltpu.HBM((heads, size, PAIR...  3.7 us
  transfers between devices with their start and end apart: 6, of which 2 were waited for; matrix products, arithmetic and copies ran while one was open for 0% of the time, Pallas kernels for 21%

profile of v9, /device:TPU:2, one launch (start us, length us, event | category | flops | bytes accessed | tf_op | source)
XLA Modules:
  0.0 162.4 jit_solution(12596359105219968836)
XLA Ops:
  0.6 3.7 %pack_heads.1 = (bf16[16,768,128]{2,1,0:T(8,128)(2,1)}, bf16[16,256,128]{2,1,0:T(8,128)(2,1)}) custom-call(bf16[512,1024]{1,0:T(8,128)(2,1)} %k_hbm.1, bf16[512,1024]{1,0:T(8,128)(2,1)} %v_hbm.1, bf16[512,1024]{1,0:T(8,128)(2,1)} %q_hbm.1, bf16[512,1024]{1,0:T(8,128)(2,1)} %g_hbm.1), custom_call_target="tpu_custom_call" | custom-call | tf_op jit(solution)/shard_map/pack_heads/pallas_call | solution.py:107
  4.3 47.8 %all_to_all.20.x_hbm = bf16[16,768,128]{2,1,0:T(8,128)(2,1)} all-to-all(bf16[16,768,128]{2,1,0:T(8,128)(2,1)} %get-tuple-element.26), channel_id=1, replica_groups=mesh['slab'=8,'seq'=16] {'seq'}, dimensions={0} | all-to-all | bytes 6291456 | tf_op jit(solution)/shard_map/all_to_all | solution.py:486
  52.1 0.0 copy-start.1
  52.1 0.0 copy-start
  52.1 3.8 %all-to-all-start = ((bf16[16,256,128]{2,1,0:T(8,128)(2,1)}), bf16[16,256,128]{2,1,0:T(8,128)(2,1)S(1)}, u32[]{:S(2)}, u32[]{:S(2)}) async-start(bf16[16,256,128]{2,1,0:T(8,128)(2,1)} %get-tuple-element.25), calls=%async_computation | async-start | bytes 2097152 | tf_op jit(solution)/shard_map/all_to_all | solution.py:486
  55.9 1.0 take_faces.1
  57.0 1.9 %collective-permute-start = (bf16[2,512,128]{2,1,0:T(8,128)(2,1)S(1)}, bf16[2,512,128]{2,1,0:T(8,128)(2,1)S(1)}, u32[]{:S(2)}, u32[]{:S(2)}) collective-permute-start(bf16[2,512,128]{2,1,0:T(8,128)(2,1)S(1)} %get-tuple-element.27), channel_id=1, source_target_pairs={{16,32},{32,16},{48,64},{64,48},{80,96},{96,80},{17,33},{33,17},{4... | collective-permute-start | bytes 786440 | tf_op jit(solution)/shard_map/ppermute | solution.py:498
  58.9 1.7 %collective-permute-start.1 = (bf16[2,512,128]{2,1,0:T(8,128)(2,1)S(1)}, bf16[2,512,128]{2,1,0:T(8,128)(2,1)S(1)}, u32[]{:S(2)}, u32[]{:S(2)}) collective-permute-start(bf16[2,512,128]{2,1,0:T(8,128)(2,1)S(1)} %get-tuple-element.28), channel_id=1, source_target_pairs={{0,16},{16,0},{32,48},{48,32},{64,80},{80,64},{96,112},{112,96},{1... | collective-permute-start | bytes 786440 | tf_op jit(solution)/shard_map/ppermute | solution.py:499
  60.6 0.0 copy-done.1
  60.6 0.1 copy.13
  60.7 0.1 reshape.18.pattern_ref
  60.8 3.9 %collective-permute-done.inner_ref = bf16[2,512,128]{2,1,0:T(8,128)(2,1)S(1)} collective-permute-done((bf16[2,512,128]{2,1,0:T(8,128)(2,1)S(1)}, bf16[2,512,128]{2,1,0:T(8,128)(2,1)S(1)}, u32[]{:S(2)}, u32[]{:S(2)}) %collective-permute-start) | collective-permute-done | bytes 262176 | tf_op jit(solution)/shard_map/ppermute | solution.py:498
  64.7 0.0 collective-permute-done.1.outer_ref
  64.7 0.0 copy-done
  64.7 16.3 %first_half.1 = (bf16[16,256,128]{2,1,0:T(8,128)(2,1)}, bf16[10240,128]{1,0:T(8,128)(2,1)}, f32[10240,128]{1,0:T(8,128)}) custom-call(s32[1024]{0:T(1024)S(1)} %reshape.18.pattern_ref, s32[1024]{0:T(1024)S(1)} %copy-done, s32[1]{0:T(128)} %bitcast.1.start_ref, s32[1]{0:T(128)} %bitcast.odd_ref, bf16[16,768,128]{2,1,0:T(8,128)(2,1)} %all_to_all.20.x_hbm, ...), custom_call_target="tpu_custom_call" | custom-call | flops 3221225472 | bytes 16777216 | tf_op jit(solution)/shard_map/first_half/pallas_call | solution.py:391
  81.0 0.0 all-to-all-done.qg_ref
  81.0 7.2 %all-to-all-start.2 = ((bf16[16,256,128]{2,1,0:T(8,128)(2,1)}), bf16[16,256,128]{2,1,0:T(8,128)(2,1)S(1)}, u32[]{:S(2)}, u32[]{:S(2)}) async-start(bf16[16,256,128]{2,1,0:T(8,128)(2,1)} %get-tuple-element.32), calls=%async_computation.2 | async-start | bytes 2097152 | tf_op jit(solution)/shard_map/all_to_all | solution.py:486
  88.2 16.3 %second_half.1 = (bf16[16,768,128]{2,1,0:T(8,128)(2,1)}, f32[2,512,128]{2,1,0:T(8,128)S(1)}, f32[2,512,128]{2,1,0:T(8,128)S(1)}, bf16[2,512,128]{2,1,0:T(8,128)(2,1)}, bf16[2,512,128]{2,1,0:T(8,128)(2,1)S(1)}) custom-call(s32[1024]{0:T(1024)S(1)} %reshape.18.pattern_ref, s32[1024]{0:T(1024)S(1)} %copy-done, s32[1]{0:T(128)} %bitcast.1.start_ref, ...), custom_call_target="tpu_custom_call" | custom-call | flops 3221225472 | bytes 16777216 | tf_op jit(solution)/shard_map/second_half/pallas_call | solution.py:425
  104.4 1.9 %collective-permute-start.2 = (bf16[2,512,128]{2,1,0:T(8,128)(2,1)}, bf16[2,512,128]{2,1,0:T(8,128)(2,1)S(1)}, u32[]{:S(2)}, u32[]{:S(2)}) collective-permute-start(bf16[2,512,128]{2,1,0:T(8,128)(2,1)} %get-tuple-element.38), channel_id=1, source_target_pairs={{16,32},{32,16},{48,64},{64,48},{80,96},{96,80},{17,33},{33,17},{4... | collective-permute-start | bytes 786440 | tf_op jit(solution)/shard_map/ppermute | solution.py:506
  106.4 1.7 %collective-permute-start.3 = (bf16[2,512,128]{2,1,0:T(8,128)(2,1)S(1)}, bf16[2,512,128]{2,1,0:T(8,128)(2,1)S(1)}, u32[]{:S(2)}, u32[]{:S(2)}) collective-permute-start(bf16[2,512,128]{2,1,0:T(8,128)(2,1)S(1)} %get-tuple-element.39), channel_id=1, source_target_pairs={{0,16},{16,0},{32,48},{48,32},{64,80},{80,64},{96,112},{112,96},{1... | collective-permute-start | bytes 786440 | tf_op jit(solution)/shard_map/ppermute | solution.py:507
  108.0 0.0 all-to-all-done.2.refs_0_
  108.0 1.2 unpack_first.1
  109.3 3.1 %collective-permute-done.2.inner_rim_ref = bf16[2,512,128]{2,1,0:T(8,128)(2,1)S(1)} collective-permute-done((bf16[2,512,128]{2,1,0:T(8,128)(2,1)}, bf16[2,512,128]{2,1,0:T(8,128)(2,1)S(1)}, u32[]{:S(2)}, u32[]{:S(2)}) %collective-permute-start.2) | collective-permute-done | bytes 262176 | tf_op jit(solution)/shard_map/ppermute | solution.py:506
  112.3 0.0 collective-permute-done.3.outer_rim_ref
  112.3 1.0 join_faces.1
  113.3 47.1 %all_to_all.21.refs_0_ = bf16[16,768,128]{2,1,0:T(8,128)(2,1)S(1)} all-to-all(bf16[16,768,128]{2,1,0:T(8,128)(2,1)} %join_faces.1), channel_id=1, replica_groups=mesh['slab'=8,'seq'=16] {'seq'}, dimensions={0} | all-to-all | bytes 6291456 | tf_op jit(solution)/shard_map/all_to_all | solution.py:486
  160.4 2.0 %unpack_second.1 = (bf16[512,1024]{1,0:T(8,128)(2,1)}, bf16[512,1024]{1,0:T(8,128)(2,1)}, bf16[512,1024]{1,0:T(8,128)(2,1)}, bf16[512,1024]{1,0:T(8,128)(2,1)}) custom-call(bf16[16,768,128]{2,1,0:T(8,128)(2,1)S(1)} %all_to_all.21.refs_0_, bf16[512,1024]{1,0:T(8,128)(2,1)} %get-tuple-element.40.refs_1_, ...), custom_call_target="tpu_custom_call", output_to_operand_aliasing={{2}: (1, {}), {3}: (2, {})} | custom-call | bytes 6291456 | tf_op jit(solution)/shard_map/unpack_second/pallas_call | solution.py:155
Async XLA Ops:
  52.1 8.5 %copy-start.1 = (s32[128,8]{0,1:T(8,128)S(1)}, s32[128,8]{0,1:T(8,128)}, u32[]{:S(2)}) copy-start(s32[128,8]{0,1:T(8,128)} %param.10) | copy-start | bytes 12292
  52.1 12.6 %copy-start = (s32[1024]{0:T(1024)S(1)}, s32[1024]{0:T(1024)}, u32[]{:S(2)}) copy-start(s32[1024]{0:T(1024)} %valid_ref.3) | copy-start | bytes 12292
  52.1 28.9 %all-to-all-start = ((bf16[16,256,128]{2,1,0:T(8,128)(2,1)}), bf16[16,256,128]{2,1,0:T(8,128)(2,1)S(1)}, u32[]{:S(2)}, u32[]{:S(2)}) async-start(bf16[16,256,128]{2,1,0:T(8,128)(2,1)} %get-tuple-element.25), calls=%async_computation | async-start | bytes 2097152 | tf_op jit(solution)/shard_map/all_to_all | solution.py:486
  57.0 7.7 %collective-permute-start = (bf16[2,512,128]{2,1,0:T(8,128)(2,1)S(1)}, bf16[2,512,128]{2,1,0:T(8,128)(2,1)S(1)}, u32[]{:S(2)}, u32[]{:S(2)}) collective-permute-start(bf16[2,512,128]{2,1,0:T(8,128)(2,1)S(1)} %get-tuple-element.27), channel_id=1, source_target_pairs={{16,32},{32,16},{48,64},{64,48},{80,96},{96,80},{17,33},{33,17},{4... | collective-permute-start | bytes 786440 | tf_op jit(solution)/shard_map/ppermute | solution.py:498
  58.9 5.8 %collective-permute-start.1 = (bf16[2,512,128]{2,1,0:T(8,128)(2,1)S(1)}, bf16[2,512,128]{2,1,0:T(8,128)(2,1)S(1)}, u32[]{:S(2)}, u32[]{:S(2)}) collective-permute-start(bf16[2,512,128]{2,1,0:T(8,128)(2,1)S(1)} %get-tuple-element.28), channel_id=1, source_target_pairs={{0,16},{16,0},{32,48},{48,32},{64,80},{80,64},{96,112},{112,96},{1... | collective-permute-start | bytes 786440 | tf_op jit(solution)/shard_map/ppermute | solution.py:499
  81.0 27.0 %all-to-all-start.2 = ((bf16[16,256,128]{2,1,0:T(8,128)(2,1)}), bf16[16,256,128]{2,1,0:T(8,128)(2,1)S(1)}, u32[]{:S(2)}, u32[]{:S(2)}) async-start(bf16[16,256,128]{2,1,0:T(8,128)(2,1)} %get-tuple-element.32), calls=%async_computation.2 | async-start | bytes 2097152 | tf_op jit(solution)/shard_map/all_to_all | solution.py:486
  104.4 7.9 %collective-permute-start.2 = (bf16[2,512,128]{2,1,0:T(8,128)(2,1)}, bf16[2,512,128]{2,1,0:T(8,128)(2,1)S(1)}, u32[]{:S(2)}, u32[]{:S(2)}) collective-permute-start(bf16[2,512,128]{2,1,0:T(8,128)(2,1)} %get-tuple-element.38), channel_id=1, source_target_pairs={{16,32},{32,16},{48,64},{64,48},{80,96},{96,80},{17,33},{33,17},{4... | collective-permute-start | bytes 786440 | tf_op jit(solution)/shard_map/ppermute | solution.py:506
  106.4 6.0 %collective-permute-start.3 = (bf16[2,512,128]{2,1,0:T(8,128)(2,1)S(1)}, bf16[2,512,128]{2,1,0:T(8,128)(2,1)S(1)}, u32[]{:S(2)}, u32[]{:S(2)}) collective-permute-start(bf16[2,512,128]{2,1,0:T(8,128)(2,1)S(1)} %get-tuple-element.39), channel_id=1, source_target_pairs={{0,16},{16,0},{32,48},{48,32},{64,80},{80,64},{96,112},{112,96},{1... | collective-permute-start | bytes 786440 | tf_op jit(solution)/shard_map/ppermute | solution.py:507
